TPU v7x, 32 devices: a whole 2x2x4 slice. The times are simulated.
32 devices in a mesh: gx: 8 (over y, x, core), gy: 4 (over z).
Axes of the slice: x: 2, y: 2, z: 4, core: 2. Of those that a mesh axis runs over, the one named last changes fastest.
Arguments:
- model_image: bfloat16 [16, 1024, 4096], P(None, 'gx', 'gy'), may hold values from -6 to 6
- tables: bfloat16 [8, 128, 1024], replicated, may hold values from -0.1875 to 0.1875
- observed: bfloat16 [1024, 16, 128], P(('gx', 'gy')), may hold values from -6 to 6
- aperture: int32 [1024, 4], P(('gx', 'gy')), may hold values from 0 to 31, all different within a row; in each aligned block of 32 rows (0 to 31, 32 to 63, ...) at most 8 rows name the same one
- traveltime: int32 [1024, 4, 16], P(('gx', 'gy')), may hold values from 0 to 15
- band_index: int32 [1024, 4, 16], P(('gx', 'gy')), may hold values from 0 to 7
- amplitude: bfloat16 [1024, 4, 128], P(('gx', 'gy')), may hold values from 0.019897461 to 0.19921875
Outputs:
- residual: float32 [1024, 16, 128], P(('gx', 'gy'))
- gradient: float32 [16, 1024, 4096], P(None, 'gx', 'gy')
Inputs may be any that keep to these rules, and one draw needn't show every extreme that they name: `aperture`: each trace names 4 distinct tiles. Among the traces of one device no tile is named more than 8 times, a bound that some block reaches.
All inputs are finite; a program needn't handle non-finite values.
Results may differ from a plain program's by a relative error of at most 0.006.
Values may be sent and summed in bfloat16 or wider, within the bound.
No kernel may reach another device: no remote copies, remote signals or barrier semaphores. Data moves between devices by JAX's collectives and lax.ppermute only.
A program may use at most 64 MiB of HBM per device.

v0:
```python
import jax
import jax.numpy as jnp
from jax import lax
from jax.sharding import PartitionSpec as P


def shards(model_image, tables, observed, aperture, traveltime, band_index, amplitude):
    size_x = lax.axis_size("gx")
    size_y = lax.axis_size("gy")
    devices = size_x * size_y
    depth, width_x, width_y = model_image.shape
    bands, block_len, _ = tables.shape
    traces, tile_count = aperture.shape
    trace_blocks = observed.shape[1]
    capacity = max(2, 2 * traces * tile_count // devices)
    pair_count = traces * tile_count
    slot_count = devices * capacity
    destination = aperture.reshape(pair_count)
    hits = (destination[:, None] == jnp.arange(devices, dtype=jnp.int32)[None, :]).astype(jnp.int32)
    before = jnp.cumsum(hits, axis=0) - hits
    position = destination * capacity + jnp.sum(before * hits, axis=1)
    amp_send = (
        jnp.zeros((1, slot_count, width_x), jnp.bfloat16)
        .at[0, position]
        .set(amplitude.reshape(pair_count, width_x))
    )
    band_send = (
        jnp.zeros((1, slot_count, depth), jnp.int32)
        .at[0, position]
        .set(band_index.reshape(pair_count, depth))
    )
    amp_recv, band_recv = (
        lax.all_to_all(amp_send, ("gx", "gy"), split_axis=1, concat_axis=1, tiled=True),
        lax.all_to_all(band_send, ("gx", "gy"), split_axis=1, concat_axis=1, tiled=True),
    )
    received_amp = amp_recv[0]
    received_band = band_recv[0].T
    tables_flat = tables.reshape(bands * block_len, width_y)
    rows = lax.dot_general(
        model_image.reshape(depth * width_x, width_y),
        tables_flat,
        (((1,), (1,)), ((), ())),
        preferred_element_type=jnp.float32,
    )
    rows = rows.astype(jnp.bfloat16).reshape(depth, width_x, bands * block_len)
    band_picks = jnp.arange(bands, dtype=jnp.int32)

    def model_depth(operands):
        rows_level, band_level = operands
        full = jnp.dot(received_amp, rows_level, preferred_element_type=jnp.float32).reshape(
            slot_count, bands, block_len
        )
        pick = (band_level[:, None] == band_picks[None, :]).astype(jnp.float32)
        return jnp.sum(full * pick[:, :, None], axis=1).astype(jnp.bfloat16)

    partials = lax.map(model_depth, (rows, received_band))
    returned = lax.all_to_all(partials, ("gx", "gy"), split_axis=1, concat_axis=1, tiled=True)
    mine = returned[:, position, :].reshape(depth, traces, tile_count, block_len)
    select = (traveltime[..., None] == jnp.arange(trace_blocks, dtype=jnp.int32)).astype(
        jnp.bfloat16
    )
    modeled = jnp.einsum("tkzn,ztks->tns", select, mine, preferred_element_type=jnp.float32)
    residual = modeled - observed.astype(jnp.float32)
    residual_bf = residual.astype(jnp.bfloat16)
    picked = jnp.einsum(
        "tkzn,tns->ztks", select, residual_bf, preferred_element_type=jnp.float32
    ).astype(jnp.bfloat16)
    res_send = (
        jnp.zeros((depth, slot_count, block_len), jnp.bfloat16)
        .at[:, position, :]
        .set(picked.reshape(depth, pair_count, block_len))
    )
    res_recv = lax.all_to_all(res_send, ("gx", "gy"), split_axis=1, concat_axis=1, tiled=True)

    def image_depth(operands):
        res_level, band_level = operands
        pick = (band_level[:, None] == band_picks[None, :]).astype(jnp.bfloat16)
        masked = (pick[:, :, None] * res_level[:, None, :]).reshape(slot_count, bands * block_len)
        stacks = lax.dot_general(
            received_amp, masked, (((0,), (0,)), ((), ())), preferred_element_type=jnp.float32
        )
        return jnp.dot(stacks.astype(jnp.bfloat16), tables_flat, preferred_element_type=jnp.float32)

    gradient = lax.map(image_depth, (res_recv, received_band))
    return (residual, gradient)


def solution(mesh):
    placed = (
        P(None, "gx", "gy"),
        P(),
        P(("gx", "gy"), None, None),
        P(("gx", "gy"), None),
        P(("gx", "gy"), None, None),
        P(("gx", "gy"), None, None),
        P(("gx", "gy"), None, None),
    )
    return jax.shard_map(
        shards,
        mesh=mesh,
        in_specs=placed,
        out_specs=(P(("gx", "gy"), None, None), P(None, "gx", "gy")),
        check_vma=False,
    )
```

profile of v0, /device:TPU:1, one launch (start us, length us, event | category | flops | bytes accessed | tf_op | source)
XLA Modules:
  0.0 185.5 jit_solution(13113340555178601502)
XLA Ops:
  2.8 0.8 copy.55
  3.7 0.9 scatter_custom_fusion.1
  5.1 0.9 reduce.1
  6.7 7.1 %all-to-all-start.1 = ((s32[32,1,128]{2,1,0:T(1,128)}), s32[32,1,128]{2,1,0:T(1,128)S(1)}, u32[]{:S(2)}, u32[]{:S(2)}) async-start(s32[32,1,128]{2,1,0:T(1,128)} %reshape.189), calls=%async_computation.1 | async-start | bytes 32768 | tf_op jit(solution)/shard_map/all_to_all | solution.py:34
  13.8 1.1 scatter_custom_fusion
  15.6 1.0 reduce
  17.3 3.2 %all-to-all-done.1 = s32[32,1,128]{2,1,0:T(1,128)S(1)} async-done(((s32[32,1,128]{2,1,0:T(1,128)}), s32[32,1,128]{2,1,0:T(1,128)S(1)}, u32[]{:S(2)}, u32[]{:S(2)}) %all-to-all-start.1) | async-done | bytes 16416 | tf_op jit(solution)/shard_map/all_to_all | solution.py:34
  20.5 2.9 %all-to-all-start = ((bf16[32,2,512]{2,1,0:T(2,128)(2,1)}), bf16[32,2,512]{2,1,0:T(2,128)(2,1)S(1)}, u32[]{:S(2)}, u32[]{:S(2)}) async-start(bf16[32,2,512]{2,1,0:T(2,128)(2,1)} %reshape.187), calls=%async_computation | async-start | bytes 131072 | tf_op jit(solution)/shard_map/all_to_all | solution.py:33
  23.4 9.4 %convolution_convert_fusion.1 = bf16[2048,1024]{1,0:T(8,128)(2,1)} fusion(bf16[2048,1024]{1,0:T(8,128)(2,1)} %bitcast.112, bf16[1024,1024]{1,0:T(8,128)(2,1)} %bitcast.97), kind=kOutput, calls=%fused_computation.25 | convolution fusion | flops 4297064448 | bytes 10485760 | tf_op jit(solution)/shard_map/dot_general | solution.py:39
  33.8 22.9 %while.22 = (s32[]{:T(128)}, bf16[16,256,128]{1,2,0:T(8,128)(2,1)S(1)}, bf16[16,128,1024]{2,1,0:T(8,128)(2,1)}, bf16[256,128]{1,0:T(8,128)(2,1)S(1)}, s32[16,256]{1,0:T(8,128)S(1)}, /*index=5*/s32[]{:T(128)}) while((s32[]{:T(128)}, bf16[16,256,128]{1,2,0:T(8,128)(2,1)S(1)}, bf16[16,128,1024]{2,1,0:T(8,128)(2,1)}, ...), condition=%wide.region_6.7_spmd.clone, body=%wide.region_4.6_spmd.clone.sunk | while | flops 67604480 | bytes 2641485 | solution.py:56
  33.8 1.3 fusion.43
  35.3 1.3 fusion.43
  36.7 1.3 fusion.43
  38.1 1.3 fusion.43
  39.6 1.3 fusion.43
  41.0 1.3 fusion.43
  42.4 1.3 fusion.43
  43.9 1.3 fusion.43
  45.3 1.3 fusion.43
  46.7 1.3 fusion.43
  48.1 1.3 fusion.43
  49.6 1.3 fusion.43
  51.0 1.3 fusion.43
  52.4 1.3 fusion.43
  53.9 1.3 fusion.43
  55.3 1.3 fusion.43
  56.8 1.8 copy.59
  58.5 6.0 %all-to-all-start.2 = ((bf16[16,256,128]{2,0,1:T(8,128)(2,1)}), bf16[16,256,128]{2,0,1:T(8,128)(2,1)S(1)}, u32[]{:S(2)}, u32[]{:S(2)}) async-start(bf16[16,256,128]{2,0,1:T(8,128)(2,1)} %copy.59), calls=%async_computation.2 | async-start | bytes 2097152 | tf_op jit(solution)/shard_map/all_to_all | solution.py:57
  64.6 26.2 %all-to-all-done.2 = bf16[16,256,128]{2,0,1:T(8,128)(2,1)S(1)} async-done(((bf16[16,256,128]{2,0,1:T(8,128)(2,1)}), bf16[16,256,128]{2,0,1:T(8,128)(2,1)S(1)}, u32[]{:S(2)}, u32[]{:S(2)}) %all-to-all-start.2) | async-done | bytes 1048608 | tf_op jit(solution)/shard_map/all_to_all | solution.py:57
  91.6 0.9 fusion.15
  93.0 1.1 broadcast.77
  94.1 12.4 %scatter_fusion = bf16[16,256,128]{2,0,1:T(8,128)(2,1)} fusion(bf16[16,256,128]{2,0,1:T(8,128)(2,1)} %broadcast.77, s32[128]{0:T(128)S(1)} %fusion.25, bf16[128,16,128]{2,1,0:T(8,128)(2,1)S(1)} %bitcast.104), kind=kCustom, calls=%fused_computation.3 | custom fusion | bytes 1573376 | tf_op jit(solution)/shard_map/scatter | solution.py:71
  106.5 3.2 %all-to-all-start.3 = ((bf16[16,256,128]{2,0,1:T(8,128)(2,1)}), bf16[16,256,128]{2,0,1:T(8,128)(2,1)S(1)}, u32[]{:S(2)}, u32[]{:S(2)}) async-start(bf16[16,256,128]{2,0,1:T(8,128)(2,1)} %scatter_fusion), calls=%async_computation.3 | async-start | bytes 2097152 | tf_op jit(solution)/shard_map/all_to_all | solution.py:73
  109.7 26.3 %all-to-all-done.3 = bf16[16,256,128]{2,0,1:T(8,128)(2,1)S(1)} async-done(((bf16[16,256,128]{2,0,1:T(8,128)(2,1)}), bf16[16,256,128]{2,0,1:T(8,128)(2,1)S(1)}, u32[]{:S(2)}, u32[]{:S(2)}) %all-to-all-start.3) | async-done | bytes 1048608 | tf_op jit(solution)/shard_map/all_to_all | solution.py:73
  136.1 1.3 copy.62
  137.3 48.2 %while.23 = (s32[]{:T(128)}, f32[16,128,1024]{2,1,0:T(8,128)}, s32[16,256]{1,0:T(8,128)S(1)}, bf16[16,256,128]{2,1,0:T(8,128)(2,1)}, bf16[256,128]{1,0:T(8,128)(...) while((s32[]{:T(128)}, f32[16,128,1024]{2,1,0:T(8,128)}, s32[16,256]{1,0:T(8,128)S(1)}, ...), condition=%wide.region_9.10_spmd.clone, body=%wide.region_8.9_spmd.clone.sunk | while | flops 335941632 | bytes 3952213 | solution.py:84
  137.5 0.8 dynamic-slice_bitcast_fusion.2
  138.7 1.7 fusion.49
  140.5 0.8 dynamic-slice_bitcast_fusion.2
  141.7 1.7 fusion.49
  143.5 0.8 dynamic-slice_bitcast_fusion.2
  144.7 1.7 fusion.49
  146.5 0.8 dynamic-slice_bitcast_fusion.2
  147.7 1.7 fusion.49
  149.5 0.8 dynamic-slice_bitcast_fusion.2
  150.7 1.7 fusion.49
  152.5 0.8 dynamic-slice_bitcast_fusion.2
  153.7 1.7 fusion.49
  155.5 0.8 dynamic-slice_bitcast_fusion.2
  156.7 1.7 fusion.49
  158.5 0.8 dynamic-slice_bitcast_fusion.2
  159.7 1.7 fusion.49
  162.7 1.7 fusion.49
  165.7 1.7 fusion.49
  167.6 0.8 dynamic-slice_bitcast_fusion.2
  168.8 1.7 fusion.49
  170.6 0.8 dynamic-slice_bitcast_fusion.2
  171.8 1.7 fusion.49
  173.6 0.8 dynamic-slice_bitcast_fusion.2
  174.8 1.7 fusion.49
  177.8 1.7 fusion.49
  180.8 1.7 fusion.49
  182.6 0.8 dynamic-slice_bitcast_fusion.2
  183.8 1.7 fusion.49
  (166 shorter events, 19.6 us)
Async XLA Ops:
  6.7 13.7 %all-to-all-start.1 = ((s32[32,1,128]{2,1,0:T(1,128)}), s32[32,1,128]{2,1,0:T(1,128)S(1)}, u32[]{:S(2)}, u32[]{:S(2)}) async-start(s32[32,1,128]{2,1,0:T(1,128)} %reshape.189), calls=%async_computation.1 | async-start | bytes 32768 | tf_op jit(solution)/shard_map/all_to_all | solution.py:34
  20.5 13.3 %all-to-all-start = ((bf16[32,2,512]{2,1,0:T(2,128)(2,1)}), bf16[32,2,512]{2,1,0:T(2,128)(2,1)S(1)}, u32[]{:S(2)}, u32[]{:S(2)}) async-start(bf16[32,2,512]{2,1,0:T(2,128)(2,1)} %reshape.187), calls=%async_computation | async-start | bytes 131072 | tf_op jit(solution)/shard_map/all_to_all | solution.py:33
  56.7 7.8 %copy-start.1 = (s32[32,4,16]{0,2,1:T(8,128)S(1)}, s32[32,4,16]{0,2,1:T(8,128)}, u32[]{:S(2)}) copy-start(s32[32,4,16]{0,2,1:T(8,128)} %param.15) | copy-start | bytes 24580
  56.7 34.8 %copy-start.2 = (bf16[32,16,128]{2,1,0:T(8,128)(2,1)S(1)}, bf16[32,16,128]{2,1,0:T(8,128)(2,1)}, u32[]{:S(2)}) copy-start(bf16[32,16,128]{2,1,0:T(8,128)(2,1)} %param.13) | copy-start | bytes 393220
  58.5 32.3 %all-to-all-start.2 = ((bf16[16,256,128]{2,0,1:T(8,128)(2,1)}), bf16[16,256,128]{2,0,1:T(8,128)(2,1)S(1)}, u32[]{:S(2)}, u32[]{:S(2)}) async-start(bf16[16,256,128]{2,0,1:T(8,128)(2,1)} %copy.59), calls=%async_computation.2 | async-start | bytes 2097152 | tf_op jit(solution)/shard_map/all_to_all | solution.py:57
  92.5 44.8 %copy-start.3 = (f32[32,16,128]{2,1,0:T(8,128)}, f32[32,16,128]{2,1,0:T(8,128)S(1)}, u32[]{:S(2)}) copy-start(f32[32,16,128]{2,1,0:T(8,128)S(1)} %fusion.15) | copy-start | bytes 786436
  92.5 44.8 %copy-start = (bf16[8,128,1024]{2,1,0:T(8,128)(2,1)S(1)}, bf16[8,128,1024]{2,1,0:T(8,128)(2,1)}, u32[]{:S(2)}) copy-start(bf16[8,128,1024]{2,1,0:T(8,128)(2,1)} %param.12) | copy-start | bytes 6291460
  106.5 29.5 %all-to-all-start.3 = ((bf16[16,256,128]{2,0,1:T(8,128)(2,1)}), bf16[16,256,128]{2,0,1:T(8,128)(2,1)S(1)}, u32[]{:S(2)}, u32[]{:S(2)}) async-start(bf16[16,256,128]{2,0,1:T(8,128)(2,1)} %scatter_fusion), calls=%async_computation.3 | async-start | bytes 2097152 | tf_op jit(solution)/shard_map/all_to_all | solution.py:73
where the time goes:
time: 188 us; the launch traced here: 185 us
  matrix products  58.2 us (31%)
  waiting for transfers between devices  55.7 us (30%)
  local copies, waits for them, and re-layouts  40.2 us (21%)
  starting transfers between devices  19.2 us (10%)
  other arithmetic  10.4 us (6%)
    dot_general x16, matrix products, image_depth(): jnp.dot(stacks.astype(jnp.bfloat16), tables_flat, preferred_element_type=...  26.9 us
    all_to_all x1, waiting for transfers between devices, shards(): lax.all_to_all(res_send, ('gx', 'gy'), split_axis=1, concat_axis=1, tiled...  26.3 us
    all_to_all x1, waiting for transfers between devices, shards(): lax.all_to_all(partials, ('gx', 'gy'), split_axis=1, concat_axis=1, tiled...  26.2 us
    dot_general x16, matrix products, model_depth(): jnp.dot(received_amp, rows_level, preferred_element_type=jnp.float32)  20.4 us
    mul x16, local copies, waits for them, and re-layouts, image_depth(): pick[:, :, None] * res_level[:, None, :]  13.5 us
    scatter x1, local copies, waits for them, and re-layouts, shards(): res_send = jnp.zeros((depth, slot_count, block_len), jnp.bfloat16).at[:,...  12.4 us
    dot_general x1, matrix products, shards(): lax.dot_general(model_image.reshape(depth * width_x, width_y), tables_fla...  9.45 us
    all_to_all x1, starting transfers between devices, shards(): lax.all_to_all(band_send, ('gx', 'gy'), split_axis=1, concat_axis=1, tile...  7.08 us
  transfers between devices with their start and end apart: 4, of which 3 were waited for; matrix products, arithmetic and copies ran while one was open for 7% of the time, Pallas kernels for 0%

commit v1 on v0

v1 whole, which is shorter than its diff:
```python
import functools

import jax
import jax.numpy as jnp
from jax import lax
from jax.experimental import pallas as pl
from jax.experimental.pallas import tpu as pltpu
from jax.sharding import PartitionSpec as P

BF = jnp.bfloat16
F32 = jnp.float32
VMEM = pl.BlockSpec(memory_space=pltpu.VMEM)
SMEM = pl.BlockSpec(memory_space=pltpu.SMEM)


def dot(a, b, dims=((1,), (0,))):
    return lax.dot_general(a, b, (dims, ((), ())), preferred_element_type=F32)


def iota(shape, axis):
    return lax.broadcasted_iota(jnp.int32, shape, axis)


def prep_kernel(devices, capacity, ap_ref, tt_ref, bi_ref, am_ref, msg_ref, pos_ref):
    tiles, traces = ap_ref.shape
    slots = devices * capacity
    width = am_ref.shape[2]
    depth = tt_ref.shape[1]
    before = (iota((traces, traces), 0) < iota((traces, traces), 1)).astype(BF)
    base = jnp.zeros((devices, 1), F32)
    amp = jnp.zeros((slots, width), F32)
    marks = jnp.zeros((slots, width), F32)
    for k in range(tiles):
        dest = ap_ref[k : k + 1, :]
        hit = iota((devices, traces), 0) == dest
        hits = hit.astype(F32)
        rank = jnp.sum(hits * (base + dot(hits.astype(BF), before)), axis=0, keepdims=True)
        base = base + jnp.sum(hits, axis=1, keepdims=True)
        pos = dest * capacity + rank.astype(jnp.int32)
        pos_ref[k : k + 1, :] = pos
        place = (iota((slots, traces), 0) == pos).astype(F32).astype(BF)
        amp = amp + dot(place, am_ref[:, k, :])
        levels = jnp.concatenate(
            [
                bi_ref[k].astype(F32),
                tt_ref[k].astype(F32),
                jnp.zeros((width - 2 * depth, traces), F32),
            ],
            axis=0,
        ).astype(BF)
        marks = marks + dot(place, levels, ((1,), (1,)))
    msg_ref[:, :width] = amp.astype(BF)
    msg_ref[:, width:] = marks.astype(BF)


def spread(marks, lane):
    width = marks.shape[1]
    return dot(marks, (iota((width, width), 0) == lane).astype(F32).astype(BF))


def demig_kernel(bands, blocks, msg_ref, rows_ref, out_ref, part_ref, time_ref):
    z = pl.program_id(0)
    depth, slots, block_len = part_ref.shape
    width = rows_ref.shape[1]
    amp = msg_ref[:, :width]
    marks = msg_ref[:, width:]
    band = spread(marks, z)
    time_ref[z] = spread(marks, z + depth).astype(BF)
    zero = jnp.zeros_like(amp)
    weights = jnp.concatenate([jnp.where(band == b, amp, zero) for b in range(bands)], axis=1)
    rows = jnp.concatenate(
        [rows_ref[0, :, b * block_len : (b + 1) * block_len] for b in range(bands)], axis=0
    )
    part_ref[z] = dot(weights, rows).astype(BF)

    @pl.when(z == depth - 1)
    def _():
        group = 256 // depth

        def one(g, carry):
            at = pl.ds(pl.multiple_of(g * group, group), group)
            pick = picker(time_ref[:, at, :], blocks)
            part = part_ref[:, at, :].reshape(depth * group, block_len)
            total = dot(pick, part, ((0,), (0,)))
            out_ref[at] = total.astype(BF).reshape(group, blocks, block_len)
            return carry

        lax.fori_loop(0, slots // group, one, 0)


def picker(times, blocks):
    depth, group, lanes = times.shape
    code = times.astype(F32).reshape(depth * group, lanes)
    own = (iota((depth * group, lanes), 0) % group * blocks).astype(F32)
    code = code + own
    at = iota((depth * group, lanes), 1).astype(F32)
    return jnp.concatenate(
        [(code == at + float(i)).astype(F32).astype(BF) for i in range(0, group * blocks, lanes)],
        axis=1,
    )


def residual_kernel(capacity, pos_ref, recv_ref, obs_ref, res_ref, send_ref):
    tiles, traces = pos_ref.shape
    send_ref[...] = jnp.zeros_like(send_ref)

    def one(t, carry):
        total = recv_ref[pos_ref[0, t]].astype(F32)
        for k in range(1, tiles):
            total = total + recv_ref[pos_ref[k, t]].astype(F32)
        total = total - obs_ref[t].astype(F32)
        res_ref[t] = total
        low = total.astype(BF)
        for k in range(tiles):
            send_ref[pos_ref[k, t]] = low
        return carry

    lax.fori_loop(0, traces, one, 0)


def image_kernel(bands, levels, msg_ref, blk_ref, tab_ref, out_ref, pick_ref, time_ref, amp_ref, stack_ref):
    step = pl.program_id(0)
    depth, slots, block_len = pick_ref.shape
    blocks = blk_ref.shape[1]
    width = out_ref.shape[1]
    marks = msg_ref[:, width:]

    @pl.when(step == 0)
    def _():
        amp_ref[...] = msg_ref[:, :width].astype(F32).T.astype(BF)
        for z in range(depth):
            time_ref[z] = spread(marks, z + depth).astype(BF)
        group = 256 // depth

        def one(g, carry):
            at = pl.ds(pl.multiple_of(g * group, group), group)
            pick = picker(time_ref[:, at, :], blocks)
            block = blk_ref[at].reshape(group * blocks, block_len)
            pick_ref[:, at, :] = dot(pick, block).astype(BF).reshape(depth, group, block_len)
            return carry

        lax.fori_loop(0, slots // group, one, 0)

    for i in range(levels):
        z = step * levels + i
        band = spread(marks, z)
        picked = pick_ref[z]
        zero = jnp.zeros_like(picked)
        masked = jnp.concatenate([jnp.where(band == b, picked, zero) for b in range(bands)], axis=1)
        stack_ref[i * width : (i + 1) * width, :] = dot(amp_ref[...], masked).astype(BF)
    image = dot(stack_ref[...], tab_ref[...])
    out_ref[...] = image.reshape(levels, width, image.shape[1])


def shards(model_image, tables, observed, aperture, traveltime, band_index, amplitude):
    devices = lax.axis_size("gx") * lax.axis_size("gy")
    depth, width_x, width_y = model_image.shape
    bands, block_len, _ = tables.shape
    traces, tile_count = aperture.shape
    blocks = observed.shape[1]
    capacity = max(2, 2 * traces * tile_count // devices)
    slots = devices * capacity
    tables_flat = tables.reshape(bands * block_len, width_y)

    message, position = pl.pallas_call(
        functools.partial(prep_kernel, devices, capacity),
        out_shape=(
            jax.ShapeDtypeStruct((slots, 2 * width_x), BF),
            jax.ShapeDtypeStruct((tile_count, traces), jnp.int32),
        ),
        in_specs=[VMEM] * 4,
        out_specs=(VMEM, VMEM),
        name="prep",
    )(
        aperture.T,
        traveltime.transpose(1, 2, 0),
        band_index.transpose(1, 2, 0),
        amplitude,
    )
    got = lax.all_to_all(message, ("gx", "gy"), split_axis=0, concat_axis=0, tiled=True)
    rows = lax.dot_general(
        model_image.reshape(depth * width_x, width_y),
        tables_flat,
        (((1,), (1,)), ((), ())),
        preferred_element_type=F32,
    )
    rows = rows.astype(BF).reshape(depth, width_x, bands * block_len)

    modeled = pl.pallas_call(
        functools.partial(demig_kernel, bands, blocks),
        grid=(depth,),
        out_shape=jax.ShapeDtypeStruct((slots, blocks, block_len), BF),
        in_specs=[
            pl.BlockSpec((slots, 2 * width_x), lambda z: (0, 0)),
            pl.BlockSpec((1, width_x, bands * block_len), lambda z: (z, 0, 0)),
        ],
        out_specs=pl.BlockSpec((slots, blocks, block_len), lambda z: (0, 0, 0)),
        scratch_shapes=[
            pltpu.VMEM((depth, slots, block_len), BF),
            pltpu.VMEM((depth, slots, width_x), BF),
        ],
        compiler_params=pltpu.CompilerParams(dimension_semantics=("arbitrary",)),
        name="demig",
    )(got, rows)
    returned = lax.all_to_all(modeled, ("gx", "gy"), split_axis=0, concat_axis=0, tiled=True)
    residual, outgoing = pl.pallas_call(
        functools.partial(residual_kernel, capacity),
        out_shape=(
            jax.ShapeDtypeStruct((traces, blocks, block_len), F32),
            jax.ShapeDtypeStruct((slots, blocks, block_len), BF),
        ),
        in_specs=[SMEM, VMEM, VMEM],
        out_specs=(VMEM, VMEM),
        name="resid",
    )(position, returned, observed)
    incoming = lax.all_to_all(outgoing, ("gx", "gy"), split_axis=0, concat_axis=0, tiled=True)
    levels = 4
    gradient = pl.pallas_call(
        functools.partial(image_kernel, bands, levels),
        grid=(depth // levels,),
        out_shape=jax.ShapeDtypeStruct((depth, width_x, width_y), F32),
        in_specs=[
            pl.BlockSpec((slots, 2 * width_x), lambda z: (0, 0)),
            pl.BlockSpec((slots, blocks, block_len), lambda z: (0, 0, 0)),
            pl.BlockSpec((bands * block_len, width_y), lambda z: (0, 0)),
        ],
        out_specs=pl.BlockSpec((levels, width_x, width_y), lambda z: (z, 0, 0)),
        scratch_shapes=[
            pltpu.VMEM((depth, slots, block_len), BF),
            pltpu.VMEM((depth, slots, width_x), BF),
            pltpu.VMEM((width_x, slots), BF),
            pltpu.VMEM((levels * width_x, bands * block_len), BF),
        ],
        compiler_params=pltpu.CompilerParams(dimension_semantics=("arbitrary",)),
        name="image",
    )(got, incoming, tables_flat)
    return residual, gradient


def solution(mesh):
    both = ("gx", "gy")
    placed = (
        P(None, "gx", "gy"),
        P(),
        P(both, None, None),
        P(both, None),
        P(both, None, None),
        P(both, None, None),
        P(both, None, None),
    )
    return jax.shard_map(
        shards,
        mesh=mesh,
        in_specs=placed,
        out_specs=(P(both, None, None), P(None, "gx", "gy")),
        check_vma=False,
    )
```

time: 188 us -> 119 us (0.63)
  blocking collectives: 0 us -> 61.9 us
  waiting for transfers between devices: 55.7 us -> 0.01 us
  matrix products: 58.2 us -> 9.45 us
  local copies, waits for them, and re-layouts: 40.2 us -> 0.65 us
  Pallas kernels: 0 us -> 38.4 us
  starting transfers between devices: 19.2 us -> 7.08 us
  other arithmetic: 10.4 us -> 0 us
    all_to_all x0 -> x2, blocking collectives: none -> 61.9 us  [the longest x1 32.3 us: shards(): lax.all_to_all(modeled, ('gx', 'gy'), split_axis=0, concat_axis=0, tiled=...]
    all_to_all x4 -> x1, waiting for transfers between devices: 55.7 us -> 0.01 us  [shards(): lax.all_to_all(message, ('gx', 'gy'), split_axis=0, concat_axis=0, tiled=...]
    dot_general x34 -> x0, matrix products: 48.8 us -> none  [the longest x16 26.9 us: image_depth(): jnp.dot(stacks.astype(jnp.bfloat16), tables_flat, preferred_element_type=...]
    pallas_call x0 -> x4, Pallas kernels: none -> 38.4 us  [the longest x1 16.6 us: shards(): pl.pallas_call(functools.partial(image_kernel, bands, levels), grid=(dept...]
    scatter x4 -> x0, local copies, waits for them, and re-layouts: 14.6 us -> none  [the longest x1 12.4 us: shards(): res_send = jnp.zeros((depth, slot_count, block_len), jnp.bfloat16).at[:,...]
    mul x18 -> x0, local copies, waits for them, and re-layouts: 13.7 us -> none  [the longest x16 13.5 us: image_depth(): pick[:, :, None] * res_level[:, None, :]]
    all_to_all x4 -> x1, starting transfers between devices: 19.2 us -> 7.08 us  [shards(): lax.all_to_all(message, ('gx', 'gy'), split_axis=0, concat_axis=0, tiled=...]
    mul x17 -> x0, other arithmetic: 6.04 us -> none  [the longest x16 5.36 us: image_depth(): pick[:, :, None] * res_level[:, None, :]]
  transfers between devices with their start and end apart: 4 -> 1, of which waited for: 3 -> 0; matrix products, arithmetic and copies ran while one was open for 7% -> 8% of each run, Pallas kernels for 0% -> 0%
where the time goes in v1:
time: 119 us; the launch traced here: 118 us
  blocking collectives  61.9 us (52%)
  Pallas kernels  38.4 us (32%)
  matrix products  9.45 us (8%)
  starting transfers between devices  7.08 us (6%)
    all_to_all x1, blocking collectives, shards(): lax.all_to_all(modeled, ('gx', 'gy'), split_axis=0, concat_axis=0, tiled=...  32.3 us
    all_to_all x1, blocking collectives, shards(): lax.all_to_all(outgoing, ('gx', 'gy'), split_axis=0, concat_axis=0, tiled...  29.6 us
    pallas_call x1, Pallas kernels, shards(): pl.pallas_call(functools.partial(image_kernel, bands, levels), grid=(dept...  16.6 us
    pallas_call x1, Pallas kernels, shards(): pl.pallas_call(functools.partial(demig_kernel, bands, blocks), grid=(dept...  16.6 us
    dot_general x1, matrix products, shards(): lax.dot_general(model_image.reshape(depth * width_x, width_y), tables_fla...  9.45 us
    all_to_all x1, starting transfers between devices, shards(): lax.all_to_all(message, ('gx', 'gy'), split_axis=0, concat_axis=0, tiled=...  7.08 us
    pallas_call x1, Pallas kernels, shards(): pl.pallas_call(functools.partial(residual_kernel, capacity), out_shape=(j...  2.93 us
  transfers between devices with their start and end apart: 1, of which 0 were waited for; matrix products, arithmetic and copies ran while one was open for 8% of the time, Pallas kernels for 0%

profile of v1, /device:TPU:1, one launch (start us, length us, event | category | flops | bytes accessed | tf_op | source)
XLA Modules:
  0.0 118.0 jit_solution(2493152242765585526)
XLA Ops:
  0.6 2.2 %prep.1 = (bf16[256,256]{1,0:T(8,128)(2,1)}, s32[4,32]{1,0:T(4,128)}) custom-call(s32[4,32]{1,0:T(4,128)} %bitcast.18, s32[4,16,32]{2,1,0:T(8,128)} %bitcast.16, s32[4,16,32]{2,1,0:T(8,128)} %bitcast.17, bf16[32,4,128]{2,1,0:T(4,128)(2,1)} %am_ref.1), custom_call_target="tpu_custom_call" | custom-call | tf_op jit(solution)/shard_map/prep/pallas_call | solution.py:165
  2.8 7.1 %all-to-all-start = ((bf16[32,8,256]{2,1,0:T(8,128)(2,1)}), bf16[32,8,256]{2,1,0:T(8,128)(2,1)S(1)}, u32[]{:S(2)}, u32[]{:S(2)}) async-start(bf16[32,8,256]{2,1,0:T(8,128)(2,1)} %bitcast.15), calls=%async_computation | async-start | bytes 262144 | tf_op jit(solution)/shard_map/all_to_all | solution.py:180
  9.9 9.4 %convolution_convert_fusion = bf16[2048,1024]{1,0:T(8,128)(2,1)} fusion(bf16[2048,1024]{1,0:T(8,128)(2,1)} %bitcast.19, bf16[1024,1024]{1,0:T(8,128)(2,1)} %bitcast.11), kind=kOutput, calls=%fused_computation | convolution fusion | flops 4297064448 | bytes 10485760 | tf_op jit(solution)/shard_map/dot_general | solution.py:181
  19.3 0.0 all-to-all-done
  19.3 0.0 copy-start
  19.3 0.7 copy-done
  20.0 16.6 %demig.1 = bf16[256,16,128]{2,1,0:T(8,128)(2,1)} custom-call(bf16[256,256]{1,0:T(8,128)(2,1)} %bitcast.13, bf16[16,128,1024]{2,1,0:T(8,128)(2,1)} %bitcast.10), custom_call_target="tpu_custom_call" | custom-call | tf_op jit(solution)/shard_map/demig/pallas_call | solution.py:189
  36.6 32.3 %all_to_all.21.recv_ref = bf16[256,16,128]{2,1,0:T(8,128)(2,1)} all-to-all(bf16[256,16,128]{2,1,0:T(8,128)(2,1)} %demig.1), channel_id=1, replica_groups=mesh['gx'=8,'gy'=4] {'gx','gy'}, dimensions={0} | all-to-all | bytes 2097152 | tf_op jit(solution)/shard_map/all_to_all | solution.py:205
  68.9 2.9 %resid.1 = (f32[32,16,128]{2,1,0:T(8,128)}, bf16[256,16,128]{2,1,0:T(8,128)(2,1)}) custom-call(s32[4,32]{1,0:T(4,128)} %get-tuple-element.6.pos_ref, bf16[256,16,128]{2,1,0:T(8,128)(2,1)} %all_to_all.21.recv_ref, bf16[32,16,128]{2,1,0:T(8,128)(2,1)} %obs_ref.1), custom_call_target="tpu_custom_call" | custom-call | tf_op jit(solution)/shard_map/resid/pallas_call | solution.py:206
  71.8 29.6 %all_to_all.22.blk_ref = bf16[256,16,128]{2,1,0:T(8,128)(2,1)} all-to-all(bf16[256,16,128]{2,1,0:T(8,128)(2,1)} %get-tuple-element.9), channel_id=1, replica_groups=mesh['gx'=8,'gy'=4] {'gx','gy'}, dimensions={0} | all-to-all | bytes 2097152 | tf_op jit(solution)/shard_map/all_to_all | solution.py:216
  101.4 16.6 %image.1 = f32[16,128,1024]{2,1,0:T(8,128)} custom-call(bf16[256,256]{1,0:T(8,128)(2,1)} %bitcast.14, bf16[256,16,128]{2,1,0:T(8,128)(2,1)} %all_to_all.22.blk_ref, bf16[1024,1024]{1,0:T(8,128)(2,1)} %bitcast.12), custom_call_target="tpu_custom_call" | custom-call | tf_op jit(solution)/shard_map/image/pallas_call | solution.py:218
Async XLA Ops:
  2.8 16.5 %all-to-all-start = ((bf16[32,8,256]{2,1,0:T(8,128)(2,1)}), bf16[32,8,256]{2,1,0:T(8,128)(2,1)S(1)}, u32[]{:S(2)}, u32[]{:S(2)}) async-start(bf16[32,8,256]{2,1,0:T(8,128)(2,1)} %bitcast.15), calls=%async_computation | async-start | bytes 262144 | tf_op jit(solution)/shard_map/all_to_all | solution.py:180
  19.3 0.7 copy-start

commit v2 on v1

--- a/solution.py
+++ b/solution.py
@@ -53,27 +53,34 @@
     msg_ref[:, width:] = marks.astype(BF)
 
 
-def spread(marks, lane):
+def spread(marks, first, second):
     width = marks.shape[1]
-    return dot(marks, (iota((width, width), 0) == lane).astype(F32).astype(BF))
-
-
-def demig_kernel(bands, blocks, msg_ref, rows_ref, out_ref, part_ref, time_ref):
-    z = pl.program_id(0)
+    lane = iota((width, 2 * width), 1)
+    want = jnp.where(lane < width, first, second)
+    return dot(marks, (iota((width, 2 * width), 0) == want).astype(F32).astype(BF)).astype(BF)
+
+
+def by_band(band, values, bands):
+    zero = jnp.zeros_like(values)
+    return jnp.concatenate([jnp.where(band == BF(b), values, zero) for b in range(bands)], axis=1)
+
+
+def demig_kernel(bands, blocks, levels, msg_ref, rows_ref, out_ref, part_ref, time_ref):
+    step = pl.program_id(0)
     depth, slots, block_len = part_ref.shape
     width = rows_ref.shape[1]
     amp = msg_ref[:, :width]
     marks = msg_ref[:, width:]
-    band = spread(marks, z)
-    time_ref[z] = spread(marks, z + depth).astype(BF)
-    zero = jnp.zeros_like(amp)
-    weights = jnp.concatenate([jnp.where(band == b, amp, zero) for b in range(bands)], axis=1)
-    rows = jnp.concatenate(
-        [rows_ref[0, :, b * block_len : (b + 1) * block_len] for b in range(bands)], axis=0
-    )
-    part_ref[z] = dot(weights, rows).astype(BF)
-
-    @pl.when(z == depth - 1)
+    for i in range(levels):
+        z = step * levels + i
+        both = spread(marks, z, z + depth)
+        time_ref[z] = both[:, width:]
+        rows = jnp.concatenate(
+            [rows_ref[i, :, b * block_len : (b + 1) * block_len] for b in range(bands)], axis=0
+        )
+        part_ref[z] = dot(by_band(both[:, :width], amp, bands), rows).astype(BF)
+
+    @pl.when(step == pl.num_programs(0) - 1)
     def _():
         group = 256 // depth
 
@@ -85,7 +92,7 @@
             out_ref[at] = total.astype(BF).reshape(group, blocks, block_len)
             return carry
 
-        lax.fori_loop(0, slots // group, one, 0)
+        lax.fori_loop(0, slots // group, one, 0, unroll=4)
 
 
 def picker(times, blocks):
@@ -128,8 +135,10 @@
     @pl.when(step == 0)
     def _():
         amp_ref[...] = msg_ref[:, :width].astype(F32).T.astype(BF)
-        for z in range(depth):
-            time_ref[z] = spread(marks, z + depth).astype(BF)
+        for z in range(0, depth, 2):
+            both = spread(marks, z + depth, z + 1 + depth)
+            time_ref[z] = both[:, :width]
+            time_ref[z + 1] = both[:, width:]
         group = 256 // depth
 
         def one(g, carry):
@@ -139,15 +148,15 @@
             pick_ref[:, at, :] = dot(pick, block).astype(BF).reshape(depth, group, block_len)
             return carry
 
-        lax.fori_loop(0, slots // group, one, 0)
-
-    for i in range(levels):
+        lax.fori_loop(0, slots // group, one, 0, unroll=4)
+
+    for i in range(0, levels, 2):
         z = step * levels + i
-        band = spread(marks, z)
-        picked = pick_ref[z]
-        zero = jnp.zeros_like(picked)
-        masked = jnp.concatenate([jnp.where(band == b, picked, zero) for b in range(bands)], axis=1)
-        stack_ref[i * width : (i + 1) * width, :] = dot(amp_ref[...], masked).astype(BF)
+        both = spread(marks, z, z + 1)
+        for j in range(2):
+            masked = by_band(both[:, j * width : (j + 1) * width], pick_ref[z + j], bands)
+            stack = dot(amp_ref[...], masked)
+            stack_ref[(i + j) * width : (i + j + 1) * width, :] = stack.astype(BF)
     image = dot(stack_ref[...], tab_ref[...])
     out_ref[...] = image.reshape(levels, width, image.shape[1])
 
@@ -160,6 +169,7 @@
     blocks = observed.shape[1]
     capacity = max(2, 2 * traces * tile_count // devices)
     slots = devices * capacity
+    levels = 4
     tables_flat = tables.reshape(bands * block_len, width_y)
 
     message, position = pl.pallas_call(
@@ -187,12 +197,12 @@
     rows = rows.astype(BF).reshape(depth, width_x, bands * block_len)
 
     modeled = pl.pallas_call(
-        functools.partial(demig_kernel, bands, blocks),
-        grid=(depth,),
+        functools.partial(demig_kernel, bands, blocks, levels),
+        grid=(depth // levels,),
         out_shape=jax.ShapeDtypeStruct((slots, blocks, block_len), BF),
         in_specs=[
             pl.BlockSpec((slots, 2 * width_x), lambda z: (0, 0)),
-            pl.BlockSpec((1, width_x, bands * block_len), lambda z: (z, 0, 0)),
+            pl.BlockSpec((levels, width_x, bands * block_len), lambda z: (z, 0, 0)),
         ],
         out_specs=pl.BlockSpec((slots, blocks, block_len), lambda z: (0, 0, 0)),
         scratch_shapes=[
@@ -214,7 +224,6 @@
         name="resid",
     )(position, returned, observed)
     incoming = lax.all_to_all(outgoing, ("gx", "gy"), split_axis=0, concat_axis=0, tiled=True)
-    levels = 4
     gradient = pl.pallas_call(
         functools.partial(image_kernel, bands, levels),
         grid=(depth // levels,),

time: 119 us -> 107 us (0.90)
  Pallas kernels: 38.4 us -> 26.6 us
    pallas_call x1, Pallas kernels: 16.6 us -> 8.95 us  [shards(): pl.pallas_call(functools.partial(demig_kernel, bands, blocks, levels), gr...]
    pallas_call x1, Pallas kernels: 16.6 us -> 12.6 us  [shards(): pl.pallas_call(functools.partial(image_kernel, bands, levels), grid=(dept...]
  transfers between devices with their start and end apart: 1 -> 1, of which waited for: 0 -> 0; matrix products, arithmetic and copies ran while one was open for 8% -> 9% of each run, Pallas kernels for 0% -> 0%
where the time goes in v2:
time: 107 us; the launch traced here: 106 us
  blocking collectives  61.9 us (58%)
  Pallas kernels  26.6 us (25%)
  matrix products  9.45 us (9%)
  starting transfers between devices  7.08 us (7%)
    all_to_all x1, blocking collectives, shards(): lax.all_to_all(modeled, ('gx', 'gy'), split_axis=0, concat_axis=0, tiled=...  32.3 us
    all_to_all x1, blocking collectives, shards(): lax.all_to_all(outgoing, ('gx', 'gy'), split_axis=0, concat_axis=0, tiled...  29.6 us
    pallas_call x1, Pallas kernels, shards(): pl.pallas_call(functools.partial(image_kernel, bands, levels), grid=(dept...  12.6 us
    dot_general x1, matrix products, shards(): lax.dot_general(model_image.reshape(depth * width_x, width_y), tables_fla...  9.45 us
    pallas_call x1, Pallas kernels, shards(): pl.pallas_call(functools.partial(demig_kernel, bands, blocks, levels), gr...  8.95 us
    all_to_all x1, starting transfers between devices, shards(): lax.all_to_all(message, ('gx', 'gy'), split_axis=0, concat_axis=0, tiled=...  7.08 us
    pallas_call x1, Pallas kernels, shards(): pl.pallas_call(functools.partial(residual_kernel, capacity), out_shape=(j...  2.93 us
    pallas_call x1, Pallas kernels, shards(): pl.pallas_call(functools.partial(prep_kernel, devices, capacity), out_sha...  2.17 us
  transfers between devices with their start and end apart: 1, of which 0 were waited for; matrix products, arithmetic and copies ran while one was open for 9% of the time, Pallas kernels for 0%

profile of v2, /device:TPU:1, one launch (start us, length us, event | category | flops | bytes accessed | tf_op | source)
XLA Modules:
  0.0 106.3 jit_solution(14726368772762393490)
XLA Ops:
  0.6 2.2 %prep.1 = (bf16[256,256]{1,0:T(8,128)(2,1)}, s32[4,32]{1,0:T(4,128)}) custom-call(s32[4,32]{1,0:T(4,128)} %bitcast.18, s32[4,16,32]{2,1,0:T(8,128)} %bitcast.16, s32[4,16,32]{2,1,0:T(8,128)} %bitcast.17, bf16[32,4,128]{2,1,0:T(4,128)(2,1)} %am_ref.1), custom_call_target="tpu_custom_call" | custom-call | tf_op jit(solution)/shard_map/prep/pallas_call | solution.py:175
  2.8 7.1 %all-to-all-start = ((bf16[32,8,256]{2,1,0:T(8,128)(2,1)}), bf16[32,8,256]{2,1,0:T(8,128)(2,1)S(1)}, u32[]{:S(2)}, u32[]{:S(2)}) async-start(bf16[32,8,256]{2,1,0:T(8,128)(2,1)} %bitcast.15), calls=%async_computation | async-start | bytes 262144 | tf_op jit(solution)/shard_map/all_to_all | solution.py:190
  9.9 9.4 %convolution_convert_fusion = bf16[2048,1024]{1,0:T(8,128)(2,1)} fusion(bf16[2048,1024]{1,0:T(8,128)(2,1)} %bitcast.19, bf16[1024,1024]{1,0:T(8,128)(2,1)} %bitcast.11), kind=kOutput, calls=%fused_computation | convolution fusion | flops 4297064448 | bytes 10485760 | tf_op jit(solution)/shard_map/dot_general | solution.py:191
  19.3 0.0 all-to-all-done
  19.3 0.0 copy-start
  19.3 0.7 copy-done
  20.0 9.0 %demig.1 = bf16[256,16,128]{2,1,0:T(8,128)(2,1)} custom-call(bf16[256,256]{1,0:T(8,128)(2,1)} %bitcast.13, bf16[16,128,1024]{2,1,0:T(8,128)(2,1)} %bitcast.10), custom_call_target="tpu_custom_call" | custom-call | tf_op jit(solution)/shard_map/demig/pallas_call | solution.py:199
  29.0 32.3 %all_to_all.21.recv_ref = bf16[256,16,128]{2,1,0:T(8,128)(2,1)} all-to-all(bf16[256,16,128]{2,1,0:T(8,128)(2,1)} %demig.1), channel_id=1, replica_groups=mesh['gx'=8,'gy'=4] {'gx','gy'}, dimensions={0} | all-to-all | bytes 2097152 | tf_op jit(solution)/shard_map/all_to_all | solution.py:215
  61.2 2.9 %resid.1 = (f32[32,16,128]{2,1,0:T(8,128)}, bf16[256,16,128]{2,1,0:T(8,128)(2,1)}) custom-call(s32[4,32]{1,0:T(4,128)} %get-tuple-element.6.pos_ref, bf16[256,16,128]{2,1,0:T(8,128)(2,1)} %all_to_all.21.recv_ref, bf16[32,16,128]{2,1,0:T(8,128)(2,1)} %obs_ref.1), custom_call_target="tpu_custom_call" | custom-call | tf_op jit(solution)/shard_map/resid/pallas_call | solution.py:216
  64.2 29.6 %all_to_all.22.blk_ref = bf16[256,16,128]{2,1,0:T(8,128)(2,1)} all-to-all(bf16[256,16,128]{2,1,0:T(8,128)(2,1)} %get-tuple-element.9), channel_id=1, replica_groups=mesh['gx'=8,'gy'=4] {'gx','gy'}, dimensions={0} | all-to-all | bytes 2097152 | tf_op jit(solution)/shard_map/all_to_all | solution.py:226
  93.7 12.6 %image.1 = f32[16,128,1024]{2,1,0:T(8,128)} custom-call(bf16[256,256]{1,0:T(8,128)(2,1)} %bitcast.14, bf16[256,16,128]{2,1,0:T(8,128)(2,1)} %all_to_all.22.blk_ref, bf16[1024,1024]{1,0:T(8,128)(2,1)} %bitcast.12), custom_call_target="tpu_custom_call" | custom-call | tf_op jit(solution)/shard_map/image/pallas_call | solution.py:227
Async XLA Ops:
  2.8 16.5 %all-to-all-start = ((bf16[32,8,256]{2,1,0:T(8,128)(2,1)}), bf16[32,8,256]{2,1,0:T(8,128)(2,1)S(1)}, u32[]{:S(2)}, u32[]{:S(2)}) async-start(bf16[32,8,256]{2,1,0:T(8,128)(2,1)} %bitcast.15), calls=%async_computation | async-start | bytes 262144 | tf_op jit(solution)/shard_map/all_to_all | solution.py:190
  19.3 0.7 copy-start

commit v3 on v2

--- a/solution.py
+++ b/solution.py
@@ -9,6 +9,7 @@
 
 BF = jnp.bfloat16
 F32 = jnp.float32
+GRANT = pltpu.CompilerParams(vmem_limit_bytes=20 * 1024 * 1024)
 VMEM = pl.BlockSpec(memory_space=pltpu.VMEM)
 SMEM = pl.BlockSpec(memory_space=pltpu.SMEM)
 
@@ -53,6 +54,12 @@
     msg_ref[:, width:] = marks.astype(BF)
 
 
+def rows_kernel(image_ref, tab_ref, out_ref):
+    levels, width, cells = image_ref.shape
+    rows = dot(image_ref[...].reshape(levels * width, cells), tab_ref[...], ((1,), (1,)))
+    out_ref[...] = rows.astype(BF).reshape(out_ref.shape)
+
+
 def spread(marks, first, second):
     width = marks.shape[1]
     lane = iota((width, 2 * width), 1)
@@ -97,13 +104,12 @@
 
 def picker(times, blocks):
     depth, group, lanes = times.shape
-    code = times.astype(F32).reshape(depth * group, lanes)
-    own = (iota((depth * group, lanes), 0) % group * blocks).astype(F32)
-    code = code + own
-    at = iota((depth * group, lanes), 1).astype(F32)
+    own = (iota((group, lanes), 0) * blocks).astype(F32).astype(BF)
+    code = (times + own[None]).reshape(depth * group, lanes)
+    at = iota(code.shape, 1).astype(F32).astype(BF)
+    one, zero = jnp.ones_like(code), jnp.zeros_like(code)
     return jnp.concatenate(
-        [(code == at + float(i)).astype(F32).astype(BF) for i in range(0, group * blocks, lanes)],
-        axis=1,
+        [jnp.where(code == at + BF(i), one, zero) for i in range(0, group * blocks, lanes)], axis=1
     )
 
 
@@ -112,17 +118,18 @@
     send_ref[...] = jnp.zeros_like(send_ref)
 
     def one(t, carry):
-        total = recv_ref[pos_ref[0, t]].astype(F32)
+        at = [pos_ref[k, t] for k in range(tiles)]
+        total = recv_ref[at[0]].astype(F32)
         for k in range(1, tiles):
-            total = total + recv_ref[pos_ref[k, t]].astype(F32)
+            total = total + recv_ref[at[k]].astype(F32)
         total = total - obs_ref[t].astype(F32)
         res_ref[t] = total
         low = total.astype(BF)
         for k in range(tiles):
-            send_ref[pos_ref[k, t]] = low
+            send_ref[at[k]] = low
         return carry
 
-    lax.fori_loop(0, traces, one, 0)
+    lax.fori_loop(0, traces, one, 0, unroll=4)
 
 
 def image_kernel(bands, levels, msg_ref, blk_ref, tab_ref, out_ref, pick_ref, time_ref, amp_ref, stack_ref):
@@ -188,14 +195,23 @@
         amplitude,
     )
     got = lax.all_to_all(message, ("gx", "gy"), split_axis=0, concat_axis=0, tiled=True)
-    rows = lax.dot_general(
-        model_image.reshape(depth * width_x, width_y),
-        tables_flat,
-        (((1,), (1,)), ((), ())),
-        preferred_element_type=F32,
-    )
-    rows = rows.astype(BF).reshape(depth, width_x, bands * block_len)
-
+    rows = pl.pallas_call(
+        rows_kernel,
+        grid=(depth // levels,),
+        out_shape=jax.ShapeDtypeStruct((depth, width_x, bands * block_len), BF),
+        in_specs=[
+            pl.BlockSpec((levels, width_x, width_y), lambda z: (z, 0, 0)),
+            pl.BlockSpec((bands * block_len, width_y), lambda z: (0, 0)),
+        ],
+        out_specs=pl.BlockSpec((levels, width_x, bands * block_len), lambda z: (z, 0, 0)),
+        cost_estimate=pl.CostEstimate(
+            flops=2 * depth * width_x * width_y * bands * block_len,
+            bytes_accessed=4 * depth * width_x * width_y,
+            transcendentals=0,
+        ),
+        name="rows",
+    )(model_image, tables_flat)
+    rows = pltpu.with_memory_space_constraint(rows, pltpu.HBM)
     modeled = pl.pallas_call(
         functools.partial(demig_kernel, bands, blocks, levels),
         grid=(depth // levels,),
@@ -209,7 +225,7 @@
             pltpu.VMEM((depth, slots, block_len), BF),
             pltpu.VMEM((depth, slots, width_x), BF),
         ],
-        compiler_params=pltpu.CompilerParams(dimension_semantics=("arbitrary",)),
+        compiler_params=GRANT,
         name="demig",
     )(got, rows)
     returned = lax.all_to_all(modeled, ("gx", "gy"), split_axis=0, concat_axis=0, tiled=True)
@@ -221,6 +237,7 @@
         ),
         in_specs=[SMEM, VMEM, VMEM],
         out_specs=(VMEM, VMEM),
+        compiler_params=GRANT,
         name="resid",
     )(position, returned, observed)
     incoming = lax.all_to_all(outgoing, ("gx", "gy"), split_axis=0, concat_axis=0, tiled=True)
@@ -240,7 +257,7 @@
             pltpu.VMEM((width_x, slots), BF),
             pltpu.VMEM((levels * width_x, bands * block_len), BF),
         ],
-        compiler_params=pltpu.CompilerParams(dimension_semantics=("arbitrary",)),
+        compiler_params=GRANT,
         name="image",
     )(got, incoming, tables_flat)
     return residual, gradient

time: 107 us -> 100 us (0.935)
  matrix products: 9.45 us -> 0 us
  Pallas kernels: 26.6 us -> 31 us
    dot_general x1 -> x0, matrix products: 9.45 us -> none  [shards(): lax.dot_general(model_image.reshape(depth * width_x, width_y), tables_fla...]
    pallas_call x0 -> x1, Pallas kernels: none -> 8.47 us  [shards(): pl.pallas_call(rows_kernel, grid=(depth // levels,), out_shape=jax.ShapeD...]
    pallas_call x1, Pallas kernels: 12.6 us -> 10.6 us  [shards(): pl.pallas_call(functools.partial(image_kernel, bands, levels), grid=(dept...]
    pallas_call x1, Pallas kernels: 2.93 us -> 1.71 us  [shards(): pl.pallas_call(functools.partial(residual_kernel, capacity), out_shape=(j...]
  transfers between devices with their start and end apart: 1 -> 1, of which waited for: 0 -> 0; matrix products, arithmetic and copies ran while one was open for 9% -> 0% of each run, Pallas kernels for 0% -> 8%
where the time goes in v3:
time: 100 us
  blocking collectives  61.2 us (61%)
  Pallas kernels  31 us (31%)
  starting transfers between devices  7.08 us (7%)
    all_to_all x1, blocking collectives, shards(): lax.all_to_all(modeled, ('gx', 'gy'), split_axis=0, concat_axis=0, tiled=...  31.9 us
    all_to_all x1, blocking collectives, shards(): lax.all_to_all(outgoing, ('gx', 'gy'), split_axis=0, concat_axis=0, tiled...  29.3 us
    pallas_call x1, Pallas kernels, shards(): pl.pallas_call(functools.partial(image_kernel, bands, levels), grid=(dept...  10.6 us
    pallas_call x1, Pallas kernels, shards(): pl.pallas_call(rows_kernel, grid=(depth // levels,), out_shape=jax.ShapeD...  8.47 us
    pallas_call x1, Pallas kernels, shards(): pl.pallas_call(functools.partial(demig_kernel, bands, blocks, levels), gr...  8.02 us
    all_to_all x1, starting transfers between devices, shards(): lax.all_to_all(message, ('gx', 'gy'), split_axis=0, concat_axis=0, tiled=...  7.08 us
    pallas_call x1, Pallas kernels, shards(): pl.pallas_call(functools.partial(prep_kernel, devices, capacity), out_sha...  2.17 us
  transfers between devices with their start and end apart: 1, of which 0 were waited for; matrix products, arithmetic and copies ran while one was open for 0% of the time, Pallas kernels for 8%

profile of v3, /device:TPU:1, one launch (start us, length us, event | category | flops | bytes accessed | tf_op | source)
XLA Modules:
  0.0 100.0 jit_solution(3523532584544370815)
XLA Ops:
  0.6 2.2 %prep.1 = (bf16[256,256]{1,0:T(8,128)(2,1)}, s32[4,32]{1,0:T(4,128)}) custom-call(s32[4,32]{1,0:T(4,128)} %bitcast.13, s32[4,16,32]{2,1,0:T(8,128)} %bitcast.11, s32[4,16,32]{2,1,0:T(8,128)} %bitcast.12, bf16[32,4,128]{2,1,0:T(4,128)(2,1)} %am_ref.1), custom_call_target="tpu_custom_call" | custom-call | tf_op jit(solution)/shard_map/prep/pallas_call | solution.py:182
  2.8 7.1 %all-to-all-start = ((bf16[32,8,256]{2,1,0:T(8,128)(2,1)}), bf16[32,8,256]{2,1,0:T(8,128)(2,1)S(1)}, u32[]{:S(2)}, u32[]{:S(2)}) async-start(bf16[32,8,256]{2,1,0:T(8,128)(2,1)} %bitcast.10), calls=%async_computation | async-start | bytes 262144 | tf_op jit(solution)/shard_map/all_to_all | solution.py:197
  9.9 8.5 %rows.1.rows_ref = bf16[16,128,1024]{2,1,0:T(8,128)(2,1)} custom-call(bf16[16,128,1024]{2,1,0:T(8,128)(2,1)} %image_ref.1, bf16[1024,1024]{1,0:T(8,128)(2,1)} %bitcast.6), custom_call_target="tpu_custom_call" | custom-call | flops 4294967296 | bytes 8388608 | tf_op jit(solution)/shard_map/rows/pallas_call | solution.py:198
  18.4 0.0 copy-start.1
  18.4 0.0 copy-start.2
  18.4 0.0 all-to-all-done
  18.4 0.0 copy-start
  18.4 8.0 %demig.1 = bf16[256,16,128]{2,1,0:T(8,128)(2,1)S(1)} custom-call(bf16[256,256]{1,0:T(8,128)(2,1)S(1)} %bitcast.8, bf16[16,128,1024]{2,1,0:T(8,128)(2,1)} %rows.1.rows_ref), custom_call_target="tpu_custom_call" | custom-call | tf_op jit(solution)/shard_map/demig/pallas_call | solution.py:215
  26.4 31.9 %all_to_all.21.recv_ref = bf16[256,16,128]{2,1,0:T(8,128)(2,1)S(1)} all-to-all(bf16[256,16,128]{2,1,0:T(8,128)(2,1)S(1)} %demig.1), channel_id=1, replica_groups=mesh['gx'=8,'gy'=4] {'gx','gy'}, dimensions={0} | all-to-all | bytes 2097152 | tf_op jit(solution)/shard_map/all_to_all | solution.py:231
  58.4 0.0 copy-done.1
  58.4 0.0 copy-done.2
  58.4 1.7 %resid.1 = (f32[32,16,128]{2,1,0:T(8,128)}, bf16[256,16,128]{2,1,0:T(8,128)(2,1)S(1)}) custom-call(s32[4,32]{1,0:T(4,128)S(1)} %copy-done.2, bf16[256,16,128]{2,1,0:T(8,128)(2,1)S(1)} %all_to_all.21.recv_ref, bf16[32,16,128]{2,1,0:T(8,128)(2,1)S(1)} %copy-done.1), custom_call_target="tpu_custom_call" | custom-call | tf_op jit(solution)/shard_map/resid/pallas_call | solution.py:232
  60.1 29.3 %all_to_all.22.blk_ref = bf16[256,16,128]{2,1,0:T(8,128)(2,1)S(1)} all-to-all(bf16[256,16,128]{2,1,0:T(8,128)(2,1)S(1)} %get-tuple-element.9), channel_id=1, replica_groups=mesh['gx'=8,'gy'=4] {'gx','gy'}, dimensions={0} | all-to-all | bytes 2097152 | tf_op jit(solution)/shard_map/all_to_all | solution.py:243
  89.3 0.0 copy-done
  89.3 10.6 %image.1 = f32[16,128,1024]{2,1,0:T(8,128)} custom-call(bf16[256,256]{1,0:T(8,128)(2,1)S(1)} %bitcast.9, bf16[256,16,128]{2,1,0:T(8,128)(2,1)S(1)} %all_to_all.22.blk_ref, bf16[1024,1024]{1,0:T(8,128)(2,1)S(1)} %bitcast.7), custom_call_target="tpu_custom_call" | custom-call | tf_op jit(solution)/shard_map/image/pallas_call | solution.py:244
Async XLA Ops:
  2.8 15.6 %all-to-all-start = ((bf16[32,8,256]{2,1,0:T(8,128)(2,1)}), bf16[32,8,256]{2,1,0:T(8,128)(2,1)S(1)}, u32[]{:S(2)}, u32[]{:S(2)}) async-start(bf16[32,8,256]{2,1,0:T(8,128)(2,1)} %bitcast.10), calls=%async_computation | async-start | bytes 262144 | tf_op jit(solution)/shard_map/all_to_all | solution.py:197
  18.4 40.0 %copy-start.1 = (bf16[32,16,128]{2,1,0:T(8,128)(2,1)S(1)}, bf16[32,16,128]{2,1,0:T(8,128)(2,1)}, u32[]{:S(2)}) copy-start(bf16[32,16,128]{2,1,0:T(8,128)(2,1)} %obs_ref.1) | copy-start | bytes 393220
  18.4 40.0 %copy-start.2 = (s32[4,32]{1,0:T(4,128)S(1)}, s32[4,32]{1,0:T(4,128)}, u32[]{:S(2)}) copy-start(s32[4,32]{1,0:T(4,128)} %get-tuple-element.6.pos_ref) | copy-start | bytes 1540
  18.4 71.0 %copy-start = (bf16[8,128,1024]{2,1,0:T(8,128)(2,1)S(1)}, bf16[8,128,1024]{2,1,0:T(8,128)(2,1)}, u32[]{:S(2)}) copy-start(bf16[8,128,1024]{2,1,0:T(8,128)(2,1)} %param.8) | copy-start | bytes 6291460

commit v4 on v3

v4 whole, which is shorter than its diff:
```python
import functools

import jax
import jax.numpy as jnp
from jax import lax
from jax.experimental import pallas as pl
from jax.experimental.pallas import tpu as pltpu
from jax.sharding import PartitionSpec as P

BF = jnp.bfloat16
F32 = jnp.float32
GRANT = pltpu.CompilerParams(vmem_limit_bytes=20 * 1024 * 1024)
VMEM = pl.BlockSpec(memory_space=pltpu.VMEM)


def dot(a, b, dims=((1,), (0,))):
    return lax.dot_general(a, b, (dims, ((), ())), preferred_element_type=F32)


def iota(shape, axis):
    return lax.broadcasted_iota(jnp.int32, shape, axis)


def prep_kernel(devices, capacity, ap_ref, bi_ref, am_ref, msg_ref, place_ref):
    tiles, traces = ap_ref.shape
    slots = devices * capacity
    width = am_ref.shape[2]
    depth = bi_ref.shape[1]
    before = (iota((traces, traces), 0) < iota((traces, traces), 1)).astype(BF)
    base = jnp.zeros((devices, 1), F32)
    amp = jnp.zeros((slots, width), F32)
    marks = jnp.zeros((slots, width), F32)
    for k in range(tiles):
        dest = ap_ref[k : k + 1, :]
        hit = iota((devices, traces), 0) == dest
        hits = hit.astype(F32)
        rank = jnp.sum(hits * (base + dot(hits.astype(BF), before)), axis=0, keepdims=True)
        base = base + jnp.sum(hits, axis=1, keepdims=True)
        pos = dest * capacity + rank.astype(jnp.int32)
        place = (iota((slots, traces), 0) == pos).astype(F32).astype(BF)
        place_ref[:, k * traces : (k + 1) * traces] = place
        amp = amp + dot(place, am_ref[:, k, :])
        levels = jnp.concatenate(
            [bi_ref[k].astype(F32), jnp.zeros((width - depth, traces), F32)], axis=0
        ).astype(BF)
        marks = marks + dot(place, levels, ((1,), (1,)))
    msg_ref[:, :width] = amp.astype(BF)
    msg_ref[:, width:] = marks.astype(BF)


def codes_kernel(blocks, place_ref, tt_ref, take_ref, pick_ref, drop_ref):
    tiles, depth, traces = tt_ref.shape
    group = 256 // blocks
    take_ref[...] = place_ref[...].astype(F32).T.astype(BF)
    size = depth * group
    lanes = 128
    at = iota((size, lanes), 1).astype(F32).astype(BF)
    row = iota((size, 1), 0)
    level = (row // group == iota((size, depth), 1)).astype(F32).astype(BF)
    for k in range(tiles):
        times = dot(level, tt_ref[k].astype(F32).astype(BF))
        for h in range(traces // group):
            own = iota((size, traces), 1) == row % group + h * group
            code = jnp.where(own, times, 0.0).astype(BF)
            code = dot(code, jnp.ones((traces, lanes), F32).astype(BF))
            code = (code + (row % group * blocks).astype(F32)).astype(BF)
            one, zero = jnp.ones_like(code), jnp.zeros_like(code)
            pick = jnp.concatenate(
                [jnp.where(code == at + BF(i), one, zero) for i in range(0, group * blocks, lanes)],
                axis=1,
            )
            pick_ref[k * (traces // group) + h] = pick
            drop_ref[k * (traces // group) + h] = pick.astype(F32).T.astype(BF)


def by_band(band, values, bands):
    zero = jnp.zeros_like(values)
    return jnp.concatenate([jnp.where(band == BF(b), values, zero) for b in range(bands)], axis=1)


def spread(marks, first, second):
    width = marks.shape[1]
    lane = iota((width, 2 * width), 1)
    want = jnp.where(lane < width, first, second)
    return dot(marks, (iota((width, 2 * width), 0) == want).astype(F32).astype(BF)).astype(BF)


def put(ref, z, value):
    if len(ref.shape) == 4:
        ref[:, z] = value.reshape(ref.shape[0], ref.shape[2], ref.shape[3])
    else:
        ref[z] = value


def get(ref, z):
    if len(ref.shape) == 4:
        return ref[:, z].reshape(ref.shape[0] * ref.shape[2], ref.shape[3])
    return ref[z]


def rows_kernel(image_ref, tab_ref, out_ref):
    levels, width, cells = image_ref.shape
    rows = dot(image_ref[...].reshape(levels * width, cells), tab_ref[...], ((1,), (1,)))
    out_ref[...] = rows.astype(BF).reshape(out_ref.shape)


def demig(bands, first, msg_ref, rows, out_ref):
    levels, width, long = rows.shape
    block_len = long // bands
    amp = msg_ref[:, :width]
    marks = msg_ref[:, width:]
    for i in range(0, levels, 2):
        z = first + i
        both = spread(marks, z, z + 1)
        for j in range(2):
            level = jnp.concatenate(
                [rows[i + j, :, b * block_len : (b + 1) * block_len] for b in range(bands)], axis=0
            )
            weights = by_band(both[:, j * width : (j + 1) * width], amp, bands)
            put(out_ref, i + j, dot(weights, level).astype(BF))


def demig_kernel(bands, base, msg_ref, rows_ref, out_ref):
    levels = rows_ref.shape[0]
    demig(bands, base + pl.program_id(0) * levels, msg_ref, rows_ref[...], out_ref)


def whole_kernel(bands, base, msg_ref, image_ref, tab_ref, out_ref):
    levels, width, cells = image_ref.shape
    rows = dot(image_ref[...].reshape(levels * width, cells), tab_ref[...], ((1,), (1,)))
    rows = rows.astype(BF).reshape(levels, width, tab_ref.shape[0])
    demig(bands, base + pl.program_id(0) * levels, msg_ref, rows, out_ref)


def residual_kernel(depth, parts, *refs):
    place_ref, take_ref, pick_ref, drop_ref, obs_ref = refs[:5]
    recv = refs[5 : 5 + parts]
    res_ref, send_ref, pair_ref = refs[5 + parts :]
    traces, blocks, block_len = obs_ref.shape
    group = 256 // blocks
    halves = traces // group
    tiles = pick_ref.shape[0] // halves
    take = take_ref[...]
    per = depth // parts
    for z in range(depth):
        pair_ref[z] = dot(take, get(recv[z // per], z % per)).astype(BF)
    for h in range(halves):
        total = -obs_ref[h * group : (h + 1) * group].astype(F32).reshape(group * blocks, block_len)
        for k in range(tiles):
            at = slice(k * traces + h * group, k * traces + (h + 1) * group)
            part = pair_ref[:, at, :].reshape(depth * group, block_len)
            total = total + dot(drop_ref[k * halves + h], part)
        res_ref[h * group : (h + 1) * group] = total.reshape(group, blocks, block_len)
        low = total.astype(BF)
        for k in range(tiles):
            at = slice(k * traces + h * group, k * traces + (h + 1) * group)
            got = dot(pick_ref[k * halves + h], low).astype(BF)
            pair_ref[:, at, :] = got.reshape(depth, group, block_len)
    place = place_ref[...]
    for z in range(depth):
        put(send_ref, z, dot(place, pair_ref[z]).astype(BF))


def image_kernel(bands, msg_ref, blk_ref, tab_ref, out_ref, amp_ref, stack_ref):
    step = pl.program_id(0)
    levels, width, cells = out_ref.shape
    marks = msg_ref[:, width:]

    @pl.when(step == 0)
    def _():
        amp_ref[...] = msg_ref[:, :width].astype(F32).T.astype(BF)

    for i in range(0, levels, 2):
        z = step * levels + i
        both = spread(marks, z, z + 1)
        for j in range(2):
            masked = by_band(both[:, j * width : (j + 1) * width], get(blk_ref, i + j), bands)
            stack = dot(amp_ref[...], masked)
            stack_ref[(i + j) * width : (i + j + 1) * width, :] = stack.astype(BF)
    out_ref[...] = dot(stack_ref[...], tab_ref[...]).reshape(levels, width, cells)


def shards(model_image, tables, observed, aperture, traveltime, band_index, amplitude):
    devices = lax.axis_size("gx") * lax.axis_size("gy")
    depth, width_x, width_y = model_image.shape
    bands, block_len, _ = tables.shape
    traces, tile_count = aperture.shape
    blocks = observed.shape[1]
    capacity = max(2, 2 * traces * tile_count // devices)
    slots = devices * capacity
    pairs = traces * tile_count
    long = bands * block_len
    levels = 4
    aligned = capacity % 8 == 0
    groups = pairs * blocks // 256
    tables_flat = tables.reshape(long, width_y)

    def cost(flops, moved):
        return pl.CostEstimate(flops=flops, bytes_accessed=moved, transcendentals=0)

    def shape_of(count):
        if aligned:
            return (devices, count, capacity, block_len)
        return (count, slots, block_len)

    def block_of(count):
        if aligned:
            return pl.BlockSpec((devices, count, capacity, block_len), lambda z: (0, z, 0, 0))
        return pl.BlockSpec((count, slots, block_len), lambda z: (z, 0, 0))

    def exchange(x):
        if not aligned:
            x = x.reshape(-1, devices, capacity, block_len).transpose(1, 0, 2, 3)
        x = lax.all_to_all(x, ("gx", "gy"), split_axis=0, concat_axis=0, tiled=True)
        if not aligned:
            x = x.transpose(1, 0, 2, 3).reshape(-1, slots, block_len)
        return x

    message, place = pl.pallas_call(
        functools.partial(prep_kernel, devices, capacity),
        out_shape=(
            jax.ShapeDtypeStruct((slots, 2 * width_x), BF),
            jax.ShapeDtypeStruct((slots, pairs), BF),
        ),
        in_specs=[VMEM] * 3,
        out_specs=(VMEM, VMEM),
        name="prep",
    )(aperture.T, band_index.transpose(1, 2, 0), amplitude)
    got = lax.all_to_all(message, ("gx", "gy"), split_axis=0, concat_axis=0, tiled=True)

    half = depth // 2
    rows = pl.pallas_call(
        rows_kernel,
        grid=(half // levels,),
        out_shape=jax.ShapeDtypeStruct((half, width_x, long), BF),
        in_specs=[
            pl.BlockSpec((levels, width_x, width_y), lambda z: (z, 0, 0)),
            pl.BlockSpec((long, width_y), lambda z: (0, 0)),
        ],
        out_specs=pl.BlockSpec((levels, width_x, long), lambda z: (z, 0, 0)),
        cost_estimate=cost(2 * half * width_x * width_y * long, 4 * half * width_x * width_y),
        name="rows",
    )(model_image, tables_flat)
    rows = pltpu.with_memory_space_constraint(rows, pltpu.HBM)
    message_spec = pl.BlockSpec((slots, 2 * width_x), lambda z: (0, 0))
    first = pl.pallas_call(
        functools.partial(demig_kernel, bands, 0),
        grid=(half // levels,),
        out_shape=jax.ShapeDtypeStruct(shape_of(half), BF),
        in_specs=[message_spec, pl.BlockSpec((levels, width_x, long), lambda z: (z, 0, 0))],
        out_specs=block_of(levels),
        compiler_params=GRANT,
        cost_estimate=cost(2 * half * slots * width_x * long, 2 * half * width_x * long),
        name="demig",
    )(got, rows)
    back = exchange(first)
    _, image_late = lax.optimization_barrier((first, model_image))
    second = pl.pallas_call(
        functools.partial(whole_kernel, bands, half),
        grid=((depth - half) // levels,),
        out_shape=jax.ShapeDtypeStruct(shape_of(depth - half), BF),
        in_specs=[
            message_spec,
            pl.BlockSpec((levels, width_x, width_y), lambda z: (z + half // levels, 0, 0)),
            pl.BlockSpec((long, width_y), lambda z: (0, 0)),
        ],
        out_specs=block_of(levels),
        cost_estimate=cost(
            2 * (depth - half) * width_x * long * (width_y + slots), 4 * half * width_x * width_y
        ),
        name="whole",
    )(got, image_late, tables_flat)
    back_late = exchange(second)
    take, pick, drop = pl.pallas_call(
        functools.partial(codes_kernel, blocks),
        out_shape=(
            jax.ShapeDtypeStruct((pairs, slots), BF),
            jax.ShapeDtypeStruct((groups, 256, 256), BF),
            jax.ShapeDtypeStruct((groups, 256, 256), BF),
        ),
        in_specs=[VMEM, VMEM],
        out_specs=(VMEM,) * 3,
        compiler_params=GRANT,
        cost_estimate=cost(groups * 256 * 256 * 256, groups * 256 * 256 * 4),
        name="codes",
    )(place, traveltime.transpose(1, 2, 0))
    residual, outgoing = pl.pallas_call(
        functools.partial(residual_kernel, depth, 2),
        out_shape=(
            jax.ShapeDtypeStruct((traces, blocks, block_len), F32),
            jax.ShapeDtypeStruct(shape_of(depth), BF),
        ),
        in_specs=[VMEM] * 7,
        out_specs=(VMEM, VMEM),
        scratch_shapes=[pltpu.VMEM((depth, pairs, block_len), BF)],
        compiler_params=GRANT,
        cost_estimate=cost(4 * depth * slots * pairs * block_len, 4 * depth * slots * block_len),
        name="resid",
    )(place, take, pick, drop, observed, back, back_late)
    incoming = exchange(outgoing)
    gradient = pl.pallas_call(
        functools.partial(image_kernel, bands),
        grid=(depth // levels,),
        out_shape=jax.ShapeDtypeStruct((depth, width_x, width_y), F32),
        in_specs=[
            message_spec,
            block_of(levels),
            pl.BlockSpec((long, width_y), lambda z: (0, 0)),
        ],
        out_specs=pl.BlockSpec((levels, width_x, width_y), lambda z: (z, 0, 0)),
        scratch_shapes=[
            pltpu.VMEM((width_x, slots), BF),
            pltpu.VMEM((levels * width_x, long), BF),
        ],
        compiler_params=GRANT,
        cost_estimate=cost(
            2 * depth * width_x * long * (width_y + slots), 4 * depth * width_x * width_y
        ),
        name="image",
    )(got, incoming, tables_flat)
    return residual, gradient


def solution(mesh):
    both = ("gx", "gy")
    placed = (
        P(None, "gx", "gy"),
        P(),
        P(both, None, None),
        P(both, None),
        P(both, None, None),
        P(both, None, None),
        P(both, None, None),
    )
    return jax.shard_map(
        shards,
        mesh=mesh,
        in_specs=placed,
        out_specs=(P(both, None, None), P(None, "gx", "gy")),
        check_vma=False,
    )
```

time: 100 us -> 102 us (1.020)
  blocking collectives: 61.2 us -> 29.3 us
  waiting for transfers between devices: 0.01 us -> 22.3 us
  starting transfers between devices: 7.08 us -> 14.2 us
  local copies, waits for them, and re-layouts: 0.01 us -> 4.42 us
    all_to_all x2 -> x1, blocking collectives: 61.2 us -> 29.3 us  [exchange(): x = lax.all_to_all(x, ('gx', 'gy'), split_axis=0, concat_axis=0, tiled=True)]
    all_to_all x0 -> x2, waiting for transfers between devices: none -> 20.5 us  [exchange(): x = lax.all_to_all(x, ('gx', 'gy'), split_axis=0, concat_axis=0, tiled=True)]
    all_to_all x0 -> x2, starting transfers between devices: none -> 7.12 us  [exchange(): x = lax.all_to_all(x, ('gx', 'gy'), split_axis=0, concat_axis=0, tiled=True)]
    unnamed x6 -> x20, local copies, waits for them, and re-layouts: 0.01 us -> 4.42 us
    all_to_all x1, waiting for transfers between devices: 0.01 us -> 1.88 us  [shards(): lax.all_to_all(message, ('gx', 'gy'), split_axis=0, concat_axis=0, tiled=...]
    pallas_call x4 -> x6, Pallas kernels: 28.8 us -> 28.5 us  [the longest x1 9.18 us: shards(): pl.pallas_call(functools.partial(image_kernel, bands), grid=(depth // lev...]
  transfers between devices with their start and end apart: 1 -> 3, of which waited for: 0 -> 3; matrix products, arithmetic and copies ran while one was open for 0% -> 0% of each run, Pallas kernels for 8% -> 13%
where the time goes in v4:
time: 102 us
  Pallas kernels  30.7 us (30%)
  blocking collectives  29.3 us (29%)
  waiting for transfers between devices  22.3 us (22%)
  starting transfers between devices  14.2 us (14%)
  local copies, waits for them, and re-layouts  4.42 us (4%)
    all_to_all x1, blocking collectives, exchange(): x = lax.all_to_all(x, ('gx', 'gy'), split_axis=0, concat_axis=0, tiled=True)  29.3 us
    all_to_all x2, waiting for transfers between devices, exchange(): x = lax.all_to_all(x, ('gx', 'gy'), split_axis=0, concat_axis=0, tiled=True)  20.5 us
    pallas_call x1, Pallas kernels, shards(): pl.pallas_call(functools.partial(image_kernel, bands), grid=(depth // lev...  9.18 us
    all_to_all x2, starting transfers between devices, exchange(): x = lax.all_to_all(x, ('gx', 'gy'), split_axis=0, concat_axis=0, tiled=True)  7.12 us
    all_to_all x1, starting transfers between devices, shards(): lax.all_to_all(message, ('gx', 'gy'), split_axis=0, concat_axis=0, tiled=...  7.08 us
    pallas_call x1, Pallas kernels, shards(): pl.pallas_call(functools.partial(whole_kernel, bands, half), grid=((depth...  7.07 us
    pallas_call x1, Pallas kernels, shards(): pl.pallas_call(rows_kernel, grid=(half // levels,), out_shape=jax.ShapeDt...  5.49 us
    unnamed x20, local copies, waits for them, and re-layouts  4.42 us
  transfers between devices with their start and end apart: 3, of which 3 were waited for; matrix products, arithmetic and copies ran while one was open for 0% of the time, Pallas kernels for 13%

profile of v4, /device:TPU:1, one launch (start us, length us, event | category | flops | bytes accessed | tf_op | source)
XLA Modules:
  0.0 101.6 jit_solution(13575097440840183051)
XLA Ops:
  0.6 2.2 %prep.1 = (bf16[256,256]{1,0:T(8,128)(2,1)}, bf16[256,128]{1,0:T(8,128)(2,1)}) custom-call(s32[4,32]{1,0:T(4,128)} %bitcast.15, s32[4,16,32]{2,1,0:T(8,128)} %bitcast.14, bf16[32,4,128]{2,1,0:T(4,128)(2,1)} %am_ref.1), custom_call_target="tpu_custom_call" | custom-call | tf_op jit(solution)/shard_map/prep/pallas_call | solution.py:219
  2.8 7.1 %all-to-all-start = ((bf16[32,8,256]{2,1,0:T(8,128)(2,1)}), bf16[32,8,256]{2,1,0:T(8,128)(2,1)S(1)}, u32[]{:S(2)}, u32[]{:S(2)}) async-start(bf16[32,8,256]{2,1,0:T(8,128)(2,1)} %bitcast.13), calls=%async_computation | async-start | bytes 262144 | tf_op jit(solution)/shard_map/all_to_all | solution.py:229
  9.9 5.5 %rows.1.rows_ref = bf16[8,128,1024]{2,1,0:T(8,128)(2,1)} custom-call(bf16[16,128,1024]{2,1,0:T(8,128)(2,1)} %image_ref.2, bf16[1024,1024]{1,0:T(8,128)(2,1)} %bitcast.6), custom_call_target="tpu_custom_call" | custom-call | flops 2147483648 | bytes 4194304 | tf_op jit(solution)/shard_map/rows/pallas_call | solution.py:232
  15.4 1.9 %all-to-all-done = bf16[32,8,256]{2,1,0:T(8,128)(2,1)S(1)} async-done(((bf16[32,8,256]{2,1,0:T(8,128)(2,1)}), bf16[32,8,256]{2,1,0:T(8,128)(2,1)S(1)}, u32[]{:S(2)}, u32[]{:S(2)}) %all-to-all-start) | async-done | bytes 131104 | tf_op jit(solution)/shard_map/all_to_all | solution.py:229
  17.3 0.0 copy-start.5
  17.3 4.0 %demig.1 = bf16[32,8,8,128]{3,2,1,0:T(8,128)(2,1)} custom-call(bf16[256,256]{1,0:T(8,128)(2,1)S(1)} %bitcast.9, bf16[8,128,1024]{2,1,0:T(8,128)(2,1)} %rows.1.rows_ref), custom_call_target="tpu_custom_call" | custom-call | flops 536870912 | bytes 2097152 | tf_op jit(solution)/shard_map/demig/pallas_call | solution.py:246
  21.2 4.0 %all-to-all-start.1 = ((bf16[32,8,8,128]{3,2,1,0:T(8,128)(2,1)}), bf16[32,8,8,128]{3,2,1,0:T(8,128)(2,1)S(1)}, u32[]{:S(2)}, u32[]{:S(2)}) async-start(bf16[32,8,8,128]{3,2,1,0:T(8,128)(2,1)} %demig.1), calls=%async_computation.1 | async-start | bytes 1048576 | tf_op jit(solution)/shard_map/all_to_all | solution.py:214
  25.2 0.0 copy-done.5
  25.2 0.0 copy-start.8
  25.2 0.0 copy-start.9
  25.2 0.0 copy-start.7
  25.3 7.1 %whole.1 = bf16[32,8,8,128]{3,2,1,0:T(8,128)(2,1)} custom-call(bf16[256,256]{1,0:T(8,128)(2,1)} %bitcast.10, bf16[16,128,1024]{2,1,0:T(8,128)(2,1)} %image_ref.2, bf16[1024,1024]{1,0:T(8,128)(2,1)} %bitcast.7), custom_call_target="tpu_custom_call" | custom-call | flops 2684354560 | bytes 4194304 | tf_op jit(solution)/shard_map/whole/pallas_call | solution.py:258
  32.3 0.0 copy-start
  32.3 8.1 %all-to-all-done.1.refs_5_ = bf16[32,8,8,128]{3,2,1,0:T(8,128)(2,1)S(1)} async-done(((bf16[32,8,8,128]{3,2,1,0:T(8,128)(2,1)}), bf16[32,8,8,128]{3,2,1,0:T(8,128)(2,1)S(1)}, u32[]{:S(2)}, u32[]{:S(2)}) %all-to-all-start.1) | async-done | bytes 524320 | tf_op jit(solution)/shard_map/all_to_all | solution.py:214
  40.5 3.2 %all-to-all-start.2 = ((bf16[32,8,8,128]{3,2,1,0:T(8,128)(2,1)}), bf16[32,8,8,128]{3,2,1,0:T(8,128)(2,1)S(1)}, u32[]{:S(2)}, u32[]{:S(2)}) async-start(bf16[32,8,8,128]{3,2,1,0:T(8,128)(2,1)} %whole.1), calls=%async_computation.2 | async-start | bytes 1048576 | tf_op jit(solution)/shard_map/all_to_all | solution.py:214
  43.6 0.0 copy-done.8
  43.6 0.0 copy-done.9
  43.7 1.0 codes.1
  44.6 0.0 copy-start.1
  44.7 1.0 copy-done.1
  45.6 0.0 copy-start.3
  45.6 1.0 copy-done.3
  46.6 12.3 %all-to-all-done.2.refs_6_ = bf16[32,8,8,128]{3,2,1,0:T(8,128)(2,1)S(1)} async-done(((bf16[32,8,8,128]{3,2,1,0:T(8,128)(2,1)}), bf16[32,8,8,128]{3,2,1,0:T(8,128)(2,1)S(1)}, u32[]{:S(2)}, u32[]{:S(2)}) %all-to-all-start.2) | async-done | bytes 524320 | tf_op jit(solution)/shard_map/all_to_all | solution.py:214
  58.9 0.0 copy-done.7
  58.9 0.0 copy-start.2
  58.9 1.2 %copy-done.2 = bf16[8,256,256]{2,1,0:T(8,128)(2,1)S(1)} copy-done((bf16[8,256,256]{2,1,0:T(8,128)(2,1)S(1)}, bf16[8,256,256]{2,1,0:T(8,128)(2,1)}, u32[]{:S(2)}) %copy-start.2) | copy-done | bytes 1048600
  60.1 0.0 copy-start.4
  60.1 1.2 %copy-done.4 = bf16[8,256,256]{2,1,0:T(8,128)(2,1)S(1)} copy-done((bf16[8,256,256]{2,1,0:T(8,128)(2,1)S(1)}, bf16[8,256,256]{2,1,0:T(8,128)(2,1)}, u32[]{:S(2)}) %copy-start.4) | copy-done | bytes 1048600
  61.4 0.0 copy-start.6
  61.4 1.8 %resid.1 = (f32[32,16,128]{2,1,0:T(8,128)}, bf16[32,16,8,128]{3,2,1,0:T(8,128)(2,1)S(1)}) custom-call(bf16[256,128]{1,0:T(8,128)(2,1)S(1)} %copy-done.8, bf16[128,256]{1,0:T(8,128)(2,1)S(1)} %get-tuple-element.11.refs_1_, bf16[8,256,256]{2,1,0:T(8,128)(2,1)S(1)} %copy-done.2, bf16[8,256,256]{2,1,0:T(8,128)(2,1)S(1)} %copy-done.4, ...), custom_call_target="tpu_custom_call" | custom-call | flops 268435456 | bytes 2097152 | tf_op jit(solution)/shard_map/resid/pallas_call | solution.py:287
  63.2 29.3 %all_to_all.26.blk_ref = bf16[32,16,8,128]{3,2,1,0:T(8,128)(2,1)S(1)} all-to-all(bf16[32,16,8,128]{3,2,1,0:T(8,128)(2,1)S(1)} %get-tuple-element.17), channel_id=1, replica_groups=mesh['gx'=8,'gy'=4] {'gx','gy'}, dimensions={0} | all-to-all | bytes 2097152 | tf_op jit(solution)/shard_map/all_to_all | solution.py:214
  92.4 0.0 copy-done
  92.4 0.0 copy-done.6
  92.4 9.2 %image.1 = f32[16,128,1024]{2,1,0:T(8,128)} custom-call(bf16[256,256]{1,0:T(8,128)(2,1)S(1)} %bitcast.11, bf16[32,16,8,128]{3,2,1,0:T(8,128)(2,1)S(1)} %all_to_all.26.blk_ref, bf16[1024,1024]{1,0:T(8,128)(2,1)S(1)} %bitcast.8), custom_call_target="tpu_custom_call" | custom-call | flops 5368709120 | bytes 8388608 | tf_op jit(solution)/shard_map/image/pallas_call | solution.py:301
Async XLA Ops:
  2.8 14.5 %all-to-all-start = ((bf16[32,8,256]{2,1,0:T(8,128)(2,1)}), bf16[32,8,256]{2,1,0:T(8,128)(2,1)S(1)}, u32[]{:S(2)}, u32[]{:S(2)}) async-start(bf16[32,8,256]{2,1,0:T(8,128)(2,1)} %bitcast.13), calls=%async_computation | async-start | bytes 262144 | tf_op jit(solution)/shard_map/all_to_all | solution.py:229
  17.3 8.0 %copy-start.5 = (bf16[32,8,256]{2,1,0:T(8,128)(2,1)}, bf16[32,8,256]{2,1,0:T(8,128)(2,1)S(1)}, u32[]{:S(2)}) copy-start(bf16[32,8,256]{2,1,0:T(8,128)(2,1)S(1)} %all-to-all-done) | copy-start | bytes 393220
  21.2 19.2 %all-to-all-start.1 = ((bf16[32,8,8,128]{3,2,1,0:T(8,128)(2,1)}), bf16[32,8,8,128]{3,2,1,0:T(8,128)(2,1)S(1)}, u32[]{:S(2)}, u32[]{:S(2)}) async-start(bf16[32,8,8,128]{3,2,1,0:T(8,128)(2,1)} %demig.1), calls=%async_computation.1 | async-start | bytes 1048576 | tf_op jit(solution)/shard_map/all_to_all | solution.py:214
  25.2 18.4 %copy-start.8 = (bf16[256,128]{1,0:T(8,128)(2,1)S(1)}, bf16[256,128]{1,0:T(8,128)(2,1)}, u32[]{:S(2)}) copy-start(bf16[256,128]{1,0:T(8,128)(2,1)} %get-tuple-element.10.place_ref.refs_0_) | copy-start | bytes 196612
  25.2 18.4 %copy-start.9 = (s32[32,4,16]{0,2,1:T(8,128)S(1)}, s32[32,4,16]{0,2,1:T(8,128)}, u32[]{:S(2)}) copy-start(s32[32,4,16]{0,2,1:T(8,128)} %param.11) | copy-start | bytes 24580
  25.2 33.7 %copy-start.7 = (bf16[32,16,128]{2,1,0:T(8,128)(2,1)S(1)}, bf16[32,16,128]{2,1,0:T(8,128)(2,1)}, u32[]{:S(2)}) copy-start(bf16[32,16,128]{2,1,0:T(8,128)(2,1)} %refs_4_.1) | copy-start | bytes 393220
  32.3 60.1 %copy-start = (bf16[8,128,1024]{2,1,0:T(8,128)(2,1)S(1)}, bf16[8,128,1024]{2,1,0:T(8,128)(2,1)}, u32[]{:S(2)}) copy-start(bf16[8,128,1024]{2,1,0:T(8,128)(2,1)} %param.8) | copy-start | bytes 6291460
  40.5 18.4 %all-to-all-start.2 = ((bf16[32,8,8,128]{3,2,1,0:T(8,128)(2,1)}), bf16[32,8,8,128]{3,2,1,0:T(8,128)(2,1)S(1)}, u32[]{:S(2)}, u32[]{:S(2)}) async-start(bf16[32,8,8,128]{3,2,1,0:T(8,128)(2,1)} %whole.1), calls=%async_computation.2 | async-start | bytes 1048576 | tf_op jit(solution)/shard_map/all_to_all | solution.py:214
  44.6 1.0 copy-start.1
  45.6 1.0 copy-start.3
  58.9 1.2 %copy-start.2 = (bf16[8,256,256]{2,1,0:T(8,128)(2,1)S(1)}, bf16[8,256,256]{2,1,0:T(8,128)(2,1)}, u32[]{:S(2)}) copy-start(bf16[8,256,256]{2,1,0:T(8,128)(2,1)} %copy-done.1) | copy-start | bytes 3145732
  60.1 1.2 %copy-start.4 = (bf16[8,256,256]{2,1,0:T(8,128)(2,1)S(1)}, bf16[8,256,256]{2,1,0:T(8,128)(2,1)}, u32[]{:S(2)}) copy-start(bf16[8,256,256]{2,1,0:T(8,128)(2,1)} %copy-done.3) | copy-start | bytes 3145732
  61.4 31.1 %copy-start.6 = (bf16[32,8,256]{2,1,0:T(8,128)(2,1)S(1)}, bf16[32,8,256]{2,1,0:T(8,128)(2,1)}, u32[]{:S(2)}) copy-start(bf16[32,8,256]{2,1,0:T(8,128)(2,1)} %copy-done.5) | copy-start | bytes 393220

commit v5 on v4

--- a/solution.py
+++ b/solution.py
@@ -104,46 +104,34 @@
     out_ref[...] = rows.astype(BF).reshape(out_ref.shape)
 
 
-def demig(bands, first, msg_ref, rows, out_ref):
-    levels, width, long = rows.shape
+def demig_kernel(bands, msg_ref, rows_ref, out_ref):
+    levels, width, long = rows_ref.shape
     block_len = long // bands
     amp = msg_ref[:, :width]
     marks = msg_ref[:, width:]
     for i in range(0, levels, 2):
-        z = first + i
+        z = pl.program_id(0) * levels + i
         both = spread(marks, z, z + 1)
         for j in range(2):
             level = jnp.concatenate(
-                [rows[i + j, :, b * block_len : (b + 1) * block_len] for b in range(bands)], axis=0
+                [rows_ref[i + j, :, b * block_len : (b + 1) * block_len] for b in range(bands)],
+                axis=0,
             )
             weights = by_band(both[:, j * width : (j + 1) * width], amp, bands)
             put(out_ref, i + j, dot(weights, level).astype(BF))
 
 
-def demig_kernel(bands, base, msg_ref, rows_ref, out_ref):
-    levels = rows_ref.shape[0]
-    demig(bands, base + pl.program_id(0) * levels, msg_ref, rows_ref[...], out_ref)
-
-
-def whole_kernel(bands, base, msg_ref, image_ref, tab_ref, out_ref):
-    levels, width, cells = image_ref.shape
-    rows = dot(image_ref[...].reshape(levels * width, cells), tab_ref[...], ((1,), (1,)))
-    rows = rows.astype(BF).reshape(levels, width, tab_ref.shape[0])
-    demig(bands, base + pl.program_id(0) * levels, msg_ref, rows, out_ref)
-
-
-def residual_kernel(depth, parts, *refs):
-    place_ref, take_ref, pick_ref, drop_ref, obs_ref = refs[:5]
-    recv = refs[5 : 5 + parts]
-    res_ref, send_ref, pair_ref = refs[5 + parts :]
+def residual_kernel(
+    place_ref, take_ref, pick_ref, drop_ref, obs_ref, recv_ref, res_ref, send_ref, pair_ref
+):
+    depth = pair_ref.shape[0]
     traces, blocks, block_len = obs_ref.shape
     group = 256 // blocks
     halves = traces // group
     tiles = pick_ref.shape[0] // halves
     take = take_ref[...]
-    per = depth // parts
     for z in range(depth):
-        pair_ref[z] = dot(take, get(recv[z // per], z % per)).astype(BF)
+        pair_ref[z] = dot(take, get(recv_ref, z)).astype(BF)
     for h in range(halves):
         total = -obs_ref[h * group : (h + 1) * group].astype(F32).reshape(group * blocks, block_len)
         for k in range(tiles):
@@ -228,49 +216,31 @@
     )(aperture.T, band_index.transpose(1, 2, 0), amplitude)
     got = lax.all_to_all(message, ("gx", "gy"), split_axis=0, concat_axis=0, tiled=True)
 
-    half = depth // 2
     rows = pl.pallas_call(
         rows_kernel,
-        grid=(half // levels,),
-        out_shape=jax.ShapeDtypeStruct((half, width_x, long), BF),
+        grid=(depth // levels,),
+        out_shape=jax.ShapeDtypeStruct((depth, width_x, long), BF),
         in_specs=[
             pl.BlockSpec((levels, width_x, width_y), lambda z: (z, 0, 0)),
             pl.BlockSpec((long, width_y), lambda z: (0, 0)),
         ],
         out_specs=pl.BlockSpec((levels, width_x, long), lambda z: (z, 0, 0)),
-        cost_estimate=cost(2 * half * width_x * width_y * long, 4 * half * width_x * width_y),
+        cost_estimate=cost(2 * depth * width_x * width_y * long, 4 * depth * width_x * width_y),
         name="rows",
     )(model_image, tables_flat)
     rows = pltpu.with_memory_space_constraint(rows, pltpu.HBM)
     message_spec = pl.BlockSpec((slots, 2 * width_x), lambda z: (0, 0))
-    first = pl.pallas_call(
-        functools.partial(demig_kernel, bands, 0),
-        grid=(half // levels,),
-        out_shape=jax.ShapeDtypeStruct(shape_of(half), BF),
+    partials = pl.pallas_call(
+        functools.partial(demig_kernel, bands),
+        grid=(depth // levels,),
+        out_shape=jax.ShapeDtypeStruct(shape_of(depth), BF),
         in_specs=[message_spec, pl.BlockSpec((levels, width_x, long), lambda z: (z, 0, 0))],
         out_specs=block_of(levels),
         compiler_params=GRANT,
-        cost_estimate=cost(2 * half * slots * width_x * long, 2 * half * width_x * long),
+        cost_estimate=cost(2 * depth * slots * width_x * long, 2 * depth * width_x * long),
         name="demig",
     )(got, rows)
-    back = exchange(first)
-    _, image_late = lax.optimization_barrier((first, model_image))
-    second = pl.pallas_call(
-        functools.partial(whole_kernel, bands, half),
-        grid=((depth - half) // levels,),
-        out_shape=jax.ShapeDtypeStruct(shape_of(depth - half), BF),
-        in_specs=[
-            message_spec,
-            pl.BlockSpec((levels, width_x, width_y), lambda z: (z + half // levels, 0, 0)),
-            pl.BlockSpec((long, width_y), lambda z: (0, 0)),
-        ],
-        out_specs=block_of(levels),
-        cost_estimate=cost(
-            2 * (depth - half) * width_x * long * (width_y + slots), 4 * half * width_x * width_y
-        ),
-        name="whole",
-    )(got, image_late, tables_flat)
-    back_late = exchange(second)
+    returned = exchange(partials)
     take, pick, drop = pl.pallas_call(
         functools.partial(codes_kernel, blocks),
         out_shape=(
@@ -285,18 +255,18 @@
         name="codes",
     )(place, traveltime.transpose(1, 2, 0))
     residual, outgoing = pl.pallas_call(
-        functools.partial(residual_kernel, depth, 2),
+        residual_kernel,
         out_shape=(
             jax.ShapeDtypeStruct((traces, blocks, block_len), F32),
             jax.ShapeDtypeStruct(shape_of(depth), BF),
         ),
-        in_specs=[VMEM] * 7,
+        in_specs=[VMEM] * 6,
         out_specs=(VMEM, VMEM),
         scratch_shapes=[pltpu.VMEM((depth, pairs, block_len), BF)],
         compiler_params=GRANT,
         cost_estimate=cost(4 * depth * slots * pairs * block_len, 4 * depth * slots * block_len),
         name="resid",
-    )(place, take, pick, drop, observed, back, back_late)
+    )(place, take, pick, drop, observed, returned)
     incoming = exchange(outgoing)
     gradient = pl.pallas_call(
         functools.partial(image_kernel, bands),

time: 102 us -> 97.8 us (0.959)
  local copies, waits for them, and re-layouts: 4.42 us -> 0.76 us
  waiting for transfers between devices: 22.3 us -> 24.6 us
  Pallas kernels: 30.7 us -> 29 us
  starting transfers between devices: 14.2 us -> 12.9 us
    all_to_all x2 -> x1, waiting for transfers between devices: 20.5 us -> 24.6 us  [exchange(): x = lax.all_to_all(x, ('gx', 'gy'), split_axis=0, concat_axis=0, tiled=True)]
    unnamed x20 -> x8, local copies, waits for them, and re-layouts: 4.42 us -> 0.76 us
    all_to_all x1, waiting for transfers between devices: 1.88 us -> 0.01 us  [shards(): lax.all_to_all(message, ('gx', 'gy'), split_axis=0, concat_axis=0, tiled=...]
    pallas_call x4 -> x3, Pallas kernels: 18.3 us -> 16.7 us  [the longest x1 8.47 us: shards(): pl.pallas_call(rows_kernel, grid=(depth // levels,), out_shape=jax.ShapeD...]
    all_to_all x2 -> x1, starting transfers between devices: 7.12 us -> 5.83 us  [exchange(): x = lax.all_to_all(x, ('gx', 'gy'), split_axis=0, concat_axis=0, tiled=True)]
  transfers between devices with their start and end apart: 3 -> 2, of which waited for: 3 -> 1; matrix products, arithmetic and copies ran while one was open for 0% -> 0% of each run, Pallas kernels for 13% -> 10%
where the time goes in v5:
time: 97.8 us; the launch traced here: 97.2 us
  blocking collectives  29.3 us (30%)
  Pallas kernels  29 us (30%)
  waiting for transfers between devices  24.6 us (25%)
  starting transfers between devices  12.9 us (13%)
    all_to_all x1, blocking collectives, exchange(): x = lax.all_to_all(x, ('gx', 'gy'), split_axis=0, concat_axis=0, tiled=True)  29.3 us
    all_to_all x1, waiting for transfers between devices, exchange(): x = lax.all_to_all(x, ('gx', 'gy'), split_axis=0, concat_axis=0, tiled=True)  24.6 us
    pallas_call x1, Pallas kernels, shards(): pl.pallas_call(functools.partial(image_kernel, bands), grid=(depth // lev...  9.18 us
    pallas_call x1, Pallas kernels, shards(): pl.pallas_call(rows_kernel, grid=(depth // levels,), out_shape=jax.ShapeD...  8.47 us
    all_to_all x1, starting transfers between devices, shards(): lax.all_to_all(message, ('gx', 'gy'), split_axis=0, concat_axis=0, tiled=...  7.08 us
    pallas_call x1, Pallas kernels, shards(): pl.pallas_call(functools.partial(demig_kernel, bands), grid=(depth // lev...  6.44 us
    all_to_all x1, starting transfers between devices, exchange(): x = lax.all_to_all(x, ('gx', 'gy'), split_axis=0, concat_axis=0, tiled=True)  5.83 us
    pallas_call x1, Pallas kernels, shards(): pl.pallas_call(functools.partial(prep_kernel, devices, capacity), out_sha...  2.16 us
  transfers between devices with their start and end apart: 2, of which 1 were waited for; matrix products, arithmetic and copies ran while one was open for 0% of the time, Pallas kernels for 10%

profile of v5, /device:TPU:1, one launch (start us, length us, event | category | flops | bytes accessed | tf_op | source)
XLA Modules:
  0.0 97.2 jit_solution(5524548612220261343)
XLA Ops:
  0.6 2.2 %prep.1 = (bf16[256,256]{1,0:T(8,128)(2,1)}, bf16[256,128]{1,0:T(8,128)(2,1)}) custom-call(s32[4,32]{1,0:T(4,128)} %bitcast.13, s32[4,16,32]{2,1,0:T(8,128)} %bitcast.12, bf16[32,4,128]{2,1,0:T(4,128)(2,1)} %am_ref.1), custom_call_target="tpu_custom_call" | custom-call | tf_op jit(solution)/shard_map/prep/pallas_call | solution.py:207
  2.8 7.1 %all-to-all-start = ((bf16[32,8,256]{2,1,0:T(8,128)(2,1)}), bf16[32,8,256]{2,1,0:T(8,128)(2,1)S(1)}, u32[]{:S(2)}, u32[]{:S(2)}) async-start(bf16[32,8,256]{2,1,0:T(8,128)(2,1)} %bitcast.11), calls=%async_computation | async-start | bytes 262144 | tf_op jit(solution)/shard_map/all_to_all | solution.py:217
  9.9 8.5 %rows.1.rows_ref = bf16[16,128,1024]{2,1,0:T(8,128)(2,1)} custom-call(bf16[16,128,1024]{2,1,0:T(8,128)(2,1)} %image_ref.1, bf16[1024,1024]{1,0:T(8,128)(2,1)} %bitcast.8), custom_call_target="tpu_custom_call" | custom-call | flops 4294967296 | bytes 8388608 | tf_op jit(solution)/shard_map/rows/pallas_call | solution.py:219
  18.3 0.0 copy-start.1
  18.3 0.0 copy-start
  18.4 0.0 all-to-all-done
  18.4 6.4 %demig.1 = bf16[32,16,8,128]{3,2,1,0:T(8,128)(2,1)} custom-call(bf16[256,256]{1,0:T(8,128)(2,1)S(1)} %bitcast.6, bf16[16,128,1024]{2,1,0:T(8,128)(2,1)} %rows.1.rows_ref), custom_call_target="tpu_custom_call" | custom-call | flops 1073741824 | bytes 4194304 | tf_op jit(solution)/shard_map/demig/pallas_call | solution.py:233
  24.8 5.8 %all-to-all-start.1 = ((bf16[32,16,8,128]{3,2,1,0:T(8,128)(2,1)}), bf16[32,16,8,128]{3,2,1,0:T(8,128)(2,1)S(1)}, u32[]{:S(2)}, u32[]{:S(2)}) async-start(bf16[32,16,8,128]{3,2,1,0:T(8,128)(2,1)} %demig.1), calls=%async_computation.1 | async-start | bytes 2097152 | tf_op jit(solution)/shard_map/all_to_all | solution.py:202
  30.6 0.0 copy-done.1
  30.6 0.0 copy-start.3
  30.7 0.7 copy-done.3
  31.4 1.0 %codes.1 = (bf16[128,256]{1,0:T(8,128)(2,1)S(1)}, bf16[8,256,256]{2,1,0:T(8,128)(2,1)S(1)}, bf16[8,256,256]{2,1,0:T(8,128)(2,1)S(1)}) custom-call(bf16[256,128]{1,0:T(8,128)(2,1)S(1)} %copy-done.1, s32[4,16,32]{2,1,0:T(8,128)S(1)} %bitcast.10), custom_call_target="tpu_custom_call" | custom-call | flops 134217728 | bytes 2097152 | tf_op jit(solution)/shard_map/codes/pallas_call | solution.py:244
  32.4 24.6 %all-to-all-done.1.recv_ref = bf16[32,16,8,128]{3,2,1,0:T(8,128)(2,1)S(1)} async-done(((bf16[32,16,8,128]{3,2,1,0:T(8,128)(2,1)}), bf16[32,16,8,128]{3,2,1,0:T(8,128)(2,1)S(1)}, u32[]{:S(2)}, u32[]{:S(2)}) %all-to-all-start.1) | async-done | bytes 1048608 | tf_op jit(solution)/shard_map/all_to_all | solution.py:202
  57.0 0.0 copy-start.2
  57.0 0.0 copy-done
  57.0 1.8 %resid.1 = (f32[32,16,128]{2,1,0:T(8,128)}, bf16[32,16,8,128]{3,2,1,0:T(8,128)(2,1)S(1)}) custom-call(bf16[256,128]{1,0:T(8,128)(2,1)S(1)} %copy-done.1, bf16[128,256]{1,0:T(8,128)(2,1)S(1)} %get-tuple-element.10.take_ref, bf16[8,256,256]{2,1,0:T(8,128)(2,1)S(1)} %get-tuple-element.11.pick_ref, bf16[8,256,256]{2,1,0:T(8,128)(2,1)S(1)} %get-tuple-element.12.drop_ref, ...), custom_call_target="tpu_custom_call" | custom-call | flops 268435456 | bytes 2097152 | tf_op jit(solution)/shard_map/resid/pallas_call | solution.py:257
  58.8 29.3 %all_to_all.21.blk_ref = bf16[32,16,8,128]{3,2,1,0:T(8,128)(2,1)S(1)} all-to-all(bf16[32,16,8,128]{3,2,1,0:T(8,128)(2,1)S(1)} %get-tuple-element.15), channel_id=1, replica_groups=mesh['gx'=8,'gy'=4] {'gx','gy'}, dimensions={0} | all-to-all | bytes 2097152 | tf_op jit(solution)/shard_map/all_to_all | solution.py:202
  88.0 0.0 copy-done.2
  88.0 9.2 %image.1 = f32[16,128,1024]{2,1,0:T(8,128)} custom-call(bf16[256,256]{1,0:T(8,128)(2,1)S(1)} %bitcast.7, bf16[32,16,8,128]{3,2,1,0:T(8,128)(2,1)S(1)} %all_to_all.21.blk_ref, bf16[1024,1024]{1,0:T(8,128)(2,1)S(1)} %bitcast.9), custom_call_target="tpu_custom_call" | custom-call | flops 5368709120 | bytes 8388608 | tf_op jit(solution)/shard_map/image/pallas_call | solution.py:271
Async XLA Ops:
  2.8 15.6 %all-to-all-start = ((bf16[32,8,256]{2,1,0:T(8,128)(2,1)}), bf16[32,8,256]{2,1,0:T(8,128)(2,1)S(1)}, u32[]{:S(2)}, u32[]{:S(2)}) async-start(bf16[32,8,256]{2,1,0:T(8,128)(2,1)} %bitcast.11), calls=%async_computation | async-start | bytes 262144 | tf_op jit(solution)/shard_map/all_to_all | solution.py:217
  18.3 12.3 %copy-start.1 = (bf16[256,128]{1,0:T(8,128)(2,1)S(1)}, bf16[256,128]{1,0:T(8,128)(2,1)}, u32[]{:S(2)}) copy-start(bf16[256,128]{1,0:T(8,128)(2,1)} %get-tuple-element.9.place_ref) | copy-start | bytes 196612
  18.3 38.6 %copy-start = (bf16[32,16,128]{2,1,0:T(8,128)(2,1)S(1)}, bf16[32,16,128]{2,1,0:T(8,128)(2,1)}, u32[]{:S(2)}) copy-start(bf16[32,16,128]{2,1,0:T(8,128)(2,1)} %obs_ref.1) | copy-start | bytes 393220
  24.8 32.2 %all-to-all-start.1 = ((bf16[32,16,8,128]{3,2,1,0:T(8,128)(2,1)}), bf16[32,16,8,128]{3,2,1,0:T(8,128)(2,1)S(1)}, u32[]{:S(2)}, u32[]{:S(2)}) async-start(bf16[32,16,8,128]{3,2,1,0:T(8,128)(2,1)} %demig.1), calls=%async_computation.1 | async-start | bytes 2097152 | tf_op jit(solution)/shard_map/all_to_all | solution.py:202
  30.6 0.8 copy-start.3
  57.0 31.1 %copy-start.2 = (bf16[8,128,1024]{2,1,0:T(8,128)(2,1)S(1)}, bf16[8,128,1024]{2,1,0:T(8,128)(2,1)}, u32[]{:S(2)}) copy-start(bf16[8,128,1024]{2,1,0:T(8,128)(2,1)} %param.8) | copy-start | bytes 6291460

commit v6 on v5

--- a/solution.py
+++ b/solution.py
@@ -48,9 +48,17 @@
     msg_ref[:, width:] = marks.astype(BF)
 
 
-def codes_kernel(blocks, place_ref, tt_ref, take_ref, pick_ref, drop_ref):
+def codes_kernel(
+    blocks, msg_ref, place_ref, tt_ref, take_ref, pick_ref, drop_ref, amp_ref, band_ref
+):
     tiles, depth, traces = tt_ref.shape
     group = 256 // blocks
+    width = amp_ref.shape[0]
+    amp_ref[...] = msg_ref[:, :width].astype(F32).T.astype(BF)
+    for z in range(0, depth, 2):
+        both = spread(msg_ref[:, width:], z, z + 1)
+        band_ref[z] = both[:, :width]
+        band_ref[z + 1] = both[:, width:]
     take_ref[...] = place_ref[...].astype(F32).T.astype(BF)
     size = depth * group
     lanes = 128
@@ -108,17 +116,14 @@
     levels, width, long = rows_ref.shape
     block_len = long // bands
     amp = msg_ref[:, :width]
-    marks = msg_ref[:, width:]
-    for i in range(0, levels, 2):
-        z = pl.program_id(0) * levels + i
-        both = spread(marks, z, z + 1)
-        for j in range(2):
-            level = jnp.concatenate(
-                [rows_ref[i + j, :, b * block_len : (b + 1) * block_len] for b in range(bands)],
-                axis=0,
-            )
-            weights = by_band(both[:, j * width : (j + 1) * width], amp, bands)
-            put(out_ref, i + j, dot(weights, level).astype(BF))
+    shift = (width - pl.program_id(0) * levels) % width
+    marks = pltpu.roll(msg_ref[:, width:].astype(F32), shift, 1)
+    for i in range(levels):
+        band = jnp.broadcast_to(marks[:, i : i + 1], amp.shape).astype(BF)
+        rows = jnp.concatenate(
+            [rows_ref[i, :, b * block_len : (b + 1) * block_len] for b in range(bands)], axis=0
+        )
+        put(out_ref, i, dot(by_band(band, amp, bands), rows).astype(BF))
 
 
 def residual_kernel(
@@ -130,8 +135,10 @@
     halves = traces // group
     tiles = pick_ref.shape[0] // halves
     take = take_ref[...]
-    for z in range(depth):
-        pair_ref[z] = dot(take, get(recv_ref, z)).astype(BF)
+    for z in range(0, depth, 2):
+        two = dot(take, jnp.concatenate([get(recv_ref, z), get(recv_ref, z + 1)], axis=1)).astype(BF)
+        pair_ref[z] = two[:, :block_len]
+        pair_ref[z + 1] = two[:, block_len:]
     for h in range(halves):
         total = -obs_ref[h * group : (h + 1) * group].astype(F32).reshape(group * blocks, block_len)
         for k in range(tiles):
@@ -145,26 +152,17 @@
             got = dot(pick_ref[k * halves + h], low).astype(BF)
             pair_ref[:, at, :] = got.reshape(depth, group, block_len)
     place = place_ref[...]
-    for z in range(depth):
-        put(send_ref, z, dot(place, pair_ref[z]).astype(BF))
-
-
-def image_kernel(bands, msg_ref, blk_ref, tab_ref, out_ref, amp_ref, stack_ref):
-    step = pl.program_id(0)
+    for z in range(0, depth, 2):
+        two = dot(place, jnp.concatenate([pair_ref[z], pair_ref[z + 1]], axis=1)).astype(BF)
+        put(send_ref, z, two[:, :block_len])
+        put(send_ref, z + 1, two[:, block_len:])
+
+
+def image_kernel(bands, amp_ref, band_ref, blk_ref, tab_ref, out_ref, stack_ref):
     levels, width, cells = out_ref.shape
-    marks = msg_ref[:, width:]
-
-    @pl.when(step == 0)
-    def _():
-        amp_ref[...] = msg_ref[:, :width].astype(F32).T.astype(BF)
-
-    for i in range(0, levels, 2):
-        z = step * levels + i
-        both = spread(marks, z, z + 1)
-        for j in range(2):
-            masked = by_band(both[:, j * width : (j + 1) * width], get(blk_ref, i + j), bands)
-            stack = dot(amp_ref[...], masked)
-            stack_ref[(i + j) * width : (i + j + 1) * width, :] = stack.astype(BF)
+    for i in range(levels):
+        masked = by_band(band_ref[i], get(blk_ref, i), bands)
+        stack_ref[i * width : (i + 1) * width, :] = dot(amp_ref[...], masked).astype(BF)
     out_ref[...] = dot(stack_ref[...], tab_ref[...]).reshape(levels, width, cells)
 
 
@@ -229,31 +227,35 @@
         name="rows",
     )(model_image, tables_flat)
     rows = pltpu.with_memory_space_constraint(rows, pltpu.HBM)
-    message_spec = pl.BlockSpec((slots, 2 * width_x), lambda z: (0, 0))
     partials = pl.pallas_call(
         functools.partial(demig_kernel, bands),
-        grid=(depth // levels,),
+        grid=(depth // (2 * levels),),
         out_shape=jax.ShapeDtypeStruct(shape_of(depth), BF),
-        in_specs=[message_spec, pl.BlockSpec((levels, width_x, long), lambda z: (z, 0, 0))],
-        out_specs=block_of(levels),
+        in_specs=[
+            pl.BlockSpec((slots, 2 * width_x), lambda z: (0, 0)),
+            pl.BlockSpec((2 * levels, width_x, long), lambda z: (z, 0, 0)),
+        ],
+        out_specs=block_of(2 * levels),
         compiler_params=GRANT,
         cost_estimate=cost(2 * depth * slots * width_x * long, 2 * depth * width_x * long),
         name="demig",
     )(got, rows)
     returned = exchange(partials)
-    take, pick, drop = pl.pallas_call(
+    take, pick, drop, turned, spread_bands = pl.pallas_call(
         functools.partial(codes_kernel, blocks),
         out_shape=(
             jax.ShapeDtypeStruct((pairs, slots), BF),
             jax.ShapeDtypeStruct((groups, 256, 256), BF),
             jax.ShapeDtypeStruct((groups, 256, 256), BF),
+            jax.ShapeDtypeStruct((width_x, slots), BF),
+            jax.ShapeDtypeStruct((depth, slots, width_x), BF),
         ),
-        in_specs=[VMEM, VMEM],
-        out_specs=(VMEM,) * 3,
+        in_specs=[VMEM] * 3,
+        out_specs=(VMEM,) * 5,
         compiler_params=GRANT,
         cost_estimate=cost(groups * 256 * 256 * 256, groups * 256 * 256 * 4),
         name="codes",
-    )(place, traveltime.transpose(1, 2, 0))
+    )(got, place, traveltime.transpose(1, 2, 0))
     residual, outgoing = pl.pallas_call(
         residual_kernel,
         out_shape=(
@@ -273,21 +275,19 @@
         grid=(depth // levels,),
         out_shape=jax.ShapeDtypeStruct((depth, width_x, width_y), F32),
         in_specs=[
-            message_spec,
+            pl.BlockSpec((width_x, slots), lambda z: (0, 0)),
+            pl.BlockSpec((levels, slots, width_x), lambda z: (z, 0, 0)),
             block_of(levels),
             pl.BlockSpec((long, width_y), lambda z: (0, 0)),
         ],
         out_specs=pl.BlockSpec((levels, width_x, width_y), lambda z: (z, 0, 0)),
-        scratch_shapes=[
-            pltpu.VMEM((width_x, slots), BF),
-            pltpu.VMEM((levels * width_x, long), BF),
-        ],
+        scratch_shapes=[pltpu.VMEM((levels * width_x, long), BF)],
         compiler_params=GRANT,
         cost_estimate=cost(
             2 * depth * width_x * long * (width_y + slots), 4 * depth * width_x * width_y
         ),
         name="image",
-    )(got, incoming, tables_flat)
+    )(turned, spread_bands, incoming, tables_flat)
     return residual, gradient
 
 

time: 97.8 us -> 95.7 us (0.979)
  waiting for transfers between devices: 24.6 us -> 22.7 us
  Pallas kernels: 29 us -> 27.3 us
  local copies, waits for them, and re-layouts: 0.76 us -> 2.35 us
    all_to_all x1, waiting for transfers between devices: 24.6 us -> 22.7 us  [exchange(): x = lax.all_to_all(x, ('gx', 'gy'), split_axis=0, concat_axis=0, tiled=True)]
    unnamed x8 -> x16, local copies, waits for them, and re-layouts: 0.76 us -> 2.35 us
    pallas_call x1, Pallas kernels: 6.44 us -> 5.29 us  [shards(): pl.pallas_call(functools.partial(demig_kernel, bands), grid=(depth // (2...]
where the time goes in v6:
time: 95.7 us; the launch traced here: 95.2 us
  blocking collectives  29.3 us (31%)
  Pallas kernels  27.3 us (29%)
  waiting for transfers between devices  22.7 us (24%)
  starting transfers between devices  12.9 us (13%)
  local copies, waits for them, and re-layouts  2.35 us (2%)
    all_to_all x1, blocking collectives, exchange(): x = lax.all_to_all(x, ('gx', 'gy'), split_axis=0, concat_axis=0, tiled=True)  29.3 us
    all_to_all x1, waiting for transfers between devices, exchange(): x = lax.all_to_all(x, ('gx', 'gy'), split_axis=0, concat_axis=0, tiled=True)  22.7 us
    pallas_call x1, Pallas kernels, shards(): pl.pallas_call(rows_kernel, grid=(depth // levels,), out_shape=jax.ShapeD...  8.47 us
    pallas_call x1, Pallas kernels, shards(): pl.pallas_call(functools.partial(image_kernel, bands), grid=(depth // lev...  8.45 us
    all_to_all x1, starting transfers between devices, shards(): lax.all_to_all(message, ('gx', 'gy'), split_axis=0, concat_axis=0, tiled=...  7.08 us
    all_to_all x1, starting transfers between devices, exchange(): x = lax.all_to_all(x, ('gx', 'gy'), split_axis=0, concat_axis=0, tiled=True)  5.82 us
    pallas_call x1, Pallas kernels, shards(): pl.pallas_call(functools.partial(demig_kernel, bands), grid=(depth // (2...  5.29 us
    unnamed x16, local copies, waits for them, and re-layouts  2.35 us
  transfers between devices with their start and end apart: 2, of which 1 were waited for; matrix products, arithmetic and copies ran while one was open for 0% of the time, Pallas kernels for 10%

profile of v6, /device:TPU:1, one launch (start us, length us, event | category | flops | bytes accessed | tf_op | source)
XLA Modules:
  0.0 95.2 jit_solution(6526376543819531275)
XLA Ops:
  0.6 2.2 %prep.1 = (bf16[256,256]{1,0:T(8,128)(2,1)}, bf16[256,128]{1,0:T(8,128)(2,1)}) custom-call(s32[4,32]{1,0:T(4,128)} %bitcast.13, s32[4,16,32]{2,1,0:T(8,128)} %bitcast.12, bf16[32,4,128]{2,1,0:T(4,128)(2,1)} %am_ref.1), custom_call_target="tpu_custom_call" | custom-call | tf_op jit(solution)/shard_map/prep/pallas_call | solution.py:205
  2.8 7.1 %all-to-all-start = ((bf16[32,8,256]{2,1,0:T(8,128)(2,1)}), bf16[32,8,256]{2,1,0:T(8,128)(2,1)S(1)}, u32[]{:S(2)}, u32[]{:S(2)}) async-start(bf16[32,8,256]{2,1,0:T(8,128)(2,1)} %bitcast.11), calls=%async_computation | async-start | bytes 262144 | tf_op jit(solution)/shard_map/all_to_all | solution.py:215
  9.9 8.5 %rows.1.rows_ref = bf16[16,128,1024]{2,1,0:T(8,128)(2,1)} custom-call(bf16[16,128,1024]{2,1,0:T(8,128)(2,1)} %image_ref.1, bf16[1024,1024]{1,0:T(8,128)(2,1)} %bitcast.8), custom_call_target="tpu_custom_call" | custom-call | flops 4294967296 | bytes 8388608 | tf_op jit(solution)/shard_map/rows/pallas_call | solution.py:217
  18.3 0.0 copy-start.1
  18.3 0.0 copy-start
  18.4 0.0 all-to-all-done
  18.4 5.3 %demig.1 = bf16[32,16,8,128]{3,2,1,0:T(8,128)(2,1)} custom-call(bf16[256,256]{1,0:T(8,128)(2,1)S(1)} %bitcast.6, bf16[16,128,1024]{2,1,0:T(8,128)(2,1)} %rows.1.rows_ref), custom_call_target="tpu_custom_call" | custom-call | flops 1073741824 | bytes 4194304 | tf_op jit(solution)/shard_map/demig/pallas_call | solution.py:230
  23.6 5.8 %all-to-all-start.1 = ((bf16[32,16,8,128]{3,2,1,0:T(8,128)(2,1)}), bf16[32,16,8,128]{3,2,1,0:T(8,128)(2,1)S(1)}, u32[]{:S(2)}, u32[]{:S(2)}) async-start(bf16[32,16,8,128]{3,2,1,0:T(8,128)(2,1)} %demig.1), calls=%async_computation.1 | async-start | bytes 2097152 | tf_op jit(solution)/shard_map/all_to_all | solution.py:200
  29.5 0.0 copy-done.1
  29.5 0.0 copy-start.3
  29.5 0.7 copy-done.3
  30.2 1.3 %codes.1 = (bf16[128,256]{1,0:T(8,128)(2,1)S(1)}, bf16[8,256,256]{2,1,0:T(8,128)(2,1)S(1)}, bf16[8,256,256]{2,1,0:T(8,128)(2,1)S(1)}, bf16[128,256]{1,0:T(8,128)(2,1)S(1)}, bf16[16,256,128]{2,1,0:T(8,128)(2,1)S(1)}) custom-call(bf16[256,256]{1,0:T(8,128)(2,1)S(1)} %bitcast.7, bf16[256,128]{1,0:T(8,128)(2,1)S(1)} %copy-done.1, s32[4,16,32]{2,1,0:T(8,128)S(1)} %bitcast.10), custom_call_target="tpu_custom_call" | custom-call | flops 134217728 | bytes 2097152 | tf_op jit(solution)/shard_map/codes/pallas_call | solution.py:244
  31.5 0.0 copy-start.4
  31.5 1.0 %copy-done.4 = bf16[16,256,128]{2,1,0:T(8,128)(2,1)} copy-done((bf16[16,256,128]{2,1,0:T(8,128)(2,1)}, bf16[16,256,128]{2,1,0:T(8,128)(2,1)S(1)}, u32[]{:S(2)}) %copy-start.4) | copy-done | bytes 1048600
  32.5 0.0 copy-start.6
  32.5 0.6 copy-done.6
  33.1 22.7 %all-to-all-done.1.recv_ref = bf16[32,16,8,128]{3,2,1,0:T(8,128)(2,1)S(1)} async-done(((bf16[32,16,8,128]{3,2,1,0:T(8,128)(2,1)}), bf16[32,16,8,128]{3,2,1,0:T(8,128)(2,1)S(1)}, u32[]{:S(2)}, u32[]{:S(2)}) %all-to-all-start.1) | async-done | bytes 1048608 | tf_op jit(solution)/shard_map/all_to_all | solution.py:200
  55.8 0.0 copy-start.2
  55.8 0.0 copy-start.5
  55.8 0.0 copy-start.7
  55.8 0.0 copy-done
  55.8 1.7 %resid.1 = (f32[32,16,128]{2,1,0:T(8,128)}, bf16[32,16,8,128]{3,2,1,0:T(8,128)(2,1)S(1)}) custom-call(bf16[256,128]{1,0:T(8,128)(2,1)S(1)} %copy-done.1, bf16[128,256]{1,0:T(8,128)(2,1)S(1)} %get-tuple-element.13.take_ref, bf16[8,256,256]{2,1,0:T(8,128)(2,1)S(1)} %get-tuple-element.14.pick_ref, bf16[8,256,256]{2,1,0:T(8,128)(2,1)S(1)} %get-tuple-element.15.drop_ref, ...), custom_call_target="tpu_custom_call" | custom-call | flops 268435456 | bytes 2097152 | tf_op jit(solution)/shard_map/resid/pallas_call | solution.py:259
  57.5 29.3 %all_to_all.21.blk_ref = bf16[32,16,8,128]{3,2,1,0:T(8,128)(2,1)S(1)} all-to-all(bf16[32,16,8,128]{3,2,1,0:T(8,128)(2,1)S(1)} %get-tuple-element.19), channel_id=1, replica_groups=mesh['gx'=8,'gy'=4] {'gx','gy'}, dimensions={0} | all-to-all | bytes 2097152 | tf_op jit(solution)/shard_map/all_to_all | solution.py:200
  86.8 0.0 copy-done.2
  86.8 0.0 copy-done.5
  86.8 0.0 copy-done.7
  86.8 8.5 %image.1 = f32[16,128,1024]{2,1,0:T(8,128)} custom-call(bf16[128,256]{1,0:T(8,128)(2,1)S(1)} %copy-done.7, bf16[16,256,128]{2,1,0:T(8,128)(2,1)S(1)} %copy-done.5, bf16[32,16,8,128]{3,2,1,0:T(8,128)(2,1)S(1)} %all_to_all.21.blk_ref, bf16[1024,1024]{1,0:T(8,128)(2,1)S(1)} %bitcast.9), custom_call_target="tpu_custom_call" | custom-call | flops 5368709120 | bytes 8388608 | tf_op jit(solution)/shard_map/image/pallas_call | solution.py:273
Async XLA Ops:
  2.8 15.6 %all-to-all-start = ((bf16[32,8,256]{2,1,0:T(8,128)(2,1)}), bf16[32,8,256]{2,1,0:T(8,128)(2,1)S(1)}, u32[]{:S(2)}, u32[]{:S(2)}) async-start(bf16[32,8,256]{2,1,0:T(8,128)(2,1)} %bitcast.11), calls=%async_computation | async-start | bytes 262144 | tf_op jit(solution)/shard_map/all_to_all | solution.py:215
  18.3 11.1 %copy-start.1 = (bf16[256,128]{1,0:T(8,128)(2,1)S(1)}, bf16[256,128]{1,0:T(8,128)(2,1)}, u32[]{:S(2)}) copy-start(bf16[256,128]{1,0:T(8,128)(2,1)} %get-tuple-element.11.place_ref) | copy-start | bytes 196612
  18.3 37.5 %copy-start = (bf16[32,16,128]{2,1,0:T(8,128)(2,1)S(1)}, bf16[32,16,128]{2,1,0:T(8,128)(2,1)}, u32[]{:S(2)}) copy-start(bf16[32,16,128]{2,1,0:T(8,128)(2,1)} %obs_ref.1) | copy-start | bytes 393220
  23.6 32.2 %all-to-all-start.1 = ((bf16[32,16,8,128]{3,2,1,0:T(8,128)(2,1)}), bf16[32,16,8,128]{3,2,1,0:T(8,128)(2,1)S(1)}, u32[]{:S(2)}, u32[]{:S(2)}) async-start(bf16[32,16,8,128]{3,2,1,0:T(8,128)(2,1)} %demig.1), calls=%async_computation.1 | async-start | bytes 2097152 | tf_op jit(solution)/shard_map/all_to_all | solution.py:200
  29.5 0.8 copy-start.3
  31.5 1.0 %copy-start.4 = (bf16[16,256,128]{2,1,0:T(8,128)(2,1)}, bf16[16,256,128]{2,1,0:T(8,128)(2,1)S(1)}, u32[]{:S(2)}) copy-start(bf16[16,256,128]{2,1,0:T(8,128)(2,1)S(1)} %get-tuple-element.18.band_ref) | copy-start | bytes 3145732
  32.5 0.6 copy-start.6
  55.8 31.0 %copy-start.2 = (bf16[8,128,1024]{2,1,0:T(8,128)(2,1)S(1)}, bf16[8,128,1024]{2,1,0:T(8,128)(2,1)}, u32[]{:S(2)}) copy-start(bf16[8,128,1024]{2,1,0:T(8,128)(2,1)} %param.8) | copy-start | bytes 6291460
  55.8 31.0 %copy-start.5 = (bf16[16,256,128]{2,1,0:T(8,128)(2,1)S(1)}, bf16[16,256,128]{2,1,0:T(8,128)(2,1)}, u32[]{:S(2)}) copy-start(bf16[16,256,128]{2,1,0:T(8,128)(2,1)} %copy-done.4) | copy-start | bytes 3145732
  55.8 31.0 %copy-start.7 = (bf16[128,256]{1,0:T(8,128)(2,1)S(1)}, bf16[128,256]{1,0:T(8,128)(2,1)}, u32[]{:S(2)}) copy-start(bf16[128,256]{1,0:T(8,128)(2,1)} %copy-done.6) | copy-start | bytes 196612

commit v7 on v6

--- a/solution.py
+++ b/solution.py
@@ -10,6 +10,7 @@
 BF = jnp.bfloat16
 F32 = jnp.float32
 GRANT = pltpu.CompilerParams(vmem_limit_bytes=20 * 1024 * 1024)
+ANY = pl.BlockSpec(memory_space=pl.ANY)
 VMEM = pl.BlockSpec(memory_space=pltpu.VMEM)
 
 
@@ -106,24 +107,68 @@
     return ref[z]
 
 
-def rows_kernel(image_ref, tab_ref, out_ref):
-    levels, width, cells = image_ref.shape
-    rows = dot(image_ref[...].reshape(levels * width, cells), tab_ref[...], ((1,), (1,)))
-    out_ref[...] = rows.astype(BF).reshape(out_ref.shape)
-
-
-def demig_kernel(bands, msg_ref, rows_ref, out_ref):
-    levels, width, long = rows_ref.shape
+def rows_kernel(
+    per, cols, image_hbm, tab_hbm, out_hbm, image_ref, tab_ref, out_ref, image_sem, tab_sem, out_sem
+):
+    depth, width, cells = image_ref.shape
+    pieces, strips = depth // per, tab_ref.shape[0] // cols
+
+    def image_copy(m):
+        at = pl.ds(m * per, per)
+        return pltpu.make_async_copy(image_hbm.at[at], image_ref.at[at], image_sem.at[m])
+
+    def tab_copy(n):
+        at = pl.ds(n * cols, cols)
+        return pltpu.make_async_copy(tab_hbm.at[at], tab_ref.at[at], tab_sem.at[n])
+
+    tab_copy(0).start()
+    for m in range(pieces):
+        image_copy(m).start()
+    for n in range(1, strips):
+        tab_copy(n).start()
+    sent = []
+    for n in range(strips):
+        tab_copy(n).wait()
+        strip = tab_ref[n * cols : (n + 1) * cols, :]
+        for m in range(pieces):
+            if n == 0:
+                image_copy(m).wait()
+            levels = image_ref[m * per : (m + 1) * per].reshape(per * width, cells)
+            rows = dot(levels, strip, ((1,), (1,))).astype(BF)
+            out_ref[m * per : (m + 1) * per, :, n * cols : (n + 1) * cols] = rows.reshape(
+                per, width, cols
+            )
+            at = (pl.ds(m * per, per), slice(None), pl.ds(n * cols, cols))
+            copy = pltpu.make_async_copy(
+                out_ref.at[at], out_hbm.at[at], out_sem.at[n * pieces + m]
+            )
+            copy.start()
+            sent.append(copy)
+    for copy in sent:
+        copy.wait()
+
+
+def demig_kernel(bands, per, msg_ref, rows_hbm, out_ref, rows_ref, sem):
+    depth, width, long = rows_ref.shape
     block_len = long // bands
+    pieces = depth // per
+
+    def rows_copy(m):
+        at = pl.ds(m * per, per)
+        return pltpu.make_async_copy(rows_hbm.at[at], rows_ref.at[at], sem.at[m])
+
+    for m in range(pieces):
+        rows_copy(m).start()
     amp = msg_ref[:, :width]
-    shift = (width - pl.program_id(0) * levels) % width
-    marks = pltpu.roll(msg_ref[:, width:].astype(F32), shift, 1)
-    for i in range(levels):
-        band = jnp.broadcast_to(marks[:, i : i + 1], amp.shape).astype(BF)
-        rows = jnp.concatenate(
-            [rows_ref[i, :, b * block_len : (b + 1) * block_len] for b in range(bands)], axis=0
-        )
-        put(out_ref, i, dot(by_band(band, amp, bands), rows).astype(BF))
+    marks = msg_ref[:, width:].astype(F32)
+    for m in range(pieces):
+        rows_copy(m).wait()
+        for z in range(m * per, (m + 1) * per):
+            band = jnp.broadcast_to(marks[:, z : z + 1], amp.shape).astype(BF)
+            rows = jnp.concatenate(
+                [rows_ref[z, :, b * block_len : (b + 1) * block_len] for b in range(bands)], axis=0
+            )
+            put(out_ref, z, dot(by_band(band, amp, bands), rows).astype(BF))
 
 
 def residual_kernel(
@@ -158,12 +203,23 @@
         put(send_ref, z + 1, two[:, block_len:])
 
 
-def image_kernel(bands, amp_ref, band_ref, blk_ref, tab_ref, out_ref, stack_ref):
-    levels, width, cells = out_ref.shape
-    for i in range(levels):
-        masked = by_band(band_ref[i], get(blk_ref, i), bands)
-        stack_ref[i * width : (i + 1) * width, :] = dot(amp_ref[...], masked).astype(BF)
-    out_ref[...] = dot(stack_ref[...], tab_ref[...]).reshape(levels, width, cells)
+def image_kernel(
+    bands, per, amp_ref, band_ref, blk_ref, tab_ref, out_hbm, stack_ref, out_ref, sem
+):
+    depth, width, cells = out_ref.shape
+    sent = []
+    for m in range(depth // per):
+        for z in range(m * per, (m + 1) * per):
+            masked = by_band(band_ref[z], get(blk_ref, z), bands)
+            stack_ref[z * width : (z + 1) * width, :] = dot(amp_ref[...], masked).astype(BF)
+        stack = stack_ref[m * per * width : (m + 1) * per * width, :]
+        out_ref[m * per : (m + 1) * per] = dot(stack, tab_ref[...]).reshape(per, width, cells)
+        at = pl.ds(m * per, per)
+        copy = pltpu.make_async_copy(out_ref.at[at], out_hbm.at[at], sem.at[m])
+        copy.start()
+        sent.append(copy)
+    for copy in sent:
+        copy.wait()
 
 
 def shards(model_image, tables, observed, aperture, traveltime, band_index, amplitude):
@@ -176,7 +232,6 @@
     slots = devices * capacity
     pairs = traces * tile_count
     long = bands * block_len
-    levels = 4
     aligned = capacity % 8 == 0
     groups = pairs * blocks // 256
     tables_flat = tables.reshape(long, width_y)
@@ -188,11 +243,6 @@
         if aligned:
             return (devices, count, capacity, block_len)
         return (count, slots, block_len)
-
-    def block_of(count):
-        if aligned:
-            return pl.BlockSpec((devices, count, capacity, block_len), lambda z: (0, z, 0, 0))
-        return pl.BlockSpec((count, slots, block_len), lambda z: (z, 0, 0))
 
     def exchange(x):
         if not aligned:
@@ -214,28 +264,34 @@
     )(aperture.T, band_index.transpose(1, 2, 0), amplitude)
     got = lax.all_to_all(message, ("gx", "gy"), split_axis=0, concat_axis=0, tiled=True)
 
+    per, cols = depth // 2, long // 2
     rows = pl.pallas_call(
-        rows_kernel,
-        grid=(depth // levels,),
+        functools.partial(rows_kernel, per, cols),
         out_shape=jax.ShapeDtypeStruct((depth, width_x, long), BF),
-        in_specs=[
-            pl.BlockSpec((levels, width_x, width_y), lambda z: (z, 0, 0)),
-            pl.BlockSpec((long, width_y), lambda z: (0, 0)),
+        in_specs=[ANY, ANY],
+        out_specs=ANY,
+        scratch_shapes=[
+            pltpu.VMEM((depth, width_x, width_y), BF),
+            pltpu.VMEM((long, width_y), BF),
+            pltpu.VMEM((depth, width_x, long), BF),
+            pltpu.SemaphoreType.DMA((depth // per,)),
+            pltpu.SemaphoreType.DMA((long // cols,)),
+            pltpu.SemaphoreType.DMA((depth // per * (long // cols),)),
         ],
-        out_specs=pl.BlockSpec((levels, width_x, long), lambda z: (z, 0, 0)),
         cost_estimate=cost(2 * depth * width_x * width_y * long, 4 * depth * width_x * width_y),
         name="rows",
     )(model_image, tables_flat)
     rows = pltpu.with_memory_space_constraint(rows, pltpu.HBM)
+    per = 4
     partials = pl.pallas_call(
-        functools.partial(demig_kernel, bands),
-        grid=(depth // (2 * levels),),
+        functools.partial(demig_kernel, bands, per),
         out_shape=jax.ShapeDtypeStruct(shape_of(depth), BF),
-        in_specs=[
-            pl.BlockSpec((slots, 2 * width_x), lambda z: (0, 0)),
-            pl.BlockSpec((2 * levels, width_x, long), lambda z: (z, 0, 0)),
+        in_specs=[VMEM, ANY],
+        out_specs=VMEM,
+        scratch_shapes=[
+            pltpu.VMEM((depth, width_x, long), BF),
+            pltpu.SemaphoreType.DMA((depth // per,)),
         ],
-        out_specs=block_of(2 * levels),
         compiler_params=GRANT,
         cost_estimate=cost(2 * depth * slots * width_x * long, 2 * depth * width_x * long),
         name="demig",
@@ -270,19 +326,18 @@
         name="resid",
     )(place, take, pick, drop, observed, returned)
     incoming = exchange(outgoing)
+    per = 2
     gradient = pl.pallas_call(
-        functools.partial(image_kernel, bands),
-        grid=(depth // levels,),
+        functools.partial(image_kernel, bands, per),
         out_shape=jax.ShapeDtypeStruct((depth, width_x, width_y), F32),
-        in_specs=[
-            pl.BlockSpec((width_x, slots), lambda z: (0, 0)),
-            pl.BlockSpec((levels, slots, width_x), lambda z: (z, 0, 0)),
-            block_of(levels),
-            pl.BlockSpec((long, width_y), lambda z: (0, 0)),
+        in_specs=[VMEM] * 4,
+        out_specs=ANY,
+        scratch_shapes=[
+            pltpu.VMEM((depth * width_x, long), BF),
+            pltpu.VMEM((depth, width_x, width_y), F32),
+            pltpu.SemaphoreType.DMA((depth // per,)),
         ],
-        out_specs=pl.BlockSpec((levels, width_x, width_y), lambda z: (z, 0, 0)),
-        scratch_shapes=[pltpu.VMEM((levels * width_x, long), BF)],
-        compiler_params=GRANT,
+        compiler_params=pltpu.CompilerParams(vmem_limit_bytes=32 * 1024 * 1024),
         cost_estimate=cost(
             2 * depth * width_x * long * (width_y + slots), 4 * depth * width_x * width_y
         ),

time: 95.7 us -> 93.9 us (0.981)
  Pallas kernels: 27.3 us -> 25.4 us
    pallas_call x3, Pallas kernels: 22.2 us -> 20.3 us  [the longest x1 7.89 us: shards(): pl.pallas_call(functools.partial(rows_kernel, per, cols), out_shape=jax.S...]
where the time goes in v7:
time: 93.9 us; the launch traced here: 93.5 us
  blocking collectives  29.3 us (31%)
  Pallas kernels  25.4 us (27%)
  waiting for transfers between devices  22.7 us (24%)
  starting transfers between devices  12.9 us (14%)
  local copies, waits for them, and re-layouts  2.35 us (3%)
    all_to_all x1, blocking collectives, exchange(): x = lax.all_to_all(x, ('gx', 'gy'), split_axis=0, concat_axis=0, tiled=True)  29.3 us
    all_to_all x1, waiting for transfers between devices, exchange(): x = lax.all_to_all(x, ('gx', 'gy'), split_axis=0, concat_axis=0, tiled=True)  22.7 us
    pallas_call x1, Pallas kernels, shards(): pl.pallas_call(functools.partial(rows_kernel, per, cols), out_shape=jax.S...  7.89 us
    all_to_all x1, starting transfers between devices, shards(): lax.all_to_all(message, ('gx', 'gy'), split_axis=0, concat_axis=0, tiled=...  7.08 us
    pallas_call x1, Pallas kernels, shards(): pl.pallas_call(functools.partial(image_kernel, bands, per), out_shape=jax...  7.05 us
    all_to_all x1, starting transfers between devices, exchange(): x = lax.all_to_all(x, ('gx', 'gy'), split_axis=0, concat_axis=0, tiled=True)  5.83 us
    pallas_call x1, Pallas kernels, shards(): pl.pallas_call(functools.partial(demig_kernel, bands, per), out_shape=jax...  5.32 us
    unnamed x16, local copies, waits for them, and re-layouts  2.35 us
  transfers between devices with their start and end apart: 2, of which 1 were waited for; matrix products, arithmetic and copies ran while one was open for 0% of the time, Pallas kernels for 10%

profile of v7, /device:TPU:1, one launch (start us, length us, event | category | flops | bytes accessed | tf_op | source)
XLA Modules:
  0.0 93.5 jit_solution(16712563189053124279)
XLA Ops:
  0.6 2.2 %prep.1 = (bf16[256,256]{1,0:T(8,128)(2,1)}, bf16[256,128]{1,0:T(8,128)(2,1)}) custom-call(s32[4,32]{1,0:T(4,128)} %bitcast.13, s32[4,16,32]{2,1,0:T(8,128)} %bitcast.12, bf16[32,4,128]{2,1,0:T(4,128)(2,1)} %am_ref.1), custom_call_target="tpu_custom_call" | custom-call | tf_op jit(solution)/shard_map/prep/pallas_call | solution.py:255
  2.8 7.1 %all-to-all-start = ((bf16[32,8,256]{2,1,0:T(8,128)(2,1)}), bf16[32,8,256]{2,1,0:T(8,128)(2,1)S(1)}, u32[]{:S(2)}, u32[]{:S(2)}) async-start(bf16[32,8,256]{2,1,0:T(8,128)(2,1)} %bitcast.11), calls=%async_computation | async-start | bytes 262144 | tf_op jit(solution)/shard_map/all_to_all | solution.py:265
  9.9 7.9 %rows.1.rows_hbm = bf16[16,128,1024]{2,1,0:T(8,128)(2,1)} custom-call(bf16[16,128,1024]{2,1,0:T(8,128)(2,1)} %image_hbm.1, bf16[1024,1024]{1,0:T(8,128)(2,1)} %bitcast.8), custom_call_target="tpu_custom_call" | custom-call | flops 4294967296 | bytes 8388608 | tf_op jit(solution)/shard_map/rows/pallas_call | solution.py:268
  17.8 0.0 copy-start.1
  17.8 0.0 copy-start
  17.8 0.0 all-to-all-done
  17.8 5.3 %demig.1 = bf16[32,16,8,128]{3,2,1,0:T(8,128)(2,1)} custom-call(bf16[256,256]{1,0:T(8,128)(2,1)S(1)} %bitcast.6, bf16[16,128,1024]{2,1,0:T(8,128)(2,1)} %rows.1.rows_hbm), custom_call_target="tpu_custom_call" | custom-call | flops 1073741824 | bytes 4194304 | tf_op jit(solution)/shard_map/demig/pallas_call | solution.py:286
  23.1 5.8 %all-to-all-start.1 = ((bf16[32,16,8,128]{3,2,1,0:T(8,128)(2,1)}), bf16[32,16,8,128]{3,2,1,0:T(8,128)(2,1)S(1)}, u32[]{:S(2)}, u32[]{:S(2)}) async-start(bf16[32,16,8,128]{3,2,1,0:T(8,128)(2,1)} %demig.1), calls=%async_computation.1 | async-start | bytes 2097152 | tf_op jit(solution)/shard_map/all_to_all | solution.py:250
  29.0 0.0 copy-done.1
  29.0 0.0 copy-start.3
  29.0 0.7 copy-done.3
  29.8 1.3 %codes.1 = (bf16[128,256]{1,0:T(8,128)(2,1)S(1)}, bf16[8,256,256]{2,1,0:T(8,128)(2,1)S(1)}, bf16[8,256,256]{2,1,0:T(8,128)(2,1)S(1)}, bf16[128,256]{1,0:T(8,128)(2,1)S(1)}, bf16[16,256,128]{2,1,0:T(8,128)(2,1)S(1)}) custom-call(bf16[256,256]{1,0:T(8,128)(2,1)S(1)} %bitcast.7, bf16[256,128]{1,0:T(8,128)(2,1)S(1)} %copy-done.1, s32[4,16,32]{2,1,0:T(8,128)S(1)} %bitcast.10), custom_call_target="tpu_custom_call" | custom-call | flops 134217728 | bytes 2097152 | tf_op jit(solution)/shard_map/codes/pallas_call | solution.py:300
  31.0 0.0 copy-start.4
  31.0 1.0 %copy-done.4 = bf16[16,256,128]{2,1,0:T(8,128)(2,1)} copy-done((bf16[16,256,128]{2,1,0:T(8,128)(2,1)}, bf16[16,256,128]{2,1,0:T(8,128)(2,1)S(1)}, u32[]{:S(2)}) %copy-start.4) | copy-done | bytes 1048600
  32.0 0.0 copy-start.6
  32.0 0.6 copy-done.6
  32.6 22.7 %all-to-all-done.1.recv_ref = bf16[32,16,8,128]{3,2,1,0:T(8,128)(2,1)S(1)} async-done(((bf16[32,16,8,128]{3,2,1,0:T(8,128)(2,1)}), bf16[32,16,8,128]{3,2,1,0:T(8,128)(2,1)S(1)}, u32[]{:S(2)}, u32[]{:S(2)}) %all-to-all-start.1) | async-done | bytes 1048608 | tf_op jit(solution)/shard_map/all_to_all | solution.py:250
  55.3 0.0 copy-start.2
  55.3 0.0 copy-start.5
  55.3 0.0 copy-start.7
  55.3 0.0 copy-done
  55.3 1.7 %resid.1 = (f32[32,16,128]{2,1,0:T(8,128)}, bf16[32,16,8,128]{3,2,1,0:T(8,128)(2,1)S(1)}) custom-call(bf16[256,128]{1,0:T(8,128)(2,1)S(1)} %copy-done.1, bf16[128,256]{1,0:T(8,128)(2,1)S(1)} %get-tuple-element.13.take_ref, bf16[8,256,256]{2,1,0:T(8,128)(2,1)S(1)} %get-tuple-element.14.pick_ref, bf16[8,256,256]{2,1,0:T(8,128)(2,1)S(1)} %get-tuple-element.15.drop_ref, ...), custom_call_target="tpu_custom_call" | custom-call | flops 268435456 | bytes 2097152 | tf_op jit(solution)/shard_map/resid/pallas_call | solution.py:315
  57.0 29.3 %all_to_all.21.blk_ref = bf16[32,16,8,128]{3,2,1,0:T(8,128)(2,1)S(1)} all-to-all(bf16[32,16,8,128]{3,2,1,0:T(8,128)(2,1)S(1)} %get-tuple-element.19), channel_id=1, replica_groups=mesh['gx'=8,'gy'=4] {'gx','gy'}, dimensions={0} | all-to-all | bytes 2097152 | tf_op jit(solution)/shard_map/all_to_all | solution.py:250
  86.3 0.0 copy-done.2
  86.3 0.0 copy-done.5
  86.3 0.0 copy-done.7
  86.3 7.1 %image.1 = f32[16,128,1024]{2,1,0:T(8,128)} custom-call(bf16[128,256]{1,0:T(8,128)(2,1)S(1)} %copy-done.7, bf16[16,256,128]{2,1,0:T(8,128)(2,1)S(1)} %copy-done.5, bf16[32,16,8,128]{3,2,1,0:T(8,128)(2,1)S(1)} %all_to_all.21.blk_ref, bf16[1024,1024]{1,0:T(8,128)(2,1)S(1)} %bitcast.9), custom_call_target="tpu_custom_call" | custom-call | flops 5368709120 | bytes 8388608 | tf_op jit(solution)/shard_map/image/pallas_call | solution.py:330
Async XLA Ops:
  2.8 15.0 %all-to-all-start = ((bf16[32,8,256]{2,1,0:T(8,128)(2,1)}), bf16[32,8,256]{2,1,0:T(8,128)(2,1)S(1)}, u32[]{:S(2)}, u32[]{:S(2)}) async-start(bf16[32,8,256]{2,1,0:T(8,128)(2,1)} %bitcast.11), calls=%async_computation | async-start | bytes 262144 | tf_op jit(solution)/shard_map/all_to_all | solution.py:265
  17.8 11.2 %copy-start.1 = (bf16[256,128]{1,0:T(8,128)(2,1)S(1)}, bf16[256,128]{1,0:T(8,128)(2,1)}, u32[]{:S(2)}) copy-start(bf16[256,128]{1,0:T(8,128)(2,1)} %get-tuple-element.11.place_ref) | copy-start | bytes 196612
  17.8 37.5 %copy-start = (bf16[32,16,128]{2,1,0:T(8,128)(2,1)S(1)}, bf16[32,16,128]{2,1,0:T(8,128)(2,1)}, u32[]{:S(2)}) copy-start(bf16[32,16,128]{2,1,0:T(8,128)(2,1)} %obs_ref.1) | copy-start | bytes 393220
  23.1 32.2 %all-to-all-start.1 = ((bf16[32,16,8,128]{3,2,1,0:T(8,128)(2,1)}), bf16[32,16,8,128]{3,2,1,0:T(8,128)(2,1)S(1)}, u32[]{:S(2)}, u32[]{:S(2)}) async-start(bf16[32,16,8,128]{3,2,1,0:T(8,128)(2,1)} %demig.1), calls=%async_computation.1 | async-start | bytes 2097152 | tf_op jit(solution)/shard_map/all_to_all | solution.py:250
  29.0 0.8 copy-start.3
  31.0 1.0 %copy-start.4 = (bf16[16,256,128]{2,1,0:T(8,128)(2,1)}, bf16[16,256,128]{2,1,0:T(8,128)(2,1)S(1)}, u32[]{:S(2)}) copy-start(bf16[16,256,128]{2,1,0:T(8,128)(2,1)S(1)} %get-tuple-element.18.band_ref) | copy-start | bytes 3145732
  32.0 0.6 copy-start.6
  55.3 31.0 %copy-start.2 = (bf16[8,128,1024]{2,1,0:T(8,128)(2,1)S(1)}, bf16[8,128,1024]{2,1,0:T(8,128)(2,1)}, u32[]{:S(2)}) copy-start(bf16[8,128,1024]{2,1,0:T(8,128)(2,1)} %param.8) | copy-start | bytes 6291460
  55.3 31.0 %copy-start.5 = (bf16[16,256,128]{2,1,0:T(8,128)(2,1)S(1)}, bf16[16,256,128]{2,1,0:T(8,128)(2,1)}, u32[]{:S(2)}) copy-start(bf16[16,256,128]{2,1,0:T(8,128)(2,1)} %copy-done.4) | copy-start | bytes 3145732
  55.3 31.0 %copy-start.7 = (bf16[128,256]{1,0:T(8,128)(2,1)S(1)}, bf16[128,256]{1,0:T(8,128)(2,1)}, u32[]{:S(2)}) copy-start(bf16[128,256]{1,0:T(8,128)(2,1)} %copy-done.6) | copy-start | bytes 196612

commit v8 on v7

--- a/solution.py
+++ b/solution.py
@@ -49,17 +49,17 @@
     msg_ref[:, width:] = marks.astype(BF)
 
 
-def codes_kernel(
-    blocks, msg_ref, place_ref, tt_ref, take_ref, pick_ref, drop_ref, amp_ref, band_ref
-):
+def marks_kernel(msg_ref, tab_hbm, amp_ref, tab_ref, sem):
+    width = amp_ref.shape[0]
+    copy = pltpu.make_async_copy(tab_hbm, tab_ref, sem)
+    copy.start()
+    amp_ref[...] = msg_ref[:, :width].astype(F32).T.astype(BF)
+    copy.wait()
+
+
+def codes_kernel(blocks, place_ref, tt_ref, take_ref, pick_ref, drop_ref):
     tiles, depth, traces = tt_ref.shape
     group = 256 // blocks
-    width = amp_ref.shape[0]
-    amp_ref[...] = msg_ref[:, :width].astype(F32).T.astype(BF)
-    for z in range(0, depth, 2):
-        both = spread(msg_ref[:, width:], z, z + 1)
-        band_ref[z] = both[:, :width]
-        band_ref[z + 1] = both[:, width:]
     take_ref[...] = place_ref[...].astype(F32).T.astype(BF)
     size = depth * group
     lanes = 128
@@ -87,13 +87,6 @@
     return jnp.concatenate([jnp.where(band == BF(b), values, zero) for b in range(bands)], axis=1)
 
 
-def spread(marks, first, second):
-    width = marks.shape[1]
-    lane = iota((width, 2 * width), 1)
-    want = jnp.where(lane < width, first, second)
-    return dot(marks, (iota((width, 2 * width), 0) == want).astype(F32).astype(BF)).astype(BF)
-
-
 def put(ref, z, value):
     if len(ref.shape) == 4:
         ref[:, z] = value.reshape(ref.shape[0], ref.shape[2], ref.shape[3])
@@ -108,7 +101,18 @@
 
 
 def rows_kernel(
-    per, cols, image_hbm, tab_hbm, out_hbm, image_ref, tab_ref, out_ref, image_sem, tab_sem, out_sem
+    per,
+    cols,
+    image_hbm,
+    tab_hbm,
+    out_hbm,
+    image_ref,
+    tab_ref,
+    turn_ref,
+    out_ref,
+    image_sem,
+    tab_sem,
+    out_sem,
 ):
     depth, width, cells = image_ref.shape
     pieces, strips = depth // per, tab_ref.shape[0] // cols
@@ -127,14 +131,17 @@
     for n in range(1, strips):
         tab_copy(n).start()
     sent = []
+    tab_copy(0).wait()
+    turn_ref[0] = tab_ref[:cols, :].T
     for n in range(strips):
-        tab_copy(n).wait()
-        strip = tab_ref[n * cols : (n + 1) * cols, :]
         for m in range(pieces):
             if n == 0:
                 image_copy(m).wait()
+            if m == pieces - 1 and n + 1 < strips:
+                tab_copy(n + 1).wait()
+                turn_ref[n + 1] = tab_ref[(n + 1) * cols : (n + 2) * cols, :].T
             levels = image_ref[m * per : (m + 1) * per].reshape(per * width, cells)
-            rows = dot(levels, strip, ((1,), (1,))).astype(BF)
+            rows = dot(levels, turn_ref[n]).astype(BF)
             out_ref[m * per : (m + 1) * per, :, n * cols : (n + 1) * cols] = rows.reshape(
                 per, width, cols
             )
@@ -204,13 +211,16 @@
 
 
 def image_kernel(
-    bands, per, amp_ref, band_ref, blk_ref, tab_ref, out_hbm, stack_ref, out_ref, sem
+    bands, per, msg_ref, amp_ref, blk_ref, tab_ref, out_hbm, stack_ref, out_ref, sem
 ):
     depth, width, cells = out_ref.shape
+    marks = msg_ref[:, width:].astype(F32)
     sent = []
     for m in range(depth // per):
         for z in range(m * per, (m + 1) * per):
-            masked = by_band(band_ref[z], get(blk_ref, z), bands)
+            picked = get(blk_ref, z)
+            band = jnp.broadcast_to(marks[:, z : z + 1], picked.shape).astype(BF)
+            masked = by_band(band, picked, bands)
             stack_ref[z * width : (z + 1) * width, :] = dot(amp_ref[...], masked).astype(BF)
         stack = stack_ref[m * per * width : (m + 1) * per * width, :]
         out_ref[m * per : (m + 1) * per] = dot(stack, tab_ref[...]).reshape(per, width, cells)
@@ -273,6 +283,7 @@
         scratch_shapes=[
             pltpu.VMEM((depth, width_x, width_y), BF),
             pltpu.VMEM((long, width_y), BF),
+            pltpu.VMEM((long // cols, width_y, cols), BF),
             pltpu.VMEM((depth, width_x, long), BF),
             pltpu.SemaphoreType.DMA((depth // per,)),
             pltpu.SemaphoreType.DMA((long // cols,)),
@@ -297,21 +308,19 @@
         name="demig",
     )(got, rows)
     returned = exchange(partials)
-    take, pick, drop, turned, spread_bands = pl.pallas_call(
+    take, pick, drop = pl.pallas_call(
         functools.partial(codes_kernel, blocks),
         out_shape=(
             jax.ShapeDtypeStruct((pairs, slots), BF),
             jax.ShapeDtypeStruct((groups, 256, 256), BF),
             jax.ShapeDtypeStruct((groups, 256, 256), BF),
-            jax.ShapeDtypeStruct((width_x, slots), BF),
-            jax.ShapeDtypeStruct((depth, slots, width_x), BF),
-        ),
-        in_specs=[VMEM] * 3,
-        out_specs=(VMEM,) * 5,
+        ),
+        in_specs=[VMEM] * 2,
+        out_specs=(VMEM,) * 3,
         compiler_params=GRANT,
         cost_estimate=cost(groups * 256 * 256 * 256, groups * 256 * 256 * 4),
         name="codes",
-    )(got, place, traveltime.transpose(1, 2, 0))
+    )(place, traveltime.transpose(1, 2, 0))
     residual, outgoing = pl.pallas_call(
         residual_kernel,
         out_shape=(
@@ -326,6 +335,20 @@
         name="resid",
     )(place, take, pick, drop, observed, returned)
     incoming = exchange(outgoing)
+    _, got_late = lax.optimization_barrier((residual, got))
+    turned, tables_near = pl.pallas_call(
+        marks_kernel,
+        out_shape=(
+            jax.ShapeDtypeStruct((width_x, slots), BF),
+            jax.ShapeDtypeStruct((long, width_y), BF),
+        ),
+        in_specs=[VMEM, ANY],
+        out_specs=(VMEM,) * 2,
+        scratch_shapes=[pltpu.SemaphoreType.DMA],
+        compiler_params=GRANT,
+        cost_estimate=cost(slots * width_x, 4 * long * width_y),
+        name="marks",
+    )(got_late, pltpu.with_memory_space_constraint(tables_flat, pltpu.HBM))
     per = 2
     gradient = pl.pallas_call(
         functools.partial(image_kernel, bands, per),
@@ -342,7 +365,7 @@
             2 * depth * width_x * long * (width_y + slots), 4 * depth * width_x * width_y
         ),
         name="image",
-    )(turned, spread_bands, incoming, tables_flat)
+    )(got, turned, incoming, tables_near)
     return residual, gradient
 
 

time: 93.9 us -> 94.8 us (level)
  blocking collectives: 29.3 us -> 0 us
  waiting for transfers between devices: 22.7 us -> 49.3 us
  starting transfers between devices: 12.9 us -> 16.1 us
  Pallas kernels: 25.4 us -> 27.3 us
  local copies, waits for them, and re-layouts: 2.35 us -> 0.76 us
    all_to_all x1 -> x0, blocking collectives: 29.3 us -> none  [exchange(): x = lax.all_to_all(x, ('gx', 'gy'), split_axis=0, concat_axis=0, tiled=True)]
    all_to_all x1 -> x2, waiting for transfers between devices: 22.7 us -> 49.3 us  [exchange(): x = lax.all_to_all(x, ('gx', 'gy'), split_axis=0, concat_axis=0, tiled=True)]
    all_to_all x1 -> x2, starting transfers between devices: 5.83 us -> 9 us  [exchange(): x = lax.all_to_all(x, ('gx', 'gy'), split_axis=0, concat_axis=0, tiled=True)]
    pallas_call x0 -> x1, Pallas kernels: none -> 1.6 us  [shards(): pl.pallas_call(marks_kernel, out_shape=(jax.ShapeDtypeStruct((width_x, sl...]
    unnamed x16 -> x6, local copies, waits for them, and re-layouts: 2.35 us -> 0.76 us
  transfers between devices with their start and end apart: 2 -> 3, of which waited for: 1 -> 2; matrix products, arithmetic and copies ran while one was open for 0% -> 0% of each run, Pallas kernels for 10% -> 11%
where the time goes in v8:
time: 94.8 us; the launch traced here: 94.3 us
  waiting for transfers between devices  49.3 us (52%)
  Pallas kernels  27.3 us (29%)
  starting transfers between devices  16.1 us (17%)
    all_to_all x2, waiting for transfers between devices, exchange(): x = lax.all_to_all(x, ('gx', 'gy'), split_axis=0, concat_axis=0, tiled=True)  49.3 us
    all_to_all x2, starting transfers between devices, exchange(): x = lax.all_to_all(x, ('gx', 'gy'), split_axis=0, concat_axis=0, tiled=True)  9 us
    pallas_call x1, Pallas kernels, shards(): pl.pallas_call(functools.partial(rows_kernel, per, cols), out_shape=jax.S...  7.63 us
    all_to_all x1, starting transfers between devices, shards(): lax.all_to_all(message, ('gx', 'gy'), split_axis=0, concat_axis=0, tiled=...  7.08 us
    pallas_call x1, Pallas kernels, shards(): pl.pallas_call(functools.partial(image_kernel, bands, per), out_shape=jax...  7.05 us
    pallas_call x1, Pallas kernels, shards(): pl.pallas_call(functools.partial(demig_kernel, bands, per), out_shape=jax...  5.31 us
    pallas_call x1, Pallas kernels, shards(): pl.pallas_call(residual_kernel, out_shape=(jax.ShapeDtypeStruct((traces,...  2.6 us
    pallas_call x1, Pallas kernels, shards(): pl.pallas_call(functools.partial(prep_kernel, devices, capacity), out_sha...  2.16 us
  transfers between devices with their start and end apart: 3, of which 2 were waited for; matrix products, arithmetic and copies ran while one was open for 0% of the time, Pallas kernels for 11%

profile of v8, /device:TPU:1, one launch (start us, length us, event | category | flops | bytes accessed | tf_op | source)
XLA Modules:
  0.0 94.3 jit_solution(35471767499187453)
XLA Ops:
  0.6 2.2 %prep.1 = (bf16[256,256]{1,0:T(8,128)(2,1)}, bf16[256,128]{1,0:T(8,128)(2,1)}) custom-call(s32[4,32]{1,0:T(4,128)} %bitcast.14, s32[4,16,32]{2,1,0:T(8,128)} %bitcast.13, bf16[32,4,128]{2,1,0:T(4,128)(2,1)} %am_ref.1), custom_call_target="tpu_custom_call" | custom-call | tf_op jit(solution)/shard_map/prep/pallas_call | solution.py:265
  2.8 7.1 %all-to-all-start = ((bf16[32,8,256]{2,1,0:T(8,128)(2,1)}), bf16[32,8,256]{2,1,0:T(8,128)(2,1)S(1)}, u32[]{:S(2)}, u32[]{:S(2)}) async-start(bf16[32,8,256]{2,1,0:T(8,128)(2,1)} %bitcast.12), calls=%async_computation | async-start | bytes 262144 | tf_op jit(solution)/shard_map/all_to_all | solution.py:275
  9.9 7.6 %rows.1.rows_hbm = bf16[16,128,1024]{2,1,0:T(8,128)(2,1)} custom-call(bf16[16,128,1024]{2,1,0:T(8,128)(2,1)} %image_hbm.1, bf16[1024,1024]{1,0:T(8,128)(2,1)} %bitcast.10), custom_call_target="tpu_custom_call" | custom-call | flops 4294967296 | bytes 8388608 | tf_op jit(solution)/shard_map/rows/pallas_call | solution.py:278
  17.5 0.0 copy-start.1
  17.5 0.0 copy-start
  17.5 0.0 all-to-all-done
  17.5 5.3 %demig.1 = bf16[32,16,8,128]{3,2,1,0:T(8,128)(2,1)} custom-call(bf16[256,256]{1,0:T(8,128)(2,1)S(1)} %bitcast.6, bf16[16,128,1024]{2,1,0:T(8,128)(2,1)} %rows.1.rows_hbm), custom_call_target="tpu_custom_call" | custom-call | flops 1073741824 | bytes 4194304 | tf_op jit(solution)/shard_map/demig/pallas_call | solution.py:297
  22.9 5.8 %all-to-all-start.1 = ((bf16[32,16,8,128]{3,2,1,0:T(8,128)(2,1)}), bf16[32,16,8,128]{3,2,1,0:T(8,128)(2,1)S(1)}, u32[]{:S(2)}, u32[]{:S(2)}) async-start(bf16[32,16,8,128]{3,2,1,0:T(8,128)(2,1)} %demig.1), calls=%async_computation.1 | async-start | bytes 2097152 | tf_op jit(solution)/shard_map/all_to_all | solution.py:260
  28.7 0.0 copy-done.1
  28.7 0.0 copy-start.2
  28.7 0.7 copy-done.2
  29.5 1.0 %codes.1 = (bf16[128,256]{1,0:T(8,128)(2,1)S(1)}, bf16[8,256,256]{2,1,0:T(8,128)(2,1)S(1)}, bf16[8,256,256]{2,1,0:T(8,128)(2,1)S(1)}) custom-call(bf16[256,128]{1,0:T(8,128)(2,1)S(1)} %copy-done.1, s32[4,16,32]{2,1,0:T(8,128)S(1)} %bitcast.9), custom_call_target="tpu_custom_call" | custom-call | flops 134217728 | bytes 2097152 | tf_op jit(solution)/shard_map/codes/pallas_call | solution.py:311
  30.5 24.6 %all-to-all-done.1.recv_ref = bf16[32,16,8,128]{3,2,1,0:T(8,128)(2,1)S(1)} async-done(((bf16[32,16,8,128]{3,2,1,0:T(8,128)(2,1)}), bf16[32,16,8,128]{3,2,1,0:T(8,128)(2,1)S(1)}, u32[]{:S(2)}, u32[]{:S(2)}) %all-to-all-start.1) | async-done | bytes 1048608 | tf_op jit(solution)/shard_map/all_to_all | solution.py:260
  55.0 0.0 copy-done
  55.0 2.6 %resid.1 = (f32[32,16,128]{2,1,0:T(8,128)}, bf16[32,16,8,128]{3,2,1,0:T(8,128)(2,1)}) custom-call(bf16[256,128]{1,0:T(8,128)(2,1)S(1)} %copy-done.1, bf16[128,256]{1,0:T(8,128)(2,1)S(1)} %get-tuple-element.13.take_ref, bf16[8,256,256]{2,1,0:T(8,128)(2,1)S(1)} %get-tuple-element.14.pick_ref, bf16[8,256,256]{2,1,0:T(8,128)(2,1)S(1)} %get-tuple-element.15.drop_ref, ...), custom_call_target="tpu_custom_call" | custom-call | flops 268435456 | bytes 2097152 | tf_op jit(solution)/shard_map/resid/pallas_call | solution.py:324
  57.6 3.2 %all-to-all-start.2 = ((bf16[32,16,8,128]{3,2,1,0:T(8,128)(2,1)}), bf16[32,16,8,128]{3,2,1,0:T(8,128)(2,1)S(1)}, u32[]{:S(2)}, u32[]{:S(2)}) async-start(bf16[32,16,8,128]{3,2,1,0:T(8,128)(2,1)} %get-tuple-element.20), calls=%async_computation.2 | async-start | bytes 2097152 | tf_op jit(solution)/shard_map/all_to_all | solution.py:260
  60.8 1.6 %marks.1 = (bf16[128,256]{1,0:T(8,128)(2,1)S(1)}, bf16[1024,1024]{1,0:T(8,128)(2,1)S(1)}) custom-call(bf16[256,256]{1,0:T(8,128)(2,1)S(1)} %bitcast.7, bf16[1024,1024]{1,0:T(8,128)(2,1)} %bitcast.11), custom_call_target="tpu_custom_call" | custom-call | flops 32768 | bytes 4194304 | tf_op jit(solution)/shard_map/marks/pallas_call | solution.py:339
  62.4 24.7 %all-to-all-done.2.blk_ref = bf16[32,16,8,128]{3,2,1,0:T(8,128)(2,1)S(1)} async-done(((bf16[32,16,8,128]{3,2,1,0:T(8,128)(2,1)}), bf16[32,16,8,128]{3,2,1,0:T(8,128)(2,1)S(1)}, u32[]{:S(2)}, u32[]{:S(2)}) %all-to-all-start.2) | async-done | bytes 1048608 | tf_op jit(solution)/shard_map/all_to_all | solution.py:260
  87.1 7.0 %image.1 = f32[16,128,1024]{2,1,0:T(8,128)} custom-call(bf16[256,256]{1,0:T(8,128)(2,1)S(1)} %bitcast.8, bf16[128,256]{1,0:T(8,128)(2,1)S(1)} %get-tuple-element.19.amp_ref, bf16[32,16,8,128]{3,2,1,0:T(8,128)(2,1)S(1)} %all-to-all-done.2.blk_ref, bf16[1024,1024]{1,0:T(8,128)(2,1)S(1)} %get-tuple-element.21.tab_ref), custom_call_target="tpu_custom_call" | custom-call | flops 5368709120 | bytes 8388608 | tf_op jit(solution)/shard_map/image/pallas_call | solution.py:353
Async XLA Ops:
  2.8 14.8 %all-to-all-start = ((bf16[32,8,256]{2,1,0:T(8,128)(2,1)}), bf16[32,8,256]{2,1,0:T(8,128)(2,1)S(1)}, u32[]{:S(2)}, u32[]{:S(2)}) async-start(bf16[32,8,256]{2,1,0:T(8,128)(2,1)} %bitcast.12), calls=%async_computation | async-start | bytes 262144 | tf_op jit(solution)/shard_map/all_to_all | solution.py:275
  17.5 11.2 %copy-start.1 = (bf16[256,128]{1,0:T(8,128)(2,1)S(1)}, bf16[256,128]{1,0:T(8,128)(2,1)}, u32[]{:S(2)}) copy-start(bf16[256,128]{1,0:T(8,128)(2,1)} %get-tuple-element.12.place_ref) | copy-start | bytes 196612
  17.5 37.5 %copy-start = (bf16[32,16,128]{2,1,0:T(8,128)(2,1)S(1)}, bf16[32,16,128]{2,1,0:T(8,128)(2,1)}, u32[]{:S(2)}) copy-start(bf16[32,16,128]{2,1,0:T(8,128)(2,1)} %obs_ref.1) | copy-start | bytes 393220
  22.9 32.2 %all-to-all-start.1 = ((bf16[32,16,8,128]{3,2,1,0:T(8,128)(2,1)}), bf16[32,16,8,128]{3,2,1,0:T(8,128)(2,1)S(1)}, u32[]{:S(2)}, u32[]{:S(2)}) async-start(bf16[32,16,8,128]{3,2,1,0:T(8,128)(2,1)} %demig.1), calls=%async_computation.1 | async-start | bytes 2097152 | tf_op jit(solution)/shard_map/all_to_all | solution.py:260
  28.7 0.8 copy-start.2
  57.6 29.5 %all-to-all-start.2 = ((bf16[32,16,8,128]{3,2,1,0:T(8,128)(2,1)}), bf16[32,16,8,128]{3,2,1,0:T(8,128)(2,1)S(1)}, u32[]{:S(2)}, u32[]{:S(2)}) async-start(bf16[32,16,8,128]{3,2,1,0:T(8,128)(2,1)} %get-tuple-element.20), calls=%async_computation.2 | async-start | bytes 2097152 | tf_op jit(solution)/shard_map/all_to_all | solution.py:260

commit v9 on v8

--- a/solution.py
+++ b/solution.py
@@ -49,17 +49,11 @@
     msg_ref[:, width:] = marks.astype(BF)
 
 
-def marks_kernel(msg_ref, tab_hbm, amp_ref, tab_ref, sem):
-    width = amp_ref.shape[0]
-    copy = pltpu.make_async_copy(tab_hbm, tab_ref, sem)
-    copy.start()
-    amp_ref[...] = msg_ref[:, :width].astype(F32).T.astype(BF)
-    copy.wait()
-
-
-def codes_kernel(blocks, place_ref, tt_ref, take_ref, pick_ref, drop_ref):
+def codes_kernel(blocks, msg_ref, place_ref, tt_ref, take_ref, pick_ref, drop_ref, amp_ref):
     tiles, depth, traces = tt_ref.shape
     group = 256 // blocks
+    width = amp_ref.shape[0]
+    amp_ref[...] = msg_ref[:, :width].astype(F32).T.astype(BF)
     take_ref[...] = place_ref[...].astype(F32).T.astype(BF)
     size = depth * group
     lanes = 128
@@ -308,19 +302,20 @@
         name="demig",
     )(got, rows)
     returned = exchange(partials)
-    take, pick, drop = pl.pallas_call(
+    take, pick, drop, turned = pl.pallas_call(
         functools.partial(codes_kernel, blocks),
         out_shape=(
             jax.ShapeDtypeStruct((pairs, slots), BF),
             jax.ShapeDtypeStruct((groups, 256, 256), BF),
             jax.ShapeDtypeStruct((groups, 256, 256), BF),
+            jax.ShapeDtypeStruct((width_x, slots), BF),
         ),
-        in_specs=[VMEM] * 2,
-        out_specs=(VMEM,) * 3,
+        in_specs=[VMEM] * 3,
+        out_specs=(VMEM,) * 4,
         compiler_params=GRANT,
         cost_estimate=cost(groups * 256 * 256 * 256, groups * 256 * 256 * 4),
         name="codes",
-    )(place, traveltime.transpose(1, 2, 0))
+    )(got, place, traveltime.transpose(1, 2, 0))
     residual, outgoing = pl.pallas_call(
         residual_kernel,
         out_shape=(
@@ -335,20 +330,6 @@
         name="resid",
     )(place, take, pick, drop, observed, returned)
     incoming = exchange(outgoing)
-    _, got_late = lax.optimization_barrier((residual, got))
-    turned, tables_near = pl.pallas_call(
-        marks_kernel,
-        out_shape=(
-            jax.ShapeDtypeStruct((width_x, slots), BF),
-            jax.ShapeDtypeStruct((long, width_y), BF),
-        ),
-        in_specs=[VMEM, ANY],
-        out_specs=(VMEM,) * 2,
-        scratch_shapes=[pltpu.SemaphoreType.DMA],
-        compiler_params=GRANT,
-        cost_estimate=cost(slots * width_x, 4 * long * width_y),
-        name="marks",
-    )(got_late, pltpu.with_memory_space_constraint(tables_flat, pltpu.HBM))
     per = 2
     gradient = pl.pallas_call(
         functools.partial(image_kernel, bands, per),
@@ -365,7 +346,7 @@
             2 * depth * width_x * long * (width_y + slots), 4 * depth * width_x * width_y
         ),
         name="image",
-    )(got, turned, incoming, tables_near)
+    )(got, turned, incoming, tables_flat)
     return residual, gradient
 
 

time: 94.8 us -> 93.6 us (0.987)
  blocking collectives: 0 us -> 29.3 us
  waiting for transfers between devices: 49.3 us -> 23.9 us
  starting transfers between devices: 16.1 us -> 12.9 us
  Pallas kernels: 27.3 us -> 24.8 us
    all_to_all x0 -> x1, blocking collectives: none -> 29.3 us  [exchange(): x = lax.all_to_all(x, ('gx', 'gy'), split_axis=0, concat_axis=0, tiled=True)]
    all_to_all x2 -> x1, waiting for transfers between devices: 49.3 us -> 23.9 us  [exchange(): x = lax.all_to_all(x, ('gx', 'gy'), split_axis=0, concat_axis=0, tiled=True)]
    all_to_all x2 -> x1, starting transfers between devices: 9 us -> 5.84 us  [exchange(): x = lax.all_to_all(x, ('gx', 'gy'), split_axis=0, concat_axis=0, tiled=True)]
    pallas_call x1 -> x0, Pallas kernels: 1.6 us -> none  [shards(): pl.pallas_call(marks_kernel, out_shape=(jax.ShapeDtypeStruct((width_x, sl...]
  transfers between devices with their start and end apart: 3 -> 2, of which waited for: 2 -> 1; matrix products, arithmetic and copies ran while one was open for 0% -> 0% of each run, Pallas kernels for 11% -> 9%
where the time goes in v9:
time: 93.6 us; the launch traced here: 93.2 us
  blocking collectives  29.3 us (31%)
  Pallas kernels  24.8 us (26%)
  waiting for transfers between devices  23.9 us (26%)
  starting transfers between devices  12.9 us (14%)
  local copies, waits for them, and re-layouts  1.4 us (1%)
    all_to_all x1, blocking collectives, exchange(): x = lax.all_to_all(x, ('gx', 'gy'), split_axis=0, concat_axis=0, tiled=True)  29.3 us
    all_to_all x1, waiting for transfers between devices, exchange(): x = lax.all_to_all(x, ('gx', 'gy'), split_axis=0, concat_axis=0, tiled=True)  23.9 us
    pallas_call x1, Pallas kernels, shards(): pl.pallas_call(functools.partial(rows_kernel, per, cols), out_shape=jax.S...  7.63 us
    all_to_all x1, starting transfers between devices, shards(): lax.all_to_all(message, ('gx', 'gy'), split_axis=0, concat_axis=0, tiled=...  7.08 us
    pallas_call x1, Pallas kernels, shards(): pl.pallas_call(functools.partial(image_kernel, bands, per), out_shape=jax...  7.05 us
    all_to_all x1, starting transfers between devices, exchange(): x = lax.all_to_all(x, ('gx', 'gy'), split_axis=0, concat_axis=0, tiled=True)  5.84 us
    pallas_call x1, Pallas kernels, shards(): pl.pallas_call(functools.partial(demig_kernel, bands, per), out_shape=jax...  5.31 us
    pallas_call x1, Pallas kernels, shards(): pl.pallas_call(functools.partial(prep_kernel, devices, capacity), out_sha...  2.16 us
  transfers between devices with their start and end apart: 2, of which 1 were waited for; matrix products, arithmetic and copies ran while one was open for 0% of the time, Pallas kernels for 9%

profile of v9, /device:TPU:1, one launch (start us, length us, event | category | flops | bytes accessed | tf_op | source)
XLA Modules:
  0.0 93.2 jit_solution(12801243595270956756)
XLA Ops:
  0.6 2.2 %prep.1 = (bf16[256,256]{1,0:T(8,128)(2,1)}, bf16[256,128]{1,0:T(8,128)(2,1)}) custom-call(s32[4,32]{1,0:T(4,128)} %bitcast.14, s32[4,16,32]{2,1,0:T(8,128)} %bitcast.13, bf16[32,4,128]{2,1,0:T(4,128)(2,1)} %am_ref.1), custom_call_target="tpu_custom_call" | custom-call | tf_op jit(solution)/shard_map/prep/pallas_call | solution.py:259
  2.8 7.1 %all-to-all-start = ((bf16[32,8,256]{2,1,0:T(8,128)(2,1)}), bf16[32,8,256]{2,1,0:T(8,128)(2,1)S(1)}, u32[]{:S(2)}, u32[]{:S(2)}) async-start(bf16[32,8,256]{2,1,0:T(8,128)(2,1)} %bitcast.12), calls=%async_computation | async-start | bytes 262144 | tf_op jit(solution)/shard_map/all_to_all | solution.py:269
  9.9 7.6 %rows.1.rows_hbm = bf16[16,128,1024]{2,1,0:T(8,128)(2,1)} custom-call(bf16[16,128,1024]{2,1,0:T(8,128)(2,1)} %image_hbm.1, bf16[1024,1024]{1,0:T(8,128)(2,1)} %bitcast.9), custom_call_target="tpu_custom_call" | custom-call | flops 4294967296 | bytes 8388608 | tf_op jit(solution)/shard_map/rows/pallas_call | solution.py:272
  17.5 0.0 copy-start.1
  17.5 0.0 copy-start
  17.5 0.0 all-to-all-done
  17.5 5.3 %demig.1 = bf16[32,16,8,128]{3,2,1,0:T(8,128)(2,1)} custom-call(bf16[256,256]{1,0:T(8,128)(2,1)S(1)} %bitcast.6, bf16[16,128,1024]{2,1,0:T(8,128)(2,1)} %rows.1.rows_hbm), custom_call_target="tpu_custom_call" | custom-call | flops 1073741824 | bytes 4194304 | tf_op jit(solution)/shard_map/demig/pallas_call | solution.py:291
  22.9 5.8 %all-to-all-start.1 = ((bf16[32,16,8,128]{3,2,1,0:T(8,128)(2,1)}), bf16[32,16,8,128]{3,2,1,0:T(8,128)(2,1)S(1)}, u32[]{:S(2)}, u32[]{:S(2)}) async-start(bf16[32,16,8,128]{3,2,1,0:T(8,128)(2,1)} %demig.1), calls=%async_computation.1 | async-start | bytes 2097152 | tf_op jit(solution)/shard_map/all_to_all | solution.py:254
  28.7 0.0 copy-done.1
  28.7 0.0 copy-start.3
  28.7 0.7 copy-done.3
  29.5 1.0 %codes.1 = (bf16[128,256]{1,0:T(8,128)(2,1)S(1)}, bf16[8,256,256]{2,1,0:T(8,128)(2,1)S(1)}, bf16[8,256,256]{2,1,0:T(8,128)(2,1)S(1)}, bf16[128,256]{1,0:T(8,128)(2,1)S(1)}) custom-call(bf16[256,256]{1,0:T(8,128)(2,1)S(1)} %bitcast.7, bf16[256,128]{1,0:T(8,128)(2,1)S(1)} %copy-done.1, s32[4,16,32]{2,1,0:T(8,128)S(1)} %bitcast.11), custom_call_target="tpu_custom_call" | custom-call | flops 134217728 | bytes 2097152 | tf_op jit(solution)/shard_map/codes/pallas_call | solution.py:305
  30.5 0.0 copy-start.4
  30.5 0.6 copy-done.4
  31.1 23.9 %all-to-all-done.1.recv_ref = bf16[32,16,8,128]{3,2,1,0:T(8,128)(2,1)S(1)} async-done(((bf16[32,16,8,128]{3,2,1,0:T(8,128)(2,1)}), bf16[32,16,8,128]{3,2,1,0:T(8,128)(2,1)S(1)}, u32[]{:S(2)}, u32[]{:S(2)}) %all-to-all-start.1) | async-done | bytes 1048608 | tf_op jit(solution)/shard_map/all_to_all | solution.py:254
  55.0 0.0 copy-start.2
  55.0 0.0 copy-start.5
  55.0 0.0 copy-done
  55.0 1.7 %resid.1 = (f32[32,16,128]{2,1,0:T(8,128)}, bf16[32,16,8,128]{3,2,1,0:T(8,128)(2,1)S(1)}) custom-call(bf16[256,128]{1,0:T(8,128)(2,1)S(1)} %copy-done.1, bf16[128,256]{1,0:T(8,128)(2,1)S(1)} %get-tuple-element.12.take_ref, bf16[8,256,256]{2,1,0:T(8,128)(2,1)S(1)} %get-tuple-element.13.pick_ref, bf16[8,256,256]{2,1,0:T(8,128)(2,1)S(1)} %get-tuple-element.14.drop_ref, ...), custom_call_target="tpu_custom_call" | custom-call | flops 268435456 | bytes 2097152 | tf_op jit(solution)/shard_map/resid/pallas_call | solution.py:319
  56.7 29.3 %all_to_all.21.blk_ref = bf16[32,16,8,128]{3,2,1,0:T(8,128)(2,1)S(1)} all-to-all(bf16[32,16,8,128]{3,2,1,0:T(8,128)(2,1)S(1)} %get-tuple-element.17), channel_id=1, replica_groups=mesh['gx'=8,'gy'=4] {'gx','gy'}, dimensions={0} | all-to-all | bytes 2097152 | tf_op jit(solution)/shard_map/all_to_all | solution.py:254
  86.0 0.0 copy-done.2
  86.0 0.0 copy-done.5
  86.0 7.0 %image.1 = f32[16,128,1024]{2,1,0:T(8,128)} custom-call(bf16[256,256]{1,0:T(8,128)(2,1)S(1)} %bitcast.8, bf16[128,256]{1,0:T(8,128)(2,1)S(1)} %copy-done.5, bf16[32,16,8,128]{3,2,1,0:T(8,128)(2,1)S(1)} %all_to_all.21.blk_ref, bf16[1024,1024]{1,0:T(8,128)(2,1)S(1)} %bitcast.10), custom_call_target="tpu_custom_call" | custom-call | flops 5368709120 | bytes 8388608 | tf_op jit(solution)/shard_map/image/pallas_call | solution.py:334
Async XLA Ops:
  2.8 14.8 %all-to-all-start = ((bf16[32,8,256]{2,1,0:T(8,128)(2,1)}), bf16[32,8,256]{2,1,0:T(8,128)(2,1)S(1)}, u32[]{:S(2)}, u32[]{:S(2)}) async-start(bf16[32,8,256]{2,1,0:T(8,128)(2,1)} %bitcast.12), calls=%async_computation | async-start | bytes 262144 | tf_op jit(solution)/shard_map/all_to_all | solution.py:269
  17.5 11.2 %copy-start.1 = (bf16[256,128]{1,0:T(8,128)(2,1)S(1)}, bf16[256,128]{1,0:T(8,128)(2,1)}, u32[]{:S(2)}) copy-start(bf16[256,128]{1,0:T(8,128)(2,1)} %get-tuple-element.10.place_ref) | copy-start | bytes 196612
  17.5 37.5 %copy-start = (bf16[32,16,128]{2,1,0:T(8,128)(2,1)S(1)}, bf16[32,16,128]{2,1,0:T(8,128)(2,1)}, u32[]{:S(2)}) copy-start(bf16[32,16,128]{2,1,0:T(8,128)(2,1)} %obs_ref.1) | copy-start | bytes 393220
  22.9 32.2 %all-to-all-start.1 = ((bf16[32,16,8,128]{3,2,1,0:T(8,128)(2,1)}), bf16[32,16,8,128]{3,2,1,0:T(8,128)(2,1)S(1)}, u32[]{:S(2)}, u32[]{:S(2)}) async-start(bf16[32,16,8,128]{3,2,1,0:T(8,128)(2,1)} %demig.1), calls=%async_computation.1 | async-start | bytes 2097152 | tf_op jit(solution)/shard_map/all_to_all | solution.py:254
  28.7 0.8 copy-start.3
  30.5 0.6 copy-start.4
  55.0 31.0 %copy-start.2 = (bf16[8,128,1024]{2,1,0:T(8,128)(2,1)S(1)}, bf16[8,128,1024]{2,1,0:T(8,128)(2,1)}, u32[]{:S(2)}) copy-start(bf16[8,128,1024]{2,1,0:T(8,128)(2,1)} %param.8) | copy-start | bytes 6291460
  55.0 31.0 %copy-start.5 = (bf16[128,256]{1,0:T(8,128)(2,1)S(1)}, bf16[128,256]{1,0:T(8,128)(2,1)}, u32[]{:S(2)}) copy-start(bf16[128,256]{1,0:T(8,128)(2,1)} %copy-done.4) | copy-start | bytes 196612

commit v10 on v9

--- a/solution.py
+++ b/solution.py
@@ -49,12 +49,9 @@
     msg_ref[:, width:] = marks.astype(BF)
 
 
-def codes_kernel(blocks, msg_ref, place_ref, tt_ref, take_ref, pick_ref, drop_ref, amp_ref):
+def fill_picks(blocks, tt_ref, pick_ref):
     tiles, depth, traces = tt_ref.shape
     group = 256 // blocks
-    width = amp_ref.shape[0]
-    amp_ref[...] = msg_ref[:, :width].astype(F32).T.astype(BF)
-    take_ref[...] = place_ref[...].astype(F32).T.astype(BF)
     size = depth * group
     lanes = 128
     at = iota((size, lanes), 1).astype(F32).astype(BF)
@@ -68,12 +65,10 @@
             code = dot(code, jnp.ones((traces, lanes), F32).astype(BF))
             code = (code + (row % group * blocks).astype(F32)).astype(BF)
             one, zero = jnp.ones_like(code), jnp.zeros_like(code)
-            pick = jnp.concatenate(
+            pick_ref[k * (traces // group) + h] = jnp.concatenate(
                 [jnp.where(code == at + BF(i), one, zero) for i in range(0, group * blocks, lanes)],
                 axis=1,
             )
-            pick_ref[k * (traces // group) + h] = pick
-            drop_ref[k * (traces // group) + h] = pick.astype(F32).T.astype(BF)
 
 
 def by_band(band, values, bands):
@@ -173,14 +168,15 @@
 
 
 def residual_kernel(
-    place_ref, take_ref, pick_ref, drop_ref, obs_ref, recv_ref, res_ref, send_ref, pair_ref
+    place_ref, tt_ref, obs_ref, recv_ref, res_ref, send_ref, pair_ref, pick_ref
 ):
     depth = pair_ref.shape[0]
     traces, blocks, block_len = obs_ref.shape
     group = 256 // blocks
     halves = traces // group
     tiles = pick_ref.shape[0] // halves
-    take = take_ref[...]
+    take = place_ref[...].astype(F32).T.astype(BF)
+    fill_picks(blocks, tt_ref, pick_ref)
     for z in range(0, depth, 2):
         two = dot(take, jnp.concatenate([get(recv_ref, z), get(recv_ref, z + 1)], axis=1)).astype(BF)
         pair_ref[z] = two[:, :block_len]
@@ -190,7 +186,7 @@
         for k in range(tiles):
             at = slice(k * traces + h * group, k * traces + (h + 1) * group)
             part = pair_ref[:, at, :].reshape(depth * group, block_len)
-            total = total + dot(drop_ref[k * halves + h], part)
+            total = total + dot(pick_ref[k * halves + h], part, ((0,), (0,)))
         res_ref[h * group : (h + 1) * group] = total.reshape(group, blocks, block_len)
         low = total.astype(BF)
         for k in range(tiles):
@@ -205,9 +201,10 @@
 
 
 def image_kernel(
-    bands, per, msg_ref, amp_ref, blk_ref, tab_ref, out_hbm, stack_ref, out_ref, sem
+    bands, per, msg_ref, blk_ref, tab_ref, out_hbm, stack_ref, out_ref, sem
 ):
     depth, width, cells = out_ref.shape
+    amp = msg_ref[:, :width].astype(F32).T.astype(BF)
     marks = msg_ref[:, width:].astype(F32)
     sent = []
     for m in range(depth // per):
@@ -215,7 +212,7 @@
             picked = get(blk_ref, z)
             band = jnp.broadcast_to(marks[:, z : z + 1], picked.shape).astype(BF)
             masked = by_band(band, picked, bands)
-            stack_ref[z * width : (z + 1) * width, :] = dot(amp_ref[...], masked).astype(BF)
+            stack_ref[z * width : (z + 1) * width, :] = dot(amp, masked).astype(BF)
         stack = stack_ref[m * per * width : (m + 1) * per * width, :]
         out_ref[m * per : (m + 1) * per] = dot(stack, tab_ref[...]).reshape(per, width, cells)
         at = pl.ds(m * per, per)
@@ -302,39 +299,28 @@
         name="demig",
     )(got, rows)
     returned = exchange(partials)
-    take, pick, drop, turned = pl.pallas_call(
-        functools.partial(codes_kernel, blocks),
-        out_shape=(
-            jax.ShapeDtypeStruct((pairs, slots), BF),
-            jax.ShapeDtypeStruct((groups, 256, 256), BF),
-            jax.ShapeDtypeStruct((groups, 256, 256), BF),
-            jax.ShapeDtypeStruct((width_x, slots), BF),
-        ),
-        in_specs=[VMEM] * 3,
-        out_specs=(VMEM,) * 4,
-        compiler_params=GRANT,
-        cost_estimate=cost(groups * 256 * 256 * 256, groups * 256 * 256 * 4),
-        name="codes",
-    )(got, place, traveltime.transpose(1, 2, 0))
     residual, outgoing = pl.pallas_call(
         residual_kernel,
         out_shape=(
             jax.ShapeDtypeStruct((traces, blocks, block_len), F32),
             jax.ShapeDtypeStruct(shape_of(depth), BF),
         ),
-        in_specs=[VMEM] * 6,
+        in_specs=[VMEM] * 4,
         out_specs=(VMEM, VMEM),
-        scratch_shapes=[pltpu.VMEM((depth, pairs, block_len), BF)],
+        scratch_shapes=[
+            pltpu.VMEM((depth, pairs, block_len), BF),
+            pltpu.VMEM((groups, 256, 256), BF),
+        ],
         compiler_params=GRANT,
         cost_estimate=cost(4 * depth * slots * pairs * block_len, 4 * depth * slots * block_len),
         name="resid",
-    )(place, take, pick, drop, observed, returned)
+    )(place, traveltime.transpose(1, 2, 0), observed, returned)
     incoming = exchange(outgoing)
     per = 2
     gradient = pl.pallas_call(
         functools.partial(image_kernel, bands, per),
         out_shape=jax.ShapeDtypeStruct((depth, width_x, width_y), F32),
-        in_specs=[VMEM] * 4,
+        in_specs=[VMEM] * 3,
         out_specs=ANY,
         scratch_shapes=[
             pltpu.VMEM((depth * width_x, long), BF),
@@ -346,7 +332,7 @@
             2 * depth * width_x * long * (width_y + slots), 4 * depth * width_x * width_y
         ),
         name="image",
-    )(got, turned, incoming, tables_flat)
+    )(got, incoming, tables_flat)
     return residual, gradient
 
 

time: 93.6 us -> 93.1 us (level)
  blocking collectives: 29.3 us -> 61.2 us
  waiting for transfers between devices: 23.9 us -> 0.01 us
  starting transfers between devices: 12.9 us -> 7.08 us
  local copies, waits for them, and re-layouts: 1.4 us -> 0.02 us
  Pallas kernels: 24.8 us -> 23.6 us
    all_to_all x1 -> x2, blocking collectives: 29.3 us -> 61.2 us  [exchange(): x = lax.all_to_all(x, ('gx', 'gy'), split_axis=0, concat_axis=0, tiled=True)]
    all_to_all x1 -> x0, waiting for transfers between devices: 23.9 us -> none  [exchange(): x = lax.all_to_all(x, ('gx', 'gy'), split_axis=0, concat_axis=0, tiled=True)]
    all_to_all x1 -> x0, starting transfers between devices: 5.84 us -> none  [exchange(): x = lax.all_to_all(x, ('gx', 'gy'), split_axis=0, concat_axis=0, tiled=True)]
    unnamed x12 -> x8, local copies, waits for them, and re-layouts: 1.4 us -> 0.02 us
    pallas_call x1 -> x0, Pallas kernels: 0.97 us -> none  [shards(): pl.pallas_call(functools.partial(codes_kernel, blocks), out_shape=(jax.Sh...]
  transfers between devices with their start and end apart: 2 -> 1, of which waited for: 1 -> 0; matrix products, arithmetic and copies ran while one was open for 0% -> 0% of each run, Pallas kernels for 9% -> 8%
where the time goes in v10:
time: 93.1 us; the launch traced here: 92.8 us
  blocking collectives  61.2 us (66%)
  Pallas kernels  23.6 us (25%)
  starting transfers between devices  7.08 us (8%)
    all_to_all x2, blocking collectives, exchange(): x = lax.all_to_all(x, ('gx', 'gy'), split_axis=0, concat_axis=0, tiled=True)  61.2 us
    pallas_call x1, Pallas kernels, shards(): pl.pallas_call(functools.partial(rows_kernel, per, cols), out_shape=jax.S...  7.63 us
    all_to_all x1, starting transfers between devices, shards(): lax.all_to_all(message, ('gx', 'gy'), split_axis=0, concat_axis=0, tiled=...  7.08 us
    pallas_call x1, Pallas kernels, shards(): pl.pallas_call(functools.partial(image_kernel, bands, per), out_shape=jax...  7.02 us
    pallas_call x1, Pallas kernels, shards(): pl.pallas_call(functools.partial(demig_kernel, bands, per), out_shape=jax...  4.44 us
    pallas_call x1, Pallas kernels, shards(): pl.pallas_call(residual_kernel, out_shape=(jax.ShapeDtypeStruct((traces,...  2.35 us
    pallas_call x1, Pallas kernels, shards(): pl.pallas_call(functools.partial(prep_kernel, devices, capacity), out_sha...  2.16 us
  transfers between devices with their start and end apart: 1, of which 0 were waited for; matrix products, arithmetic and copies ran while one was open for 0% of the time, Pallas kernels for 8%

profile of v10, /device:TPU:1, one launch (start us, length us, event | category | flops | bytes accessed | tf_op | source)
XLA Modules:
  0.0 92.8 jit_solution(6540472207903801658)
XLA Ops:
  0.6 2.2 %prep.1 = (bf16[256,256]{1,0:T(8,128)(2,1)}, bf16[256,128]{1,0:T(8,128)(2,1)}) custom-call(s32[4,32]{1,0:T(4,128)} %bitcast.13, s32[4,16,32]{2,1,0:T(8,128)} %bitcast.12, bf16[32,4,128]{2,1,0:T(4,128)(2,1)} %am_ref.1), custom_call_target="tpu_custom_call" | custom-call | tf_op jit(solution)/shard_map/prep/pallas_call | solution.py:256
  2.8 7.1 %all-to-all-start = ((bf16[32,8,256]{2,1,0:T(8,128)(2,1)}), bf16[32,8,256]{2,1,0:T(8,128)(2,1)S(1)}, u32[]{:S(2)}, u32[]{:S(2)}) async-start(bf16[32,8,256]{2,1,0:T(8,128)(2,1)} %bitcast.11), calls=%async_computation | async-start | bytes 262144 | tf_op jit(solution)/shard_map/all_to_all | solution.py:266
  9.9 7.6 %rows.1.rows_hbm = bf16[16,128,1024]{2,1,0:T(8,128)(2,1)} custom-call(bf16[16,128,1024]{2,1,0:T(8,128)(2,1)} %image_hbm.1, bf16[1024,1024]{1,0:T(8,128)(2,1)} %bitcast.9), custom_call_target="tpu_custom_call" | custom-call | flops 4294967296 | bytes 8388608 | tf_op jit(solution)/shard_map/rows/pallas_call | solution.py:269
  17.5 0.0 copy-start
  17.5 0.0 copy-start.1
  17.5 0.0 copy-start.2
  17.5 0.0 all-to-all-done
  17.6 0.0 copy-start.3
  17.6 4.4 %demig.1 = bf16[32,16,8,128]{3,2,1,0:T(8,128)(2,1)S(1)} custom-call(bf16[256,256]{1,0:T(8,128)(2,1)S(1)} %bitcast.6, bf16[16,128,1024]{2,1,0:T(8,128)(2,1)} %rows.1.rows_hbm), custom_call_target="tpu_custom_call" | custom-call | flops 1073741824 | bytes 4194304 | tf_op jit(solution)/shard_map/demig/pallas_call | solution.py:288
  22.0 32.0 %all_to_all.21.recv_ref = bf16[32,16,8,128]{3,2,1,0:T(8,128)(2,1)S(1)} all-to-all(bf16[32,16,8,128]{3,2,1,0:T(8,128)(2,1)S(1)} %demig.1), channel_id=1, replica_groups=mesh['gx'=8,'gy'=4] {'gx','gy'}, dimensions={0} | all-to-all | bytes 2097152 | tf_op jit(solution)/shard_map/all_to_all | solution.py:251
  54.0 0.0 copy-done
  54.0 0.0 copy-done.1
  54.0 0.0 copy-done.2
  54.0 2.3 %resid.1 = (f32[32,16,128]{2,1,0:T(8,128)}, bf16[32,16,8,128]{3,2,1,0:T(8,128)(2,1)S(1)}) custom-call(bf16[256,128]{1,0:T(8,128)(2,1)S(1)} %copy-done.1, s32[4,16,32]{2,1,0:T(8,128)S(1)} %bitcast.8, bf16[32,16,128]{2,1,0:T(8,128)(2,1)S(1)} %copy-done, bf16[32,16,8,128]{3,2,1,0:T(8,128)(2,1)S(1)} %all_to_all.21.recv_ref), custom_call_target="tpu_custom_call" | custom-call | flops 268435456 | bytes 2097152 | tf_op jit(solution)/shard_map/resid/pallas_call | solution.py:302
  56.3 29.3 %all_to_all.22.blk_ref = bf16[32,16,8,128]{3,2,1,0:T(8,128)(2,1)S(1)} all-to-all(bf16[32,16,8,128]{3,2,1,0:T(8,128)(2,1)S(1)} %get-tuple-element.9), channel_id=1, replica_groups=mesh['gx'=8,'gy'=4] {'gx','gy'}, dimensions={0} | all-to-all | bytes 2097152 | tf_op jit(solution)/shard_map/all_to_all | solution.py:251
  85.6 0.0 copy-done.3
  85.6 7.0 %image.1 = f32[16,128,1024]{2,1,0:T(8,128)} custom-call(bf16[256,256]{1,0:T(8,128)(2,1)S(1)} %bitcast.7, bf16[32,16,8,128]{3,2,1,0:T(8,128)(2,1)S(1)} %all_to_all.22.blk_ref, bf16[1024,1024]{1,0:T(8,128)(2,1)S(1)} %bitcast.10), custom_call_target="tpu_custom_call" | custom-call | flops 5368709120 | bytes 8388608 | tf_op jit(solution)/shard_map/image/pallas_call | solution.py:320
Async XLA Ops:
  2.8 14.8 %all-to-all-start = ((bf16[32,8,256]{2,1,0:T(8,128)(2,1)}), bf16[32,8,256]{2,1,0:T(8,128)(2,1)S(1)}, u32[]{:S(2)}, u32[]{:S(2)}) async-start(bf16[32,8,256]{2,1,0:T(8,128)(2,1)} %bitcast.11), calls=%async_computation | async-start | bytes 262144 | tf_op jit(solution)/shard_map/all_to_all | solution.py:266
  17.5 36.5 %copy-start = (bf16[32,16,128]{2,1,0:T(8,128)(2,1)S(1)}, bf16[32,16,128]{2,1,0:T(8,128)(2,1)}, u32[]{:S(2)}) copy-start(bf16[32,16,128]{2,1,0:T(8,128)(2,1)} %obs_ref.1) | copy-start | bytes 393220
  17.5 36.5 %copy-start.1 = (bf16[256,128]{1,0:T(8,128)(2,1)S(1)}, bf16[256,128]{1,0:T(8,128)(2,1)}, u32[]{:S(2)}) copy-start(bf16[256,128]{1,0:T(8,128)(2,1)} %get-tuple-element.6.place_ref) | copy-start | bytes 196612
  17.5 36.5 %copy-start.2 = (s32[32,4,16]{0,2,1:T(8,128)S(1)}, s32[32,4,16]{0,2,1:T(8,128)}, u32[]{:S(2)}) copy-start(s32[32,4,16]{0,2,1:T(8,128)} %param.11) | copy-start | bytes 24580
  17.6 68.1 %copy-start.3 = (bf16[8,128,1024]{2,1,0:T(8,128)(2,1)S(1)}, bf16[8,128,1024]{2,1,0:T(8,128)(2,1)}, u32[]{:S(2)}) copy-start(bf16[8,128,1024]{2,1,0:T(8,128)(2,1)} %param.8) | copy-start | bytes 6291460

commit v11 on v9

--- a/solution.py
+++ b/solution.py
@@ -149,7 +149,7 @@
         copy.wait()
 
 
-def demig_kernel(bands, per, msg_ref, rows_hbm, out_ref, rows_ref, sem):
+def demig_kernel(bands, per, msg_ref, rows_hbm, out_hbm, rows_ref, out_ref, sem, out_sem):
     depth, width, long = rows_ref.shape
     block_len = long // bands
     pieces = depth // per
@@ -157,6 +157,12 @@
     def rows_copy(m):
         at = pl.ds(m * per, per)
         return pltpu.make_async_copy(rows_hbm.at[at], rows_ref.at[at], sem.at[m])
+
+    def out_copy(start, count, slot):
+        at = pl.ds(start, count)
+        if len(out_ref.shape) == 4:
+            at = (slice(None), at)
+        return pltpu.make_async_copy(out_ref.at[at], out_hbm.at[at], out_sem.at[slot])
 
     for m in range(pieces):
         rows_copy(m).start()
@@ -170,6 +176,13 @@
                 [rows_ref[z, :, b * block_len : (b + 1) * block_len] for b in range(bands)], axis=0
             )
             put(out_ref, z, dot(by_band(band, amp, bands), rows).astype(BF))
+        if m == pieces - 2:
+            early = out_copy(0, (m + 1) * per, 0)
+            early.start()
+    late = out_copy((pieces - 1) * per, per, 1)
+    late.start()
+    early.wait()
+    late.wait()
 
 
 def residual_kernel(
@@ -292,10 +305,12 @@
         functools.partial(demig_kernel, bands, per),
         out_shape=jax.ShapeDtypeStruct(shape_of(depth), BF),
         in_specs=[VMEM, ANY],
-        out_specs=VMEM,
+        out_specs=ANY,
         scratch_shapes=[
             pltpu.VMEM((depth, width_x, long), BF),
+            pltpu.VMEM(shape_of(depth), BF),
             pltpu.SemaphoreType.DMA((depth // per,)),
+            pltpu.SemaphoreType.DMA((2,)),
         ],
         compiler_params=GRANT,
         cost_estimate=cost(2 * depth * slots * width_x * long, 2 * depth * width_x * long),

time: 93.6 us -> 93.5 us (level)
  no operation moved by 1% of the time
where the time goes in v11:
time: 93.5 us; the launch traced here: 93.1 us
  blocking collectives  29.3 us (31%)
  Pallas kernels  24.6 us (26%)
  waiting for transfers between devices  23.9 us (26%)
  starting transfers between devices  12.9 us (14%)
  local copies, waits for them, and re-layouts  1.4 us (1%)
    all_to_all x1, blocking collectives, exchange(): x = lax.all_to_all(x, ('gx', 'gy'), split_axis=0, concat_axis=0, tiled=True)  29.3 us
    all_to_all x1, waiting for transfers between devices, exchange(): x = lax.all_to_all(x, ('gx', 'gy'), split_axis=0, concat_axis=0, tiled=True)  23.9 us
    pallas_call x1, Pallas kernels, shards(): pl.pallas_call(functools.partial(rows_kernel, per, cols), out_shape=jax.S...  7.63 us
    all_to_all x1, starting transfers between devices, shards(): lax.all_to_all(message, ('gx', 'gy'), split_axis=0, concat_axis=0, tiled=...  7.08 us
    pallas_call x1, Pallas kernels, shards(): pl.pallas_call(functools.partial(image_kernel, bands, per), out_shape=jax...  7.05 us
    all_to_all x1, starting transfers between devices, exchange(): x = lax.all_to_all(x, ('gx', 'gy'), split_axis=0, concat_axis=0, tiled=True)  5.84 us
    pallas_call x1, Pallas kernels, shards(): pl.pallas_call(functools.partial(demig_kernel, bands, per), out_shape=jax...  5.14 us
    pallas_call x1, Pallas kernels, shards(): pl.pallas_call(functools.partial(prep_kernel, devices, capacity), out_sha...  2.16 us
  transfers between devices with their start and end apart: 2, of which 1 were waited for; matrix products, arithmetic and copies ran while one was open for 0% of the time, Pallas kernels for 9%

profile of v11, /device:TPU:1, one launch (start us, length us, event | category | flops | bytes accessed | tf_op | source)
XLA Modules:
  0.0 93.1 jit_solution(12983402473835026825)
XLA Ops:
  0.6 2.2 %prep.1 = (bf16[256,256]{1,0:T(8,128)(2,1)}, bf16[256,128]{1,0:T(8,128)(2,1)}) custom-call(s32[4,32]{1,0:T(4,128)} %bitcast.14, s32[4,16,32]{2,1,0:T(8,128)} %bitcast.13, bf16[32,4,128]{2,1,0:T(4,128)(2,1)} %am_ref.1), custom_call_target="tpu_custom_call" | custom-call | tf_op jit(solution)/shard_map/prep/pallas_call | solution.py:272
  2.8 7.1 %all-to-all-start = ((bf16[32,8,256]{2,1,0:T(8,128)(2,1)}), bf16[32,8,256]{2,1,0:T(8,128)(2,1)S(1)}, u32[]{:S(2)}, u32[]{:S(2)}) async-start(bf16[32,8,256]{2,1,0:T(8,128)(2,1)} %bitcast.12), calls=%async_computation | async-start | bytes 262144 | tf_op jit(solution)/shard_map/all_to_all | solution.py:282
  9.9 7.6 %rows.1.rows_hbm = bf16[16,128,1024]{2,1,0:T(8,128)(2,1)} custom-call(bf16[16,128,1024]{2,1,0:T(8,128)(2,1)} %image_hbm.1, bf16[1024,1024]{1,0:T(8,128)(2,1)} %bitcast.9), custom_call_target="tpu_custom_call" | custom-call | flops 4294967296 | bytes 8388608 | tf_op jit(solution)/shard_map/rows/pallas_call | solution.py:285
  17.5 0.0 copy-start.1
  17.5 0.0 copy-start
  17.5 0.0 all-to-all-done
  17.5 5.1 %demig.1 = bf16[32,16,8,128]{3,2,1,0:T(8,128)(2,1)} custom-call(bf16[256,256]{1,0:T(8,128)(2,1)S(1)} %bitcast.6, bf16[16,128,1024]{2,1,0:T(8,128)(2,1)} %rows.1.rows_hbm), custom_call_target="tpu_custom_call" | custom-call | flops 1073741824 | bytes 4194304 | tf_op jit(solution)/shard_map/demig/pallas_call | solution.py:304
  22.7 5.8 %all-to-all-start.1 = ((bf16[32,16,8,128]{3,2,1,0:T(8,128)(2,1)}), bf16[32,16,8,128]{3,2,1,0:T(8,128)(2,1)S(1)}, u32[]{:S(2)}, u32[]{:S(2)}) async-start(bf16[32,16,8,128]{3,2,1,0:T(8,128)(2,1)} %demig.1), calls=%async_computation.1 | async-start | bytes 2097152 | tf_op jit(solution)/shard_map/all_to_all | solution.py:267
  28.5 0.0 copy-done.1
  28.6 0.0 copy-start.3
  28.6 0.7 copy-done.3
  29.3 1.0 %codes.1 = (bf16[128,256]{1,0:T(8,128)(2,1)S(1)}, bf16[8,256,256]{2,1,0:T(8,128)(2,1)S(1)}, bf16[8,256,256]{2,1,0:T(8,128)(2,1)S(1)}, bf16[128,256]{1,0:T(8,128)(2,1)S(1)}) custom-call(bf16[256,256]{1,0:T(8,128)(2,1)S(1)} %bitcast.7, bf16[256,128]{1,0:T(8,128)(2,1)S(1)} %copy-done.1, s32[4,16,32]{2,1,0:T(8,128)S(1)} %bitcast.11), custom_call_target="tpu_custom_call" | custom-call | flops 134217728 | bytes 2097152 | tf_op jit(solution)/shard_map/codes/pallas_call | solution.py:320
  30.3 0.0 copy-start.4
  30.3 0.6 copy-done.4
  30.9 23.9 %all-to-all-done.1.recv_ref = bf16[32,16,8,128]{3,2,1,0:T(8,128)(2,1)S(1)} async-done(((bf16[32,16,8,128]{3,2,1,0:T(8,128)(2,1)}), bf16[32,16,8,128]{3,2,1,0:T(8,128)(2,1)S(1)}, u32[]{:S(2)}, u32[]{:S(2)}) %all-to-all-start.1) | async-done | bytes 1048608 | tf_op jit(solution)/shard_map/all_to_all | solution.py:267
  54.9 0.0 copy-start.2
  54.9 0.0 copy-start.5
  54.9 0.0 copy-done
  54.9 1.7 %resid.1 = (f32[32,16,128]{2,1,0:T(8,128)}, bf16[32,16,8,128]{3,2,1,0:T(8,128)(2,1)S(1)}) custom-call(bf16[256,128]{1,0:T(8,128)(2,1)S(1)} %copy-done.1, bf16[128,256]{1,0:T(8,128)(2,1)S(1)} %get-tuple-element.12.take_ref, bf16[8,256,256]{2,1,0:T(8,128)(2,1)S(1)} %get-tuple-element.13.pick_ref, bf16[8,256,256]{2,1,0:T(8,128)(2,1)S(1)} %get-tuple-element.14.drop_ref, ...), custom_call_target="tpu_custom_call" | custom-call | flops 268435456 | bytes 2097152 | tf_op jit(solution)/shard_map/resid/pallas_call | solution.py:334
  56.6 29.3 %all_to_all.21.blk_ref = bf16[32,16,8,128]{3,2,1,0:T(8,128)(2,1)S(1)} all-to-all(bf16[32,16,8,128]{3,2,1,0:T(8,128)(2,1)S(1)} %get-tuple-element.17), channel_id=1, replica_groups=mesh['gx'=8,'gy'=4] {'gx','gy'}, dimensions={0} | all-to-all | bytes 2097152 | tf_op jit(solution)/shard_map/all_to_all | solution.py:267
  85.8 0.0 copy-done.2
  85.8 0.0 copy-done.5
  85.8 7.1 %image.1 = f32[16,128,1024]{2,1,0:T(8,128)} custom-call(bf16[256,256]{1,0:T(8,128)(2,1)S(1)} %bitcast.8, bf16[128,256]{1,0:T(8,128)(2,1)S(1)} %copy-done.5, bf16[32,16,8,128]{3,2,1,0:T(8,128)(2,1)S(1)} %all_to_all.21.blk_ref, bf16[1024,1024]{1,0:T(8,128)(2,1)S(1)} %bitcast.10), custom_call_target="tpu_custom_call" | custom-call | flops 5368709120 | bytes 8388608 | tf_op jit(solution)/shard_map/image/pallas_call | solution.py:349
Async XLA Ops:
  2.8 14.8 %all-to-all-start = ((bf16[32,8,256]{2,1,0:T(8,128)(2,1)}), bf16[32,8,256]{2,1,0:T(8,128)(2,1)S(1)}, u32[]{:S(2)}, u32[]{:S(2)}) async-start(bf16[32,8,256]{2,1,0:T(8,128)(2,1)} %bitcast.12), calls=%async_computation | async-start | bytes 262144 | tf_op jit(solution)/shard_map/all_to_all | solution.py:282
  17.5 11.0 %copy-start.1 = (bf16[256,128]{1,0:T(8,128)(2,1)S(1)}, bf16[256,128]{1,0:T(8,128)(2,1)}, u32[]{:S(2)}) copy-start(bf16[256,128]{1,0:T(8,128)(2,1)} %get-tuple-element.10.place_ref) | copy-start | bytes 196612
  17.5 37.4 %copy-start = (bf16[32,16,128]{2,1,0:T(8,128)(2,1)S(1)}, bf16[32,16,128]{2,1,0:T(8,128)(2,1)}, u32[]{:S(2)}) copy-start(bf16[32,16,128]{2,1,0:T(8,128)(2,1)} %obs_ref.1) | copy-start | bytes 393220
  22.7 32.2 %all-to-all-start.1 = ((bf16[32,16,8,128]{3,2,1,0:T(8,128)(2,1)}), bf16[32,16,8,128]{3,2,1,0:T(8,128)(2,1)S(1)}, u32[]{:S(2)}, u32[]{:S(2)}) async-start(bf16[32,16,8,128]{3,2,1,0:T(8,128)(2,1)} %demig.1), calls=%async_computation.1 | async-start | bytes 2097152 | tf_op jit(solution)/shard_map/all_to_all | solution.py:267
  28.6 0.8 copy-start.3
  30.3 0.6 copy-start.4
  54.9 31.0 %copy-start.2 = (bf16[8,128,1024]{2,1,0:T(8,128)(2,1)S(1)}, bf16[8,128,1024]{2,1,0:T(8,128)(2,1)}, u32[]{:S(2)}) copy-start(bf16[8,128,1024]{2,1,0:T(8,128)(2,1)} %param.8) | copy-start | bytes 6291460
  54.9 31.0 %copy-start.5 = (bf16[128,256]{1,0:T(8,128)(2,1)S(1)}, bf16[128,256]{1,0:T(8,128)(2,1)}, u32[]{:S(2)}) copy-start(bf16[128,256]{1,0:T(8,128)(2,1)} %copy-done.4) | copy-start | bytes 196612

commit v12 on v9

--- a/solution.py
+++ b/solution.py
@@ -134,17 +134,18 @@
             if m == pieces - 1 and n + 1 < strips:
                 tab_copy(n + 1).wait()
                 turn_ref[n + 1] = tab_ref[(n + 1) * cols : (n + 2) * cols, :].T
-            levels = image_ref[m * per : (m + 1) * per].reshape(per * width, cells)
-            rows = dot(levels, turn_ref[n]).astype(BF)
-            out_ref[m * per : (m + 1) * per, :, n * cols : (n + 1) * cols] = rows.reshape(
-                per, width, cols
-            )
-            at = (pl.ds(m * per, per), slice(None), pl.ds(n * cols, cols))
-            copy = pltpu.make_async_copy(
-                out_ref.at[at], out_hbm.at[at], out_sem.at[n * pieces + m]
-            )
-            copy.start()
-            sent.append(copy)
+            last = n == strips - 1 and m == pieces - 1
+            part = per // 2 if last else per
+            for start in range(m * per, (m + 1) * per, part):
+                levels = image_ref[start : start + part].reshape(part * width, cells)
+                rows = dot(levels, turn_ref[n]).astype(BF)
+                out_ref[start : start + part, :, n * cols : (n + 1) * cols] = rows.reshape(
+                    part, width, cols
+                )
+                at = (pl.ds(start, part), slice(None), pl.ds(n * cols, cols))
+                copy = pltpu.make_async_copy(out_ref.at[at], out_hbm.at[at], out_sem.at[len(sent)])
+                copy.start()
+                sent.append(copy)
     for copy in sent:
         copy.wait()
 
@@ -281,7 +282,7 @@
             pltpu.VMEM((depth, width_x, long), BF),
             pltpu.SemaphoreType.DMA((depth // per,)),
             pltpu.SemaphoreType.DMA((long // cols,)),
-            pltpu.SemaphoreType.DMA((depth // per * (long // cols),)),
+            pltpu.SemaphoreType.DMA((depth // per * (long // cols) + 1,)),
         ],
         cost_estimate=cost(2 * depth * width_x * width_y * long, 4 * depth * width_x * width_y),
         name="rows",

time: 93.6 us -> 93.5 us (level)
  no operation moved by 1% of the time
where the time goes in v12:
time: 93.5 us; the launch traced here: 93.1 us
  blocking collectives  29.3 us (31%)
  Pallas kernels  24.6 us (26%)
  waiting for transfers between devices  23.9 us (26%)
  starting transfers between devices  12.9 us (14%)
  local copies, waits for them, and re-layouts  1.4 us (1%)
    all_to_all x1, blocking collectives, exchange(): x = lax.all_to_all(x, ('gx', 'gy'), split_axis=0, concat_axis=0, tiled=True)  29.3 us
    all_to_all x1, waiting for transfers between devices, exchange(): x = lax.all_to_all(x, ('gx', 'gy'), split_axis=0, concat_axis=0, tiled=True)  23.9 us
    pallas_call x1, Pallas kernels, shards(): pl.pallas_call(functools.partial(rows_kernel, per, cols), out_shape=jax.S...  7.46 us
    all_to_all x1, starting transfers between devices, shards(): lax.all_to_all(message, ('gx', 'gy'), split_axis=0, concat_axis=0, tiled=...  7.08 us
    pallas_call x1, Pallas kernels, shards(): pl.pallas_call(functools.partial(image_kernel, bands, per), out_shape=jax...  7.04 us
    all_to_all x1, starting transfers between devices, exchange(): x = lax.all_to_all(x, ('gx', 'gy'), split_axis=0, concat_axis=0, tiled=True)  5.84 us
    pallas_call x1, Pallas kernels, shards(): pl.pallas_call(functools.partial(demig_kernel, bands, per), out_shape=jax...  5.31 us
    pallas_call x1, Pallas kernels, shards(): pl.pallas_call(functools.partial(prep_kernel, devices, capacity), out_sha...  2.16 us
  transfers between devices with their start and end apart: 2, of which 1 were waited for; matrix products, arithmetic and copies ran while one was open for 0% of the time, Pallas kernels for 9%

profile of v12, /device:TPU:1, one launch (start us, length us, event | category | flops | bytes accessed | tf_op | source)
XLA Modules:
  0.0 93.1 jit_solution(3874311363058357490)
XLA Ops:
  0.6 2.2 %prep.1 = (bf16[256,256]{1,0:T(8,128)(2,1)}, bf16[256,128]{1,0:T(8,128)(2,1)}) custom-call(s32[4,32]{1,0:T(4,128)} %bitcast.14, s32[4,16,32]{2,1,0:T(8,128)} %bitcast.13, bf16[32,4,128]{2,1,0:T(4,128)(2,1)} %am_ref.1), custom_call_target="tpu_custom_call" | custom-call | tf_op jit(solution)/shard_map/prep/pallas_call | solution.py:260
  2.8 7.1 %all-to-all-start = ((bf16[32,8,256]{2,1,0:T(8,128)(2,1)}), bf16[32,8,256]{2,1,0:T(8,128)(2,1)S(1)}, u32[]{:S(2)}, u32[]{:S(2)}) async-start(bf16[32,8,256]{2,1,0:T(8,128)(2,1)} %bitcast.12), calls=%async_computation | async-start | bytes 262144 | tf_op jit(solution)/shard_map/all_to_all | solution.py:270
  9.9 7.5 %rows.1.rows_hbm = bf16[16,128,1024]{2,1,0:T(8,128)(2,1)} custom-call(bf16[16,128,1024]{2,1,0:T(8,128)(2,1)} %image_hbm.1, bf16[1024,1024]{1,0:T(8,128)(2,1)} %bitcast.9), custom_call_target="tpu_custom_call" | custom-call | flops 4294967296 | bytes 8388608 | tf_op jit(solution)/shard_map/rows/pallas_call | solution.py:273
  17.3 0.0 copy-start.1
  17.4 0.0 copy-start
  17.4 0.0 all-to-all-done
  17.4 5.3 %demig.1 = bf16[32,16,8,128]{3,2,1,0:T(8,128)(2,1)} custom-call(bf16[256,256]{1,0:T(8,128)(2,1)S(1)} %bitcast.6, bf16[16,128,1024]{2,1,0:T(8,128)(2,1)} %rows.1.rows_hbm), custom_call_target="tpu_custom_call" | custom-call | flops 1073741824 | bytes 4194304 | tf_op jit(solution)/shard_map/demig/pallas_call | solution.py:292
  22.7 5.8 %all-to-all-start.1 = ((bf16[32,16,8,128]{3,2,1,0:T(8,128)(2,1)}), bf16[32,16,8,128]{3,2,1,0:T(8,128)(2,1)S(1)}, u32[]{:S(2)}, u32[]{:S(2)}) async-start(bf16[32,16,8,128]{3,2,1,0:T(8,128)(2,1)} %demig.1), calls=%async_computation.1 | async-start | bytes 2097152 | tf_op jit(solution)/shard_map/all_to_all | solution.py:255
  28.5 0.0 copy-done.1
  28.6 0.0 copy-start.3
  28.6 0.7 copy-done.3
  29.3 1.0 %codes.1 = (bf16[128,256]{1,0:T(8,128)(2,1)S(1)}, bf16[8,256,256]{2,1,0:T(8,128)(2,1)S(1)}, bf16[8,256,256]{2,1,0:T(8,128)(2,1)S(1)}, bf16[128,256]{1,0:T(8,128)(2,1)S(1)}) custom-call(bf16[256,256]{1,0:T(8,128)(2,1)S(1)} %bitcast.7, bf16[256,128]{1,0:T(8,128)(2,1)S(1)} %copy-done.1, s32[4,16,32]{2,1,0:T(8,128)S(1)} %bitcast.11), custom_call_target="tpu_custom_call" | custom-call | flops 134217728 | bytes 2097152 | tf_op jit(solution)/shard_map/codes/pallas_call | solution.py:306
  30.3 0.0 copy-start.4
  30.3 0.6 copy-done.4
  30.9 23.9 %all-to-all-done.1.recv_ref = bf16[32,16,8,128]{3,2,1,0:T(8,128)(2,1)S(1)} async-done(((bf16[32,16,8,128]{3,2,1,0:T(8,128)(2,1)}), bf16[32,16,8,128]{3,2,1,0:T(8,128)(2,1)S(1)}, u32[]{:S(2)}, u32[]{:S(2)}) %all-to-all-start.1) | async-done | bytes 1048608 | tf_op jit(solution)/shard_map/all_to_all | solution.py:255
  54.9 0.0 copy-start.2
  54.9 0.0 copy-start.5
  54.9 0.0 copy-done
  54.9 1.7 %resid.1 = (f32[32,16,128]{2,1,0:T(8,128)}, bf16[32,16,8,128]{3,2,1,0:T(8,128)(2,1)S(1)}) custom-call(bf16[256,128]{1,0:T(8,128)(2,1)S(1)} %copy-done.1, bf16[128,256]{1,0:T(8,128)(2,1)S(1)} %get-tuple-element.12.take_ref, bf16[8,256,256]{2,1,0:T(8,128)(2,1)S(1)} %get-tuple-element.13.pick_ref, bf16[8,256,256]{2,1,0:T(8,128)(2,1)S(1)} %get-tuple-element.14.drop_ref, ...), custom_call_target="tpu_custom_call" | custom-call | flops 268435456 | bytes 2097152 | tf_op jit(solution)/shard_map/resid/pallas_call | solution.py:320
  56.6 29.3 %all_to_all.21.blk_ref = bf16[32,16,8,128]{3,2,1,0:T(8,128)(2,1)S(1)} all-to-all(bf16[32,16,8,128]{3,2,1,0:T(8,128)(2,1)S(1)} %get-tuple-element.17), channel_id=1, replica_groups=mesh['gx'=8,'gy'=4] {'gx','gy'}, dimensions={0} | all-to-all | bytes 2097152 | tf_op jit(solution)/shard_map/all_to_all | solution.py:255
  85.8 0.0 copy-done.2
  85.8 0.0 copy-done.5
  85.9 7.0 %image.1 = f32[16,128,1024]{2,1,0:T(8,128)} custom-call(bf16[256,256]{1,0:T(8,128)(2,1)S(1)} %bitcast.8, bf16[128,256]{1,0:T(8,128)(2,1)S(1)} %copy-done.5, bf16[32,16,8,128]{3,2,1,0:T(8,128)(2,1)S(1)} %all_to_all.21.blk_ref, bf16[1024,1024]{1,0:T(8,128)(2,1)S(1)} %bitcast.10), custom_call_target="tpu_custom_call" | custom-call | flops 5368709120 | bytes 8388608 | tf_op jit(solution)/shard_map/image/pallas_call | solution.py:335
Async XLA Ops:
  2.8 14.6 %all-to-all-start = ((bf16[32,8,256]{2,1,0:T(8,128)(2,1)}), bf16[32,8,256]{2,1,0:T(8,128)(2,1)S(1)}, u32[]{:S(2)}, u32[]{:S(2)}) async-start(bf16[32,8,256]{2,1,0:T(8,128)(2,1)} %bitcast.12), calls=%async_computation | async-start | bytes 262144 | tf_op jit(solution)/shard_map/all_to_all | solution.py:270
  17.3 11.2 %copy-start.1 = (bf16[256,128]{1,0:T(8,128)(2,1)S(1)}, bf16[256,128]{1,0:T(8,128)(2,1)}, u32[]{:S(2)}) copy-start(bf16[256,128]{1,0:T(8,128)(2,1)} %get-tuple-element.10.place_ref) | copy-start | bytes 196612
  17.4 37.5 %copy-start = (bf16[32,16,128]{2,1,0:T(8,128)(2,1)S(1)}, bf16[32,16,128]{2,1,0:T(8,128)(2,1)}, u32[]{:S(2)}) copy-start(bf16[32,16,128]{2,1,0:T(8,128)(2,1)} %obs_ref.1) | copy-start | bytes 393220
  22.7 32.2 %all-to-all-start.1 = ((bf16[32,16,8,128]{3,2,1,0:T(8,128)(2,1)}), bf16[32,16,8,128]{3,2,1,0:T(8,128)(2,1)S(1)}, u32[]{:S(2)}, u32[]{:S(2)}) async-start(bf16[32,16,8,128]{3,2,1,0:T(8,128)(2,1)} %demig.1), calls=%async_computation.1 | async-start | bytes 2097152 | tf_op jit(solution)/shard_map/all_to_all | solution.py:255
  28.6 0.8 copy-start.3
  30.3 0.6 copy-start.4
  54.9 31.0 %copy-start.2 = (bf16[8,128,1024]{2,1,0:T(8,128)(2,1)S(1)}, bf16[8,128,1024]{2,1,0:T(8,128)(2,1)}, u32[]{:S(2)}) copy-start(bf16[8,128,1024]{2,1,0:T(8,128)(2,1)} %param.8) | copy-start | bytes 6291460
  54.9 31.0 %copy-start.5 = (bf16[128,256]{1,0:T(8,128)(2,1)S(1)}, bf16[128,256]{1,0:T(8,128)(2,1)}, u32[]{:S(2)}) copy-start(bf16[128,256]{1,0:T(8,128)(2,1)} %copy-done.4) | copy-start | bytes 196612

commit v13 on v9

--- a/solution.py
+++ b/solution.py
@@ -287,7 +287,7 @@
         name="rows",
     )(model_image, tables_flat)
     rows = pltpu.with_memory_space_constraint(rows, pltpu.HBM)
-    per = 4
+    per = depth // 2
     partials = pl.pallas_call(
         functools.partial(demig_kernel, bands, per),
         out_shape=jax.ShapeDtypeStruct(shape_of(depth), BF),

time: 93.6 us -> 93.6 us (level)
  no operation moved by 1% of the time
where the time goes in v13:
time: 93.6 us; the launch traced here: 93.2 us
  blocking collectives  29.3 us (31%)
  Pallas kernels  24.7 us (26%)
  waiting for transfers between devices  23.9 us (26%)
  starting transfers between devices  12.9 us (14%)
  local copies, waits for them, and re-layouts  1.4 us (1%)
    all_to_all x1, blocking collectives, exchange(): x = lax.all_to_all(x, ('gx', 'gy'), split_axis=0, concat_axis=0, tiled=True)  29.3 us
    all_to_all x1, waiting for transfers between devices, exchange(): x = lax.all_to_all(x, ('gx', 'gy'), split_axis=0, concat_axis=0, tiled=True)  23.9 us
    pallas_call x1, Pallas kernels, shards(): pl.pallas_call(functools.partial(rows_kernel, per, cols), out_shape=jax.S...  7.63 us
    all_to_all x1, starting transfers between devices, shards(): lax.all_to_all(message, ('gx', 'gy'), split_axis=0, concat_axis=0, tiled=...  7.08 us
    pallas_call x1, Pallas kernels, shards(): pl.pallas_call(functools.partial(image_kernel, bands, per), out_shape=jax...  7.05 us
    all_to_all x1, starting transfers between devices, exchange(): x = lax.all_to_all(x, ('gx', 'gy'), split_axis=0, concat_axis=0, tiled=True)  5.84 us
    pallas_call x1, Pallas kernels, shards(): pl.pallas_call(functools.partial(demig_kernel, bands, per), out_shape=jax...  5.24 us
    pallas_call x1, Pallas kernels, shards(): pl.pallas_call(functools.partial(prep_kernel, devices, capacity), out_sha...  2.16 us
  transfers between devices with their start and end apart: 2, of which 1 were waited for; matrix products, arithmetic and copies ran while one was open for 0% of the time, Pallas kernels for 9%

profile of v13, /device:TPU:1, one launch (start us, length us, event | category | flops | bytes accessed | tf_op | source)
XLA Modules:
  0.0 93.2 jit_solution(18192658035021575287)
XLA Ops:
  0.6 2.2 %prep.1 = (bf16[256,256]{1,0:T(8,128)(2,1)}, bf16[256,128]{1,0:T(8,128)(2,1)}) custom-call(s32[4,32]{1,0:T(4,128)} %bitcast.14, s32[4,16,32]{2,1,0:T(8,128)} %bitcast.13, bf16[32,4,128]{2,1,0:T(4,128)(2,1)} %am_ref.1), custom_call_target="tpu_custom_call" | custom-call | tf_op jit(solution)/shard_map/prep/pallas_call | solution.py:259
  2.8 7.1 %all-to-all-start = ((bf16[32,8,256]{2,1,0:T(8,128)(2,1)}), bf16[32,8,256]{2,1,0:T(8,128)(2,1)S(1)}, u32[]{:S(2)}, u32[]{:S(2)}) async-start(bf16[32,8,256]{2,1,0:T(8,128)(2,1)} %bitcast.12), calls=%async_computation | async-start | bytes 262144 | tf_op jit(solution)/shard_map/all_to_all | solution.py:269
  9.9 7.6 %rows.1.rows_hbm = bf16[16,128,1024]{2,1,0:T(8,128)(2,1)} custom-call(bf16[16,128,1024]{2,1,0:T(8,128)(2,1)} %image_hbm.1, bf16[1024,1024]{1,0:T(8,128)(2,1)} %bitcast.9), custom_call_target="tpu_custom_call" | custom-call | flops 4294967296 | bytes 8388608 | tf_op jit(solution)/shard_map/rows/pallas_call | solution.py:272
  17.5 0.0 copy-start.1
  17.5 0.0 copy-start
  17.5 0.0 all-to-all-done
  17.5 5.2 %demig.1 = bf16[32,16,8,128]{3,2,1,0:T(8,128)(2,1)} custom-call(bf16[256,256]{1,0:T(8,128)(2,1)S(1)} %bitcast.6, bf16[16,128,1024]{2,1,0:T(8,128)(2,1)} %rows.1.rows_hbm), custom_call_target="tpu_custom_call" | custom-call | flops 1073741824 | bytes 4194304 | tf_op jit(solution)/shard_map/demig/pallas_call | solution.py:291
  22.8 5.8 %all-to-all-start.1 = ((bf16[32,16,8,128]{3,2,1,0:T(8,128)(2,1)}), bf16[32,16,8,128]{3,2,1,0:T(8,128)(2,1)S(1)}, u32[]{:S(2)}, u32[]{:S(2)}) async-start(bf16[32,16,8,128]{3,2,1,0:T(8,128)(2,1)} %demig.1), calls=%async_computation.1 | async-start | bytes 2097152 | tf_op jit(solution)/shard_map/all_to_all | solution.py:254
  28.6 0.0 copy-done.1
  28.7 0.0 copy-start.3
  28.7 0.7 copy-done.3
  29.4 1.0 %codes.1 = (bf16[128,256]{1,0:T(8,128)(2,1)S(1)}, bf16[8,256,256]{2,1,0:T(8,128)(2,1)S(1)}, bf16[8,256,256]{2,1,0:T(8,128)(2,1)S(1)}, bf16[128,256]{1,0:T(8,128)(2,1)S(1)}) custom-call(bf16[256,256]{1,0:T(8,128)(2,1)S(1)} %bitcast.7, bf16[256,128]{1,0:T(8,128)(2,1)S(1)} %copy-done.1, s32[4,16,32]{2,1,0:T(8,128)S(1)} %bitcast.11), custom_call_target="tpu_custom_call" | custom-call | flops 134217728 | bytes 2097152 | tf_op jit(solution)/shard_map/codes/pallas_call | solution.py:305
  30.4 0.0 copy-start.4
  30.4 0.6 copy-done.4
  31.0 23.9 %all-to-all-done.1.recv_ref = bf16[32,16,8,128]{3,2,1,0:T(8,128)(2,1)S(1)} async-done(((bf16[32,16,8,128]{3,2,1,0:T(8,128)(2,1)}), bf16[32,16,8,128]{3,2,1,0:T(8,128)(2,1)S(1)}, u32[]{:S(2)}, u32[]{:S(2)}) %all-to-all-start.1) | async-done | bytes 1048608 | tf_op jit(solution)/shard_map/all_to_all | solution.py:254
  55.0 0.0 copy-start.2
  55.0 0.0 copy-start.5
  55.0 0.0 copy-done
  55.0 1.7 %resid.1 = (f32[32,16,128]{2,1,0:T(8,128)}, bf16[32,16,8,128]{3,2,1,0:T(8,128)(2,1)S(1)}) custom-call(bf16[256,128]{1,0:T(8,128)(2,1)S(1)} %copy-done.1, bf16[128,256]{1,0:T(8,128)(2,1)S(1)} %get-tuple-element.12.take_ref, bf16[8,256,256]{2,1,0:T(8,128)(2,1)S(1)} %get-tuple-element.13.pick_ref, bf16[8,256,256]{2,1,0:T(8,128)(2,1)S(1)} %get-tuple-element.14.drop_ref, ...), custom_call_target="tpu_custom_call" | custom-call | flops 268435456 | bytes 2097152 | tf_op jit(solution)/shard_map/resid/pallas_call | solution.py:319
  56.7 29.3 %all_to_all.21.blk_ref = bf16[32,16,8,128]{3,2,1,0:T(8,128)(2,1)S(1)} all-to-all(bf16[32,16,8,128]{3,2,1,0:T(8,128)(2,1)S(1)} %get-tuple-element.17), channel_id=1, replica_groups=mesh['gx'=8,'gy'=4] {'gx','gy'}, dimensions={0} | all-to-all | bytes 2097152 | tf_op jit(solution)/shard_map/all_to_all | solution.py:254
  85.9 0.0 copy-done.2
  85.9 0.0 copy-done.5
  85.9 7.1 %image.1 = f32[16,128,1024]{2,1,0:T(8,128)} custom-call(bf16[256,256]{1,0:T(8,128)(2,1)S(1)} %bitcast.8, bf16[128,256]{1,0:T(8,128)(2,1)S(1)} %copy-done.5, bf16[32,16,8,128]{3,2,1,0:T(8,128)(2,1)S(1)} %all_to_all.21.blk_ref, bf16[1024,1024]{1,0:T(8,128)(2,1)S(1)} %bitcast.10), custom_call_target="tpu_custom_call" | custom-call | flops 5368709120 | bytes 8388608 | tf_op jit(solution)/shard_map/image/pallas_call | solution.py:334
Async XLA Ops:
  2.8 14.8 %all-to-all-start = ((bf16[32,8,256]{2,1,0:T(8,128)(2,1)}), bf16[32,8,256]{2,1,0:T(8,128)(2,1)S(1)}, u32[]{:S(2)}, u32[]{:S(2)}) async-start(bf16[32,8,256]{2,1,0:T(8,128)(2,1)} %bitcast.12), calls=%async_computation | async-start | bytes 262144 | tf_op jit(solution)/shard_map/all_to_all | solution.py:269
  17.5 11.1 %copy-start.1 = (bf16[256,128]{1,0:T(8,128)(2,1)S(1)}, bf16[256,128]{1,0:T(8,128)(2,1)}, u32[]{:S(2)}) copy-start(bf16[256,128]{1,0:T(8,128)(2,1)} %get-tuple-element.10.place_ref) | copy-start | bytes 196612
  17.5 37.5 %copy-start = (bf16[32,16,128]{2,1,0:T(8,128)(2,1)S(1)}, bf16[32,16,128]{2,1,0:T(8,128)(2,1)}, u32[]{:S(2)}) copy-start(bf16[32,16,128]{2,1,0:T(8,128)(2,1)} %obs_ref.1) | copy-start | bytes 393220
  22.8 32.2 %all-to-all-start.1 = ((bf16[32,16,8,128]{3,2,1,0:T(8,128)(2,1)}), bf16[32,16,8,128]{3,2,1,0:T(8,128)(2,1)S(1)}, u32[]{:S(2)}, u32[]{:S(2)}) async-start(bf16[32,16,8,128]{3,2,1,0:T(8,128)(2,1)} %demig.1), calls=%async_computation.1 | async-start | bytes 2097152 | tf_op jit(solution)/shard_map/all_to_all | solution.py:254
  28.7 0.8 copy-start.3
  30.4 0.6 copy-start.4
  55.0 31.0 %copy-start.2 = (bf16[8,128,1024]{2,1,0:T(8,128)(2,1)S(1)}, bf16[8,128,1024]{2,1,0:T(8,128)(2,1)}, u32[]{:S(2)}) copy-start(bf16[8,128,1024]{2,1,0:T(8,128)(2,1)} %param.8) | copy-start | bytes 6291460
  55.0 31.0 %copy-start.5 = (bf16[128,256]{1,0:T(8,128)(2,1)S(1)}, bf16[128,256]{1,0:T(8,128)(2,1)}, u32[]{:S(2)}) copy-start(bf16[128,256]{1,0:T(8,128)(2,1)} %copy-done.4) | copy-start | bytes 196612
